TPU v7x, 32 devices: a whole 2x2x4 slice. The times are simulated.
32 devices in a mesh: qrow: 4 (over y, x), kcol: 8 (over z, core).
Axes of the slice: x: 2, y: 2, z: 4, core: 2. Of those that a mesh axis runs over, the one named last changes fastest.
Arguments:
- query: bfloat16 [4096, 1024], P('kcol', 'qrow'), may hold values from -6 to 6
- key: bfloat16 [4096, 256], P(('kcol', 'qrow')), may hold values from -6 to 6
- value: bfloat16 [4096, 256], P(('kcol', 'qrow')), may hold values from -6 to 6
- output: bfloat16 [4096, 1024], P('kcol', 'qrow'), may hold values from -6 to 6
- grad_out: bfloat16 [4096, 1024], P('kcol', 'qrow'), may hold values from -6 to 6
- lse: float32 [16, 4096], P('qrow', 'kcol'), may hold values from 2 to 5
- doc_ids: int32 [4096], replicated, may hold values from 0 to 7, never falling along the last dimension, each value on 1 to 3072 neighbouring positions
Outputs:
- grad_query: float32 [4096, 1024], P('kcol', 'qrow')
- grad_key: float32 [4096, 256], P(('kcol', 'qrow'))
- grad_value: float32 [4096, 256], P(('kcol', 'qrow'))
Inputs may be any that keep to these rules, and one draw needn't show every extreme that they name: `doc_ids`: document ids never fall along the sequence; no document is longer than 4096 // 2 + 2 * (512) tokens.
All inputs are finite; a program needn't handle non-finite values.
Results may differ from a plain program's by a relative error of at most 0.0058.
Values may be sent and summed in bfloat16 or wider, within the bound.
No kernel may reach another device: no remote copies, remote signals or barrier semaphores. Data moves between devices by JAX's collectives and lax.ppermute only.
A program may use at most 192 MiB of HBM per device.

v0:
```python
import jax
import jax.numpy as jnp
from jax import lax
from jax.sharding import PartitionSpec as P

HEAD_DIM = 64
GROUP = 4


score_scale = 0.125


def shifted(block, axis, distance):
    devices = range(lax.axis_size(axis))
    route = [(i - distance, i) for i in devices if i - distance in devices]
    return lax.ppermute(block, axis, route)


def head_delta(grad_out, output):
    row_count = grad_out.shape[0]
    head_count = grad_out.shape[1] // HEAD_DIM
    product = grad_out.astype(jnp.float32) * output.astype(jnp.float32)
    return jnp.sum(product.reshape(row_count, head_count, HEAD_DIM), axis=2).T


def band_tile(query, grad_out, pair, lse_local, delta_local, live_mask):
    rows = query.shape[0]
    local_heads = query.shape[1] // HEAD_DIM
    query_three = query.reshape(rows, local_heads, HEAD_DIM)
    grad_three = grad_out.reshape(rows, local_heads, HEAD_DIM)
    key_group = pair[:, :HEAD_DIM]
    value_group = pair[:, HEAD_DIM:]
    scores = (
        jnp.einsum("qhd,kd->hqk", query_three, key_group, preferred_element_type=jnp.float32)
        * score_scale
    )
    weights = jnp.where(
        live_mask[None, :, :], jnp.exp(scores - lse_local[:, :, None]), jnp.float32(0.0)
    )
    value_part = jnp.einsum(
        "hqk,qhd->kd", weights.astype(jnp.bfloat16), grad_three, preferred_element_type=jnp.float32
    )
    weight_grad = jnp.einsum(
        "qhd,kd->hqk", grad_three, value_group, preferred_element_type=jnp.float32
    )
    score_grad = (weights * (weight_grad - delta_local[:, :, None])).astype(jnp.bfloat16)
    query_part = (
        jnp.einsum("hqk,kd->qhd", score_grad, key_group, preferred_element_type=jnp.float32)
        * score_scale
    )
    key_part = (
        jnp.einsum("hqk,qhd->kd", score_grad, query_three, preferred_element_type=jnp.float32)
        * score_scale
    )
    return (
        query_part.reshape(rows, local_heads * HEAD_DIM),
        jnp.concatenate([key_part, value_part], axis=1),
    )


def per_device(query, key, value, output, grad_out, lse, doc_ids):
    row_index = lax.axis_index("qrow")
    col_index = lax.axis_index("kcol")
    query_rows = query.shape[0]
    query_pos = col_index * query_rows + jnp.arange(query_rows, dtype=jnp.int32)
    query_docs = lax.dynamic_slice_in_dim(doc_ids, col_index * query_rows, query_rows, 0)
    local_heads = query.shape[1] // HEAD_DIM
    kv_group = row_index * local_heads // GROUP
    delta_local = head_delta(grad_out, output)
    panel_key, panel_value = (
        lax.all_gather(key, "qrow", axis=0, tiled=True),
        lax.all_gather(value, "qrow", axis=0, tiled=True),
    )
    own_pair = jnp.concatenate(
        [
            lax.dynamic_slice_in_dim(panel_key, kv_group * HEAD_DIM, HEAD_DIM, 1),
            lax.dynamic_slice_in_dim(panel_value, kv_group * HEAD_DIM, HEAD_DIM, 1),
        ],
        axis=1,
    )
    col_count = lax.axis_size("kcol")
    band_count = min(col_count - 1, col_count // 2 + 2)
    key_slot = jnp.arange(query_rows, dtype=jnp.int32)
    query_total = jnp.zeros((query_rows, local_heads * HEAD_DIM), jnp.float32)
    own_grads = jnp.zeros((query_rows, 2 * HEAD_DIM), jnp.float32)
    for step in range(band_count + 1):
        if step == 0:
            pair = own_pair
        else:
            pair = shifted(own_pair, "kcol", step)
        key_start = (col_index - step) * query_rows
        key_pos = key_start + key_slot
        key_docs = lax.dynamic_slice_in_dim(doc_ids, jnp.maximum(key_start, 0), query_rows, 0)
        live_mask = (
            (key_pos[None, :] >= 0)
            & (key_pos[None, :] <= query_pos[:, None])
            & (key_docs[None, :] == query_docs[:, None])
        )
        query_part, pair_grads = band_tile(query, grad_out, pair, lse, delta_local, live_mask)
        query_total = query_total + query_part
        if step == 0:
            own_grads = pair_grads
        else:
            own_grads = own_grads + shifted(pair_grads, "kcol", -step)
    feature_count = key.shape[1]
    key_full = lax.dynamic_update_slice_in_dim(
        jnp.zeros((query_rows, feature_count), jnp.float32),
        own_grads[:, :HEAD_DIM],
        kv_group * HEAD_DIM,
        1,
    )
    value_full = lax.dynamic_update_slice_in_dim(
        jnp.zeros((query_rows, feature_count), jnp.float32),
        own_grads[:, HEAD_DIM:],
        kv_group * HEAD_DIM,
        1,
    )
    grad_key, grad_value = (
        lax.psum_scatter(key_full, "qrow", scatter_dimension=0, tiled=True),
        lax.psum_scatter(value_full, "qrow", scatter_dimension=0, tiled=True),
    )
    return (query_total, grad_key, grad_value)


def solution(mesh):
    return jax.shard_map(
        per_device,
        mesh=mesh,
        in_specs=(
            P("kcol", "qrow"),
            P(("kcol", "qrow"), None),
            P(("kcol", "qrow"), None),
            P("kcol", "qrow"),
            P("kcol", "qrow"),
            P("qrow", "kcol"),
            P(),
        ),
        out_specs=(P("kcol", "qrow"), P(("kcol", "qrow"), None), P(("kcol", "qrow"), None)),
        check_vma=False,
    )
```

profile of v0, /device:TPU:16, one launch (start us, length us, event | category | flops | bytes accessed | tf_op | source)
XLA Modules:
  0.0 169.7 jit_solution(2850333152636726576)
XLA Ops:
  7.2 0.9 copy.64
  8.2 1.0 copy.66
  9.2 9.0 %all_gather.7 = bf16[512,256]{0,1:T(8,128)(2,1)S(1)} all-gather(bf16[128,256]{0,1:T(8,128)(2,1)S(1)} %copy.66), channel_id=1, replica_groups=mesh['qrow'=4,'kcol'=8] {'qrow'}, dimensions={0}, use_global_device_ids=true | all-gather | bytes 327680 | tf_op jit(solution)/shard_map/all_gather | solution.py:72
  18.2 9.0 %all_gather.6 = bf16[512,256]{0,1:T(8,128)(2,1)S(1)} all-gather(bf16[128,256]{0,1:T(8,128)(2,1)S(1)} %copy.64), channel_id=1, replica_groups=mesh['qrow'=4,'kcol'=8] {'qrow'}, dimensions={0}, use_global_device_ids=true | all-gather | bytes 327680 | tf_op jit(solution)/shard_map/all_gather | solution.py:71
  27.8 1.4 collective-permute-start.5
  29.3 1.3 collective-permute-start.4
  30.6 1.3 collective-permute-start.3
  31.9 1.9 %collective-permute-start.2 = (bf16[512,128]{0,1:T(8,128)(2,1)}, bf16[512,128]{0,1:T(8,128)(2,1)S(1)}, u32[]{:S(2)}, u32[]{:S(2)}) collective-permute-start(bf16[512,128]{0,1:T(8,128)(2,1)} %pad_maximum_fusion.6), channel_id=1, source_target_pairs={{0,3},{1,4},{2,5},{3,6},{4,7},{8,11},{9,12},{10,13},{11,14},{12,15... | collective-permute-start | bytes 393224 | tf_op jit(solution)/shard_map/ppermute | solution.py:16
  33.8 2.8 %collective-permute-start.1 = (bf16[512,128]{0,1:T(8,128)(2,1)}, bf16[512,128]{0,1:T(8,128)(2,1)S(1)}, u32[]{:S(2)}, u32[]{:S(2)}) collective-permute-start(bf16[512,128]{0,1:T(8,128)(2,1)} %pad_maximum_fusion.6), channel_id=1, source_target_pairs={{0,2},{1,3},{2,4},{3,5},{4,6},{5,7},{8,10},{9,11},{10,12},{11,13},... | collective-permute-start | bytes 393224 | tf_op jit(solution)/shard_map/ppermute | solution.py:16
  36.8 1.1 copy.67
  37.9 1.1 copy.65
  39.0 1.1 copy.69
  40.1 2.7 %fusion.97 = f32[512,512,4]{1,0,2:T(8,128)} fusion(bf16[512,4,64]{0,2,1:T(8,128)(2,1)S(1)} %bitcast.275, bf16[512,64]{0,1:T(8,128)(2,1)S(1)} %constant_dynamic-slice_fusion.1), kind=kOutput, calls=%fused_computation.128 | convolution fusion | flops 134217728 | bytes 4521984 | tf_op jit(solution)/shard_map/qhd,kd->hqk/dot_general | solution.py:34
  43.0 2.1 %compare_and_fusion.4 = (pred[512,512]{0,1:T(8,128)(4,1)S(1)}, pred[512,512]{0,1:T(8,128)(4,1)S(1)}, pred[512,512]{0,1:T(8,128)(4,1)S(1)}, pred[512,512]{0,1:T(8...) fusion(s32[512]{0:T(512)S(1)} %get-tuple-element.15, s32[512]{0:T(512)S(1)} %get-tuple-element.26, ...), kind=kLoop, calls=%fused_computation.95 | loop fusion | flops 6291456 | bytes 1602560 | tf_op jit(solution)/shard_map/and | solution.py:95
  45.1 3.2 %fusion.61 = f32[512,64]{0,1:T(8,128)S(1)} fusion(bf16[512,4,64]{0,2,1:T(8,128)(2,1)S(1)} %bitcast.290, f32[512,512,4]{1,0,2:T(8,128)} %fusion.97, f32[4,512]{1,0:T(4,128)S(1)} %copy-done.20, pred[512,512]{0,1:T(8,128)(4,1)S(1)} %get-tuple-element.24), kind=kOutput, calls=%fused_computation.70 | convolution fusion | flops 138412032 | bytes 4857856 | tf_op jit(solution)/shard_map/hqk,qhd->kd/dot_general | solution.py:40
  48.3 1.5 fusion.25
  50.2 1.9 %collective-permute-start = (bf16[512,128]{0,1:T(8,128)(2,1)}, bf16[512,128]{0,1:T(8,128)(2,1)S(1)}, u32[]{:S(2)}, u32[]{:S(2)}) collective-permute-start(bf16[512,128]{0,1:T(8,128)(2,1)} %pad_maximum_fusion.6), channel_id=1, source_target_pairs={{0,1},{1,2},{2,3},{3,4},{4,5},{5,6},{6,7},{8,9},{9,10},{10,11},{11... | collective-permute-start | bytes 393224 | tf_op jit(solution)/shard_map/ppermute | solution.py:16
  52.1 1.6 fusion.108
  53.7 1.0 fusion.79
  54.7 2.4 %fusion.1 = bf16[4,512,512]{1,2,0:T(8,128)(2,1)S(1)} fusion(f32[512,512,4]{1,0,2:T(8,128)S(1)} %fusion.108, bf16[512,4,64]{0,2,1:T(8,128)(2,1)S(1)} %bitcast.293, f32[4,512]{1,0:T(4,128)S(1)} %bitcast.305, f32[4,512]{1,0:T(4,128)S(1)} %copy-done.20, pred[512,512]{0,1:T(8,128)(4,1)S(1)} %compare_and_fusion, bf16[512,128]{0,1:T(8,128)(2,1)} %collective-permute-done.5), kind=kOutput, calls=%fused_computation.2 | convolution fusion | flops 140509184 | bytes 6897664 | tf_op jit(solution)/shard_map/qhd,kd->hqk/dot_general | solution.py:43
  58.6 1.6 fusion.106
  60.1 1.0 fusion.76
  61.1 2.4 %fusion.5 = bf16[4,512,512]{1,2,0:T(8,128)(2,1)S(1)} fusion(f32[512,512,4]{1,0,2:T(8,128)S(1)} %fusion.106, bf16[512,4,64]{0,2,1:T(8,128)(2,1)S(1)} %bitcast.295, f32[4,512]{1,0:T(4,128)S(1)} %bitcast.306, f32[4,512]{1,0:T(4,128)S(1)} %copy-done.20, pred[512,512]{0,1:T(8,128)(4,1)S(1)} %get-tuple-element.23, bf16[512,128]{0,1:T(8,128)(2,1)} %collective-permute-done.4), kind=kOutput, calls=%fused_computation.8 | convolution fusion | flops 140509184 | bytes 6897664 | tf_op jit(solution)/shard_map/qhd,kd->hqk/dot_general | solution.py:43
  64.3 0.9 collective-permute-start.10
  65.9 1.0 fusion.73
  66.9 1.5 fusion.9
  69.3 6.5 %collective-permute-start.9 = (f32[512,128]{0,1:T(8,128)S(1)}, f32[512,128]{0,1:T(8,128)S(1)}, u32[]{:S(2)}, u32[]{:S(2)}) collective-permute-start(f32[512,128]{0,1:T(8,128)S(1)} %pad_maximum_fusion.3), channel_id=1, source_target_pairs={{4,0},{5,1},{6,2},{7,3},{12,8},{13,9},{14,10},{15,11},{20,16},{21,... | collective-permute-start | bytes 786440 | tf_op jit(solution)/shard_map/ppermute | solution.py:16
  76.6 1.0 fusion.70
  77.6 1.5 fusion.13
  79.9 1.9 %collective-permute-start.8 = (f32[512,128]{0,1:T(8,128)S(1)}, f32[512,128]{0,1:T(8,128)S(1)}, u32[]{:S(2)}, u32[]{:S(2)}) collective-permute-start(f32[512,128]{0,1:T(8,128)S(1)} %pad_maximum_fusion.2), channel_id=1, source_target_pairs={{3,0},{4,1},{5,2},{6,3},{7,4},{11,8},{12,9},{13,10},{14,11},{15,12... | collective-permute-start | bytes 786440 | tf_op jit(solution)/shard_map/ppermute | solution.py:16
  82.6 1.0 fusion.67
  83.6 1.5 fusion.17
  85.9 2.1 %collective-permute-start.7 = (f32[512,128]{0,1:T(8,128)S(1)}, f32[512,128]{0,1:T(8,128)S(1)}, u32[]{:S(2)}, u32[]{:S(2)}) collective-permute-start(f32[512,128]{0,1:T(8,128)S(1)} %pad_maximum_fusion.1), channel_id=1, source_target_pairs={{2,0},{3,1},{4,2},{5,3},{6,4},{7,5},{10,8},{11,9},{12,10},{13,11},... | collective-permute-start | bytes 786440 | tf_op jit(solution)/shard_map/ppermute | solution.py:16
  88.8 1.0 fusion.64
  89.8 1.5 fusion.21
  92.2 1.9 %collective-permute-start.6 = (f32[512,128]{0,1:T(8,128)S(1)}, f32[512,128]{0,1:T(8,128)S(1)}, u32[]{:S(2)}, u32[]{:S(2)}) collective-permute-start(f32[512,128]{0,1:T(8,128)S(1)} %pad_maximum_fusion), channel_id=1, source_target_pairs={{1,0},{2,1},{3,2},{4,3},{5,4},{6,5},{7,6},{9,8},{10,9},{11,10},{12... | collective-permute-start | bytes 786440 | tf_op jit(solution)/shard_map/ppermute | solution.py:16
  94.9 2.1 %collective-permute-done.8 = f32[512,128]{0,1:T(8,128)S(1)} collective-permute-done((f32[512,128]{0,1:T(8,128)S(1)}, f32[512,128]{0,1:T(8,128)S(1)}, u32[]{:S(2)}, u32[]{:S(2)}) %collective-permute-start.8) | collective-permute-done | bytes 262176 | tf_op jit(solution)/shard_map/ppermute | solution.py:16
  97.0 5.6 %collective-permute-done.7 = f32[512,128]{0,1:T(8,128)S(1)} collective-permute-done((f32[512,128]{0,1:T(8,128)S(1)}, f32[512,128]{0,1:T(8,128)S(1)}, u32[]{:S(2)}, u32[]{:S(2)}) %collective-permute-start.7) | collective-permute-done | bytes 262176 | tf_op jit(solution)/shard_map/ppermute | solution.py:16
  102.6 4.7 %collective-permute-done.6 = f32[512,128]{0,1:T(8,128)S(1)} collective-permute-done((f32[512,128]{0,1:T(8,128)S(1)}, f32[512,128]{0,1:T(8,128)S(1)}, u32[]{:S(2)}, u32[]{:S(2)}) %collective-permute-start.6) | collective-permute-done | bytes 262176 | tf_op jit(solution)/shard_map/ppermute | solution.py:16
  107.6 1.9 %dynamic_update_slice.7 = f32[512,256]{1,0:T(8,128)S(1)} dynamic-update-slice(f32[512,256]{1,0:T(8,128)S(1)} %broadcast.461.clone.1, f32[512,64]{1,0:T(8,128)S(1)} %copy.92, s32[]{:T(128)} %constant.46.clone.1, s32[]{:T(128)S(6)} %select_n.44) | dynamic-update-slice | bytes 262148 | tf_op jit(solution)/shard_map/dynamic_update_slice | solution.py:112
  110.9 3.0 %fusion.107 = f32[64,4,512]{2,0,1:T(8,128)} fusion(bf16[4,512,512]{1,2,0:T(8,128)(2,1)} %copy-done, bf16[512,128]{0,1:T(8,128)(2,1)} %collective-permute-done.5), kind=kOutput, calls=%fused_computation.138 | convolution fusion | flops 134217728 | bytes 2686976 | tf_op jit(solution)/shard_map/hqk,kd->qhd/dot_general | solution.py:48
  114.0 2.1 %fusion.105 = f32[64,4,512]{2,0,1:T(8,128)} fusion(bf16[4,512,512]{1,2,0:T(8,128)(2,1)S(1)} %copy-done.4, bf16[512,128]{0,1:T(8,128)(2,1)} %collective-permute-done.4), kind=kOutput, calls=%fused_computation.136 | convolution fusion | flops 134217728 | bytes 2686976 | tf_op jit(solution)/shard_map/hqk,kd->qhd/dot_general | solution.py:48
  116.3 1.9 %dynamic_update_slice.6 = f32[512,256]{1,0:T(8,128)S(1)} dynamic-update-slice(f32[512,256]{1,0:T(8,128)S(1)} %broadcast.461.clone, f32[512,64]{1,0:T(8,128)S(1)} %copy.91, s32[]{:T(128)} %constant.46.clone.1, s32[]{:T(128)S(6)} %select_n.44) | dynamic-update-slice | bytes 262148 | tf_op jit(solution)/shard_map/dynamic_update_slice | solution.py:106
  119.1 1.5 fusion.103
  120.6 2.4 %fusion.101 = f32[64,4,512]{2,0,1:T(8,128)S(1)} fusion(bf16[4,512,512]{1,2,0:T(8,128)(2,1)} %copy-done.5, bf16[512,128]{0,1:T(8,128)(2,1)} %copy-done.18), kind=kOutput, calls=%fused_computation.132 | convolution fusion | flops 134217728 | bytes 2686976 | tf_op jit(solution)/shard_map/hqk,kd->qhd/dot_general | solution.py:48
  124.0 1.0 copy.93
  125.0 9.4 %reduce-scatter.5.cloned.1.call-done = f32[128,256]{1,0:T(8,128)} async-done(((f32[512,256]{1,0:T(8,128)}), f32[128,256]{1,0:T(8,128)}) %reduce-scatter.5.cloned.1.call-update) | async-done | bytes 131088 | tf_op jit(solution)/shard_map/reduce_scatter | solution.py:120
  134.4 28.4 %reduce-scatter.3.cloned.1.call-done = f32[128,256]{1,0:T(8,128)} async-done(((f32[512,256]{1,0:T(8,128)}), f32[128,256]{1,0:T(8,128)}) %reduce-scatter.3.cloned.1.call-update) | async-done | bytes 131088 | tf_op jit(solution)/shard_map/reduce_scatter | solution.py:119
  (95 shorter events, 14.0 us)
Async XLA Ops:
  7.2 35.7 %copy-start.19 = (s32[4096]{0:T(1024)S(1)}, s32[4096]{0:T(1024)}, u32[]{:S(2)}) copy-start(s32[4096]{0:T(1024)} %param.13) | copy-start | bytes 49156
  7.2 127.2 %reduce-scatter.5.cloned.1.call-start = ((), (), s32[]{:S(2)}) async-start(), calls=%async_computation.3 | async-start | bytes 655360 | tf_op jit(solution)/shard_map/reduce_scatter | solution.py:120
  27.8 17.3 %copy-start.20 = (f32[4,512]{1,0:T(4,128)S(1)}, f32[4,512]{1,0:T(4,128)}, u32[]{:S(2)}) copy-start(f32[4,512]{1,0:T(4,128)} %param.12) | copy-start | bytes 24580
  27.8 22.4 %collective-permute-start.5 = (bf16[512,128]{0,1:T(8,128)(2,1)}, bf16[512,128]{0,1:T(8,128)(2,1)}, u32[]{:S(2)}, u32[]{:S(2)}) collective-permute-start(bf16[512,128]{0,1:T(8,128)(2,1)} %pad_maximum_fusion.6), channel_id=1, source_target_pairs={{0,6},{1,7},{8,14},{9,15},{16,22},{17,23},{24,30},{25,31}} | collective-permute-start | bytes 393224 | tf_op jit(solution)/shard_map/ppermute | solution.py:16
  29.3 28.6 %collective-permute-start.4 = (bf16[512,128]{0,1:T(8,128)(2,1)}, bf16[512,128]{0,1:T(8,128)(2,1)}, u32[]{:S(2)}, u32[]{:S(2)}) collective-permute-start(bf16[512,128]{0,1:T(8,128)(2,1)} %pad_maximum_fusion.6), channel_id=1, source_target_pairs={{0,5},{1,6},{2,7},{8,13},{9,14},{10,15},{16,21},{17,22},{18,23},{2... | collective-permute-start | bytes 393224 | tf_op jit(solution)/shard_map/ppermute | solution.py:16
  30.6 33.7 %collective-permute-start.3 = (bf16[512,128]{0,1:T(8,128)(2,1)}, bf16[512,128]{0,1:T(8,128)(2,1)S(1)}, u32[]{:S(2)}, u32[]{:S(2)}) collective-permute-start(bf16[512,128]{0,1:T(8,128)(2,1)} %pad_maximum_fusion.6), channel_id=1, source_target_pairs={{0,4},{1,5},{2,6},{3,7},{8,12},{9,13},{10,14},{11,15},{16,20},{17,... | collective-permute-start | bytes 393224 | tf_op jit(solution)/shard_map/ppermute | solution.py:16
  31.9 37.4 %collective-permute-start.2 = (bf16[512,128]{0,1:T(8,128)(2,1)}, bf16[512,128]{0,1:T(8,128)(2,1)S(1)}, u32[]{:S(2)}, u32[]{:S(2)}) collective-permute-start(bf16[512,128]{0,1:T(8,128)(2,1)} %pad_maximum_fusion.6), channel_id=1, source_target_pairs={{0,3},{1,4},{2,5},{3,6},{4,7},{8,11},{9,12},{10,13},{11,14},{12,15... | collective-permute-start | bytes 393224 | tf_op jit(solution)/shard_map/ppermute | solution.py:16
  33.8 46.1 %collective-permute-start.1 = (bf16[512,128]{0,1:T(8,128)(2,1)}, bf16[512,128]{0,1:T(8,128)(2,1)S(1)}, u32[]{:S(2)}, u32[]{:S(2)}) collective-permute-start(bf16[512,128]{0,1:T(8,128)(2,1)} %pad_maximum_fusion.6), channel_id=1, source_target_pairs={{0,2},{1,3},{2,4},{3,5},{4,6},{5,7},{8,10},{9,11},{10,12},{11,13},... | collective-permute-start | bytes 393224 | tf_op jit(solution)/shard_map/ppermute | solution.py:16
  42.9 5.4 %copy-start.10 = (f32[512,512,4]{1,0,2:T(8,128)S(1)}, f32[512,512,4]{1,0,2:T(8,128)}, u32[]{:S(2)}) copy-start(f32[512,512,4]{1,0,2:T(8,128)} %fusion.97) | copy-start | bytes 12582916
  50.2 35.7 %collective-permute-start = (bf16[512,128]{0,1:T(8,128)(2,1)}, bf16[512,128]{0,1:T(8,128)(2,1)S(1)}, u32[]{:S(2)}, u32[]{:S(2)}) collective-permute-start(bf16[512,128]{0,1:T(8,128)(2,1)} %pad_maximum_fusion.6), channel_id=1, source_target_pairs={{0,1},{1,2},{2,3},{3,4},{4,5},{5,6},{6,7},{8,9},{9,10},{10,11},{11... | collective-permute-start | bytes 393224 | tf_op jit(solution)/shard_map/ppermute | solution.py:16
  57.1 4.0 %copy-start = (bf16[4,512,512]{1,2,0:T(8,128)(2,1)}, bf16[4,512,512]{1,2,0:T(8,128)(2,1)S(1)}, u32[]{:S(2)}) copy-start(bf16[4,512,512]{1,2,0:T(8,128)(2,1)S(1)} %fusion.1) | copy-start | bytes 6291460
  57.9 34.3 %collective-permute-start.11 = (f32[512,128]{0,1:T(8,128)S(1)}, f32[512,128]{0,1:T(8,128)S(1)}, u32[]{:S(2)}, u32[]{:S(2)}) collective-permute-start(f32[512,128]{0,1:T(8,128)S(1)} %pad_maximum_fusion.5), channel_id=1, source_target_pairs={{6,0},{7,1},{14,8},{15,9},{22,16},{23,17},{30,24},{31,25}} | collective-permute-start | bytes 786440 | tf_op jit(solution)/shard_map/ppermute | solution.py:16
  63.5 3.4 %copy-start.3 = (bf16[4,512,512]{1,2,0:T(8,128)(2,1)}, bf16[4,512,512]{1,2,0:T(8,128)(2,1)S(1)}, u32[]{:S(2)}) copy-start(bf16[4,512,512]{1,2,0:T(8,128)(2,1)S(1)} %fusion.5) | copy-start | bytes 6291460
  64.3 12.2 %copy-start.17 = (bf16[512,128]{0,1:T(8,128)(2,1)}, bf16[512,128]{0,1:T(8,128)(2,1)S(1)}, u32[]{:S(2)}) copy-start(bf16[512,128]{0,1:T(8,128)(2,1)S(1)} %collective-permute-done.3) | copy-start | bytes 393220
  64.3 30.5 %collective-permute-start.10 = (f32[512,128]{0,1:T(8,128)S(1)}, f32[512,128]{0,1:T(8,128)S(1)}, u32[]{:S(2)}, u32[]{:S(2)}) collective-permute-start(f32[512,128]{0,1:T(8,128)S(1)} %pad_maximum_fusion.4), channel_id=1, source_target_pairs={{5,0},{6,1},{7,2},{13,8},{14,9},{15,10},{21,16},{22,17},{23,18},{2... | collective-permute-start | bytes 786440 | tf_op jit(solution)/shard_map/ppermute | solution.py:16
  68.5 9.1 %copy-start.1 = (bf16[4,512,512]{1,2,0:T(8,128)(2,1)}, bf16[4,512,512]{1,2,0:T(8,128)(2,1)S(1)}, u32[]{:S(2)}) copy-start(bf16[4,512,512]{1,2,0:T(8,128)(2,1)S(1)} %fusion.9) | copy-start | bytes 6291460
  69.3 8.3 %copy-start.18 = (bf16[512,128]{0,1:T(8,128)(2,1)}, bf16[512,128]{0,1:T(8,128)(2,1)S(1)}, u32[]{:S(2)}) copy-start(bf16[512,128]{0,1:T(8,128)(2,1)S(1)} %collective-permute-done.2) | copy-start | bytes 393220
  69.3 25.6 %collective-permute-start.9 = (f32[512,128]{0,1:T(8,128)S(1)}, f32[512,128]{0,1:T(8,128)S(1)}, u32[]{:S(2)}, u32[]{:S(2)}) collective-permute-start(f32[512,128]{0,1:T(8,128)S(1)} %pad_maximum_fusion.3), channel_id=1, source_target_pairs={{4,0},{5,1},{6,2},{7,3},{12,8},{13,9},{14,10},{15,11},{20,16},{21,... | collective-permute-start | bytes 786440 | tf_op jit(solution)/shard_map/ppermute | solution.py:16
  79.1 4.5 %copy-start.5 = (bf16[4,512,512]{1,2,0:T(8,128)(2,1)}, bf16[4,512,512]{1,2,0:T(8,128)(2,1)S(1)}, u32[]{:S(2)}) copy-start(bf16[4,512,512]{1,2,0:T(8,128)(2,1)S(1)} %fusion.13) | copy-start | bytes 6291460
  79.9 3.7 %copy-start.15 = (bf16[512,128]{0,1:T(8,128)(2,1)}, bf16[512,128]{0,1:T(8,128)(2,1)S(1)}, u32[]{:S(2)}) copy-start(bf16[512,128]{0,1:T(8,128)(2,1)S(1)} %collective-permute-done.1) | copy-start | bytes 393220
  79.9 17.0 %collective-permute-start.8 = (f32[512,128]{0,1:T(8,128)S(1)}, f32[512,128]{0,1:T(8,128)S(1)}, u32[]{:S(2)}, u32[]{:S(2)}) collective-permute-start(f32[512,128]{0,1:T(8,128)S(1)} %pad_maximum_fusion.2), channel_id=1, source_target_pairs={{3,0},{4,1},{5,2},{6,3},{7,4},{11,8},{12,9},{13,10},{14,11},{15,12... | collective-permute-start | bytes 786440 | tf_op jit(solution)/shard_map/ppermute | solution.py:16
  85.1 3.7 %copy-start.8 = (bf16[4,512,512]{1,2,0:T(8,128)(2,1)}, bf16[4,512,512]{1,2,0:T(8,128)(2,1)S(1)}, u32[]{:S(2)}) copy-start(bf16[4,512,512]{1,2,0:T(8,128)(2,1)S(1)} %fusion.17) | copy-start | bytes 6291460
  85.9 16.6 %collective-permute-start.7 = (f32[512,128]{0,1:T(8,128)S(1)}, f32[512,128]{0,1:T(8,128)S(1)}, u32[]{:S(2)}, u32[]{:S(2)}) collective-permute-start(f32[512,128]{0,1:T(8,128)S(1)} %pad_maximum_fusion.1), channel_id=1, source_target_pairs={{2,0},{3,1},{4,2},{5,3},{6,4},{7,5},{10,8},{11,9},{12,10},{13,11},... | collective-permute-start | bytes 786440 | tf_op jit(solution)/shard_map/ppermute | solution.py:16
  91.4 3.5 %copy-start.6 = (bf16[4,512,512]{1,2,0:T(8,128)(2,1)}, bf16[4,512,512]{1,2,0:T(8,128)(2,1)S(1)}, u32[]{:S(2)}) copy-start(bf16[4,512,512]{1,2,0:T(8,128)(2,1)S(1)} %fusion.21) | copy-start | bytes 6291460
  92.2 15.1 %collective-permute-start.6 = (f32[512,128]{0,1:T(8,128)S(1)}, f32[512,128]{0,1:T(8,128)S(1)}, u32[]{:S(2)}, u32[]{:S(2)}) collective-permute-start(f32[512,128]{0,1:T(8,128)S(1)} %pad_maximum_fusion), channel_id=1, source_target_pairs={{1,0},{2,1},{3,2},{4,3},{5,4},{6,5},{7,6},{9,8},{10,9},{11,10},{12... | collective-permute-start | bytes 786440 | tf_op jit(solution)/shard_map/ppermute | solution.py:16
  109.5 0.8 copy-start.12
  110.4 52.4 %reduce-scatter.3.cloned.1.call-start = ((), (), s32[]{:S(2)}) async-start(), calls=%async_computation.2 | async-start | bytes 655360 | tf_op jit(solution)/shard_map/reduce_scatter | solution.py:119
  110.4 3.5 %copy-start.4 = (bf16[4,512,512]{1,2,0:T(8,128)(2,1)S(1)}, bf16[4,512,512]{1,2,0:T(8,128)(2,1)}, u32[]{:S(2)}) copy-start(bf16[4,512,512]{1,2,0:T(8,128)(2,1)} %copy-done.3) | copy-start | bytes 6291460
  110.9 8.1 %copy-start.2 = (bf16[4,512,512]{1,2,0:T(8,128)(2,1)S(1)}, bf16[4,512,512]{1,2,0:T(8,128)(2,1)}, u32[]{:S(2)}) copy-start(bf16[4,512,512]{1,2,0:T(8,128)(2,1)} %copy-done.1) | copy-start | bytes 6291460
  118.2 0.8 copy-start.11
  119.1 3.9 %copy-start.7 = (bf16[4,512,512]{1,2,0:T(8,128)(2,1)S(1)}, bf16[4,512,512]{1,2,0:T(8,128)(2,1)}, u32[]{:S(2)}) copy-start(bf16[4,512,512]{1,2,0:T(8,128)(2,1)} %copy-done.6) | copy-start | bytes 6291460
  119.1 4.4 %copy-start.9 = (bf16[4,512,512]{1,2,0:T(8,128)(2,1)S(1)}, bf16[4,512,512]{1,2,0:T(8,128)(2,1)}, u32[]{:S(2)}) copy-start(bf16[4,512,512]{1,2,0:T(8,128)(2,1)} %copy-done.8) | copy-start | bytes 6291460
  119.1 4.4 %copy-start.13 = (f32[64,4,512]{2,0,1:T(8,128)S(1)}, f32[64,4,512]{2,0,1:T(8,128)}, u32[]{:S(2)}) copy-start(f32[64,4,512]{2,0,1:T(8,128)} %fusion.107) | copy-start | bytes 1572868
  119.1 4.4 %copy-start.14 = (f32[64,4,512]{2,0,1:T(8,128)S(1)}, f32[64,4,512]{2,0,1:T(8,128)}, u32[]{:S(2)}) copy-start(f32[64,4,512]{2,0,1:T(8,128)} %fusion.105) | copy-start | bytes 1572868
  119.1 4.4 %copy-start.16 = (bf16[512,128]{0,1:T(8,128)(2,1)S(1)}, bf16[512,128]{0,1:T(8,128)(2,1)}, u32[]{:S(2)}) copy-start(bf16[512,128]{0,1:T(8,128)(2,1)} %copy-done.15) | copy-start | bytes 393220
Sparse Core Ops, SparseCore 0:
  110.5 23.8 reduce-scatter.4
  138.0 24.7 reduce-scatter.2
where the time goes:
time: 172 us; the launch traced here: 170 us
  waiting for transfers between devices  50.2 us (29%)
  matrix products  46.1 us (27%)
  starting transfers between devices  24.8 us (14%)
  blocking collectives  18 us (10%)
  between operations  14.9 us (9%)
  local copies, waits for them, and re-layouts  12.1 us (7%)
  other arithmetic  3.63 us (2%)
    reduce_scatter x1, waiting for transfers between devices, per_device(): lax.psum_scatter(key_full, 'qrow', scatter_dimension=0, tiled=True)  28.4 us
    ppermute x12, starting transfers between devices, shifted(): return lax.ppermute(block, axis, route)  24.7 us
    dot_general x7, matrix products, band_tile(): jnp.einsum('qhd,kd->hqk', grad_three, value_group, preferred_element_type...  12.5 us
    ppermute x12, waiting for transfers between devices, shifted(): return lax.ppermute(block, axis, route)  12.4 us
    dot_general x7, matrix products, band_tile(): jnp.einsum('hqk,kd->qhd', score_grad, key_group, preferred_element_type=j...  10.5 us
    reduce_scatter x1, waiting for transfers between devices, per_device(): lax.psum_scatter(value_full, 'qrow', scatter_dimension=0, tiled=True)  9.38 us
    dot_general x7, matrix products, band_tile(): jnp.einsum('hqk,qhd->kd', weights.astype(jnp.bfloat16), grad_three, prefe...  9.15 us
    all_gather x1, blocking collectives, per_device(): lax.all_gather(value, 'qrow', axis=0, tiled=True)  9 us
  transfers between devices with their start and end apart: 14, of which 5 were waited for; matrix products, arithmetic and copies ran while one was open for 33% of the time, Pallas kernels for 0%

commit v1 on v0

v1 whole, which is shorter than its diff:
```python
import functools
import jax
import jax.numpy as jnp
from jax import lax
from jax.experimental import pallas as pl
from jax.experimental.pallas import tpu as pltpu
from jax.sharding import PartitionSpec as P

HEAD_DIM = 64
GROUP = 4
TILE = 512
LOG2E = 1.4426950408889634
SCORE_SCALE = 0.125

f32, bf16 = jnp.float32, jnp.bfloat16
VMEM_SPEC = pl.BlockSpec(memory_space=pltpu.VMEM)
SMEM_SPEC = pl.BlockSpec(memory_space=pltpu.SMEM)


def nt(a, b):
    return lax.dot_general(a, b, (((1,), (1,)), ((), ())), preferred_element_type=f32)


def nn(a, b):
    return lax.dot_general(a, b, (((1,), (0,)), ((), ())), preferred_element_type=f32)


def prep_kernel(panel, q0, q1, g0, g1, o0, o1, l0, l1, docs, q_all, g_all, q_t, g_t, stats):
    rows, feats = q0.shape
    heads = feats // HEAD_DIM
    tiles = rows // TILE
    col = lax.broadcasted_iota(jnp.int32, (feats, 128), 0) // HEAD_DIM
    lane = lax.broadcasted_iota(jnp.int32, (feats, 128), 1)
    pick = jnp.where(lane == col + heads, 1.0, 0.0).astype(bf16)
    for side, (q, g, o, l) in enumerate(((q0, g0, o0, l0), (q1, g1, o1, l1))):
        for t in range(tiles):
            at = slice(t * TILE, (t + 1) * TILE)
            dst = side * tiles + t
            qv, gv = q[at, :], g[at, :]
            q_all[dst] = qv
            g_all[dst] = gv
            q_t[dst] = (qv.astype(f32) * SCORE_SCALE).T.astype(bf16)
            g_t[dst] = gv.astype(f32).T.astype(bf16)
            product = gv.astype(f32) * o[at, :].astype(f32)
            high = product.astype(bf16)
            low = (product - high.astype(f32)).astype(bf16)
            delta = nn(high, pick) + nn(low, pick)
            doc_row = docs[pl.ds(panel[side] * tiles + t, 1), :]
            table = jnp.concatenate(
                [
                    l[:, at] * LOG2E,
                    jnp.zeros((heads, TILE), f32),
                    doc_row,
                    jnp.zeros((127 - 2 * heads, TILE), f32),
                ],
                axis=0,
            )
            stats[dst] = table.T + delta


def band_kernel(shift, heads, own, first_call, *refs):
    if first_call:
        panel, first, last, q_all, g_all, q_t, g_t, stats, docs, pair, dq, grads, acc = refs
    else:
        panel, first, last, q_all, g_all, q_t, g_t, stats, docs, pair, dq_in, dq, grads, acc = refs
    key_tiles = pair.shape[0] // TILE
    q_tiles = q_all.shape[0]
    if first_call:
        dq[...] = jnp.zeros_like(dq)
    acc[...] = jnp.zeros_like(acc)
    key_panel = panel[0] - shift

    def one(qt, kt, masked):
        keys = pl.ds(pl.multiple_of(kt * TILE, TILE), TILE)
        block = pair[keys, :]
        key = block[:, :HEAD_DIM]
        value = block[:, HEAD_DIM:]
        key_scaled = (key.astype(f32) * SCORE_SCALE).astype(bf16)
        side = qt // key_tiles
        q_base = (panel[side] * key_tiles + qt % key_tiles) * TILE
        k_base = (key_panel * key_tiles + kt) * TILE
        if masked:
            q_pos = lax.broadcasted_iota(jnp.int32, (TILE, TILE), 0) + (q_base - k_base)
            k_pos = lax.broadcasted_iota(jnp.int32, (TILE, TILE), 1)
            q_doc = stats[qt, :, 2 * heads : 2 * heads + 1]
            k_doc = docs[pl.ds(key_panel * key_tiles + kt, 1), :]
            live = (k_pos <= q_pos) & (q_doc == k_doc)
        parts = []
        key_sum = value_sum = None
        for h in range(heads):
            at = slice(h * HEAD_DIM, (h + 1) * HEAD_DIM)
            scores = nt(q_all[qt, :, at], key)
            weights = jnp.exp2(scores * (SCORE_SCALE * LOG2E) - stats[qt, :, h : h + 1])
            if masked:
                weights = jnp.where(live, weights, 0.0)
            weight_grad = nt(g_all[qt, :, at], value)
            score_grad = (weights * (weight_grad - stats[qt, :, heads + h : heads + h + 1])).astype(bf16)
            parts.append(nn(score_grad, key_scaled))
            value_part = nn(g_t[qt, at, :], weights.astype(bf16))
            key_part = nn(q_t[qt, at, :], score_grad)
            key_sum = key_part if key_sum is None else key_sum + key_part
            value_sum = value_part if value_sum is None else value_sum + value_part
        dq[qt] += jnp.concatenate(parts, axis=1)
        acc[:HEAD_DIM, keys] += key_sum
        acc[HEAD_DIM:, keys] += value_sum

    @pl.when(key_panel >= 0)
    def _():
        def step(index, carry):
            qt, kt = index // key_tiles, index % key_tiles
            side = qt // key_tiles
            q_at = panel[side] * key_tiles + qt % key_tiles
            k_at = key_panel * key_tiles + kt
            live = (k_at <= q_at) & (first[q_at] <= last[k_at])
            full = (k_at < q_at) & (first[k_at] == last[q_at])

            @pl.when(live & full)
            def _():
                one(qt, kt, False)

            @pl.when(live & jnp.logical_not(full))
            def _():
                one(qt, kt, True)

            return carry

        lax.fori_loop(0, q_tiles * key_tiles, step, 0)

    grads[...] = acc[...].astype(grads.dtype)
    if not first_call:
        del dq_in


def collect_kernel(own, *refs):
    parts, out = refs[:-1], refs[-1]
    total = own[...]
    for part in parts:
        total = total + part[...].astype(f32)
    chunk = out.shape[2]
    for i in range(out.shape[0]):
        out[i] = total[:, i * chunk : (i + 1) * chunk]


def finish_kernel(ways, got, grad_key, grad_value):
    heads = got.shape[0] // ways
    keys, values = [], []
    for g in range(heads):
        block = got[g * ways]
        for w in range(1, ways):
            block = block + got[g * ways + w]
        keys.append(block[:HEAD_DIM])
        values.append(block[HEAD_DIM:])
    grad_key[...] = jnp.concatenate(keys, axis=0).T
    grad_value[...] = jnp.concatenate(values, axis=0).T


def per_device(query, key, value, output, grad_out, lse, doc_ids):
    row_count, col_count = lax.axis_size("qrow"), lax.axis_size("kcol")
    col = lax.axis_index("kcol")
    rows, feats = query.shape
    heads = feats // HEAD_DIM
    key_rows, key_feats = key.shape
    pair_feats = 2 * HEAD_DIM
    tiles = rows // TILE
    q_tiles = 2 * tiles
    core_swap = [(i, i ^ 1) for i in range(col_count)]

    def swap(x):
        return lax.ppermute(x, "kcol", core_swap)

    q_other, g_other, o_other, l_other = swap(query), swap(grad_out), swap(output), swap(lse)

    pieces = []
    for r in range(row_count):
        g = r * heads // GROUP
        at = slice(g * HEAD_DIM, (g + 1) * HEAD_DIM)
        pieces.append(jnp.concatenate([key[:, at], value[:, at]], axis=1))
    pair = lax.all_to_all(jnp.stack(pieces), "qrow", 0, 0).reshape(rows, pair_feats)

    doc_tiles = doc_ids.reshape(-1, TILE)
    first, last = doc_tiles[:, 0], doc_tiles[:, TILE - 1]
    docs = doc_tiles.astype(f32)
    panel = jnp.stack([col, col ^ 1]).astype(jnp.int32)

    params = pltpu.CompilerParams(vmem_limit_bytes=48 << 20)
    q_all, g_all, q_t, g_t, stats = pl.pallas_call(
        prep_kernel,
        in_specs=[SMEM_SPEC] + [VMEM_SPEC] * 9,
        out_specs=[VMEM_SPEC] * 5,
        out_shape=[
            jax.ShapeDtypeStruct((q_tiles, TILE, feats), bf16),
            jax.ShapeDtypeStruct((q_tiles, TILE, feats), bf16),
            jax.ShapeDtypeStruct((q_tiles, feats, TILE), bf16),
            jax.ShapeDtypeStruct((q_tiles, feats, TILE), bf16),
            jax.ShapeDtypeStruct((q_tiles, TILE, 128), f32),
        ],
        compiler_params=params,
        name="prep",
    )(panel, query, q_other, grad_out, g_other, output, o_other, lse, l_other, docs)

    def band(distance, block, dq):
        own = distance == 0
        extra = [] if dq is None else [dq]
        return pl.pallas_call(
            functools.partial(band_kernel, 2 * distance, heads, own, dq is None),
            in_specs=[SMEM_SPEC] * 3 + [VMEM_SPEC] * (7 + len(extra)),
            out_specs=[VMEM_SPEC] * 2,
            out_shape=[
                jax.ShapeDtypeStruct((q_tiles, TILE, feats), f32),
                jax.ShapeDtypeStruct((pair_feats, rows), f32 if own else bf16),
            ],
            scratch_shapes=[pltpu.VMEM((pair_feats, rows), f32)],
            input_output_aliases={} if dq is None else {10: 0},
            compiler_params=params,
            cost_estimate=pl.CostEstimate(
                flops=10 * 2 * rows * rows * feats,
                bytes_accessed=6 << 20,
                transcendentals=2 * rows * rows * heads,
            ),
            name=f"band{distance}",
        )(panel, first, last, q_all, g_all, q_t, g_t, stats, docs, block, *extra)

    reach = min(col_count // 2 - 1, col_count // 4 + 1)
    blocks = {}
    for d in range(1, reach + 1):
        route = [(i, i + 2 * d) for i in range(col_count - 2 * d)]
        blocks[d] = lax.ppermute(pair, "kcol", route)
    dq = None
    returned = []
    for d in range(1, reach + 1):
        dq, grads = band(d, blocks[d], dq)
        route = [(i + 2 * d, i) for i in range(col_count - 2 * d)]
        returned.append(lax.ppermute(grads, "kcol", route))
    dq, own_grads = band(0, pair, dq)

    dq_partner = swap(dq[tiles:])
    grad_query = (dq[:tiles] + dq_partner).reshape(rows, feats)

    chunks = pl.pallas_call(
        collect_kernel,
        in_specs=[VMEM_SPEC] * (1 + reach),
        out_specs=VMEM_SPEC,
        out_shape=jax.ShapeDtypeStruct((row_count, pair_feats, key_rows), f32),
        name="collect",
    )(own_grads, *returned)
    got = lax.all_to_all(chunks, "qrow", 0, 0)
    grad_key, grad_value = pl.pallas_call(
        functools.partial(finish_kernel, row_count * HEAD_DIM // key_feats),
        in_specs=[VMEM_SPEC],
        out_specs=[VMEM_SPEC] * 2,
        out_shape=[jax.ShapeDtypeStruct((key_rows, key_feats), f32)] * 2,
        name="finish",
    )(got)
    return grad_query, grad_key, grad_value


def solution(mesh):
    return jax.shard_map(
        per_device,
        mesh=mesh,
        in_specs=(
            P("kcol", "qrow"),
            P(("kcol", "qrow"), None),
            P(("kcol", "qrow"), None),
            P("kcol", "qrow"),
            P("kcol", "qrow"),
            P("qrow", "kcol"),
            P(),
        ),
        out_specs=(P("kcol", "qrow"), P(("kcol", "qrow"), None), P(("kcol", "qrow"), None)),
        check_vma=False,
    )
```

time: 172 us -> 72.1 us (0.42)
  the two profiles are of different devices: /device:TPU:16 before, /device:TPU:8 now
where the time goes in v1:
time: 72.1 us; the launch traced here: 71.5 us
  waiting for transfers between devices  22 us (31%)
  Pallas kernels  19 us (26%)
  starting transfers between devices  15 us (21%)
  blocking collectives  10.2 us (14%)
  local copies, waits for them, and re-layouts  2.59 us (4%)
  other arithmetic  1.8 us (2%)
  between operations  0.88 us (1%)
    pallas_call x4, Pallas kernels, band(): pl.pallas_call(functools.partial(band_kernel, 2 * distance, heads, own, d...  14.2 us
    ppermute x3, waiting for transfers between devices, per_device(): returned.append(lax.ppermute(grads, 'kcol', route))  13 us
    all_to_all x1, blocking collectives, per_device(): got = lax.all_to_all(chunks, 'qrow', 0, 0)  10.2 us
    ppermute x3, starting transfers between devices, per_device(): blocks[d] = lax.ppermute(pair, 'kcol', route)  6.44 us
    ppermute x3, waiting for transfers between devices, per_device(): blocks[d] = lax.ppermute(pair, 'kcol', route)  4.98 us
    all_to_all x1, waiting for transfers between devices, per_device(): lax.all_to_all(jnp.stack(pieces), 'qrow', 0, 0).reshape(rows, pair_feats)  3.98 us
    ppermute x3, starting transfers between devices, per_device(): returned.append(lax.ppermute(grads, 'kcol', route))  3.87 us
    all_to_all x1, starting transfers between devices, per_device(): lax.all_to_all(jnp.stack(pieces), 'qrow', 0, 0).reshape(rows, pair_feats)  3.72 us
  transfers between devices with their start and end apart: 12, of which 4 were waited for; matrix products, arithmetic and copies ran while one was open for 0% of the time, Pallas kernels for 16%

profile of v1, /device:TPU:8, one launch (start us, length us, event | category | flops | bytes accessed | tf_op | source)
XLA Modules:
  0.0 71.5 jit_solution(9662334763456155362)
XLA Ops:
  0.6 0.9 %fusion = (bf16[128,64]{1,0:T(8,128)(2,1)S(1)}, bf16[128,64]{1,0:T(8,128)(2,1)S(1)}, bf16[128,64]{1,0:T(8,128)(2,1)S(1)}, bf16[128,64]{1,0:T(8,128)(2,1)S(1)}) fusion(bf16[128,256]{1,0:T(8,128)(2,1)} %param.8), kind=kLoop, calls=%fused_computation.9 | loop fusion | bytes 131072 | tf_op jit(solution)/shard_map/slice | solution.py:177
  1.6 0.1 fusion.1
  1.7 0.0 copy-start.3
  1.7 0.1 maximum_bitcast_fusion
  1.8 0.0 copy-start.4
  1.8 0.0 copy-start.9
  1.8 0.1 maximum_bitcast_fusion.2
  1.9 0.0 copy-start.1
  1.9 0.0 copy-start.2
  1.9 0.7 pad_maximum_fusion
  2.6 3.7 %all-to-all-start = ((bf16[4,128,128]{2,1,0:T(8,128)(2,1)}), bf16[4,128,128]{2,1,0:T(8,128)(2,1)S(1)}, u32[]{:S(2)}, u32[]{:S(2)}) async-start(bf16[4,128,128]{2,1,0:T(8,128)(2,1)} %pad_maximum_fusion), calls=%async_computation | async-start | bytes 262144 | tf_op jit(solution)/shard_map/all_to_all | solution.py:178
  6.3 0.0 collective-permute-start
  6.3 0.5 collective-permute-start.2
  6.8 0.1 collective-permute-start.1
  6.9 0.4 collective-permute-start.3
  7.4 4.0 %all-to-all-done = bf16[4,128,128]{2,1,0:T(8,128)(2,1)S(1)} async-done(((bf16[4,128,128]{2,1,0:T(8,128)(2,1)}), bf16[4,128,128]{2,1,0:T(8,128)(2,1)S(1)}, u32[]{:S(2)}, u32[]{:S(2)}) %all-to-all-start) | async-done | bytes 131104 | tf_op jit(solution)/shard_map/all_to_all | solution.py:178
  11.3 3.5 %collective-permute-start.6 = (bf16[512,128]{1,0:T(8,128)(2,1)S(1)}, bf16[512,128]{1,0:T(8,128)(2,1)S(1)}, u32[]{:S(2)}, u32[]{:S(2)}) collective-permute-start(bf16[512,128]{1,0:T(8,128)(2,1)S(1)} %bitcast.13), channel_id=1, source_target_pairs={{0,2},{1,3},{2,4},{3,5},{4,6},{5,7},{8,10},{9,11},{10,12},{11,13},... | collective-permute-start | bytes 393224 | tf_op jit(solution)/shard_map/ppermute | solution.py:227
  14.8 0.2 slice_reduce_fusion
  15.0 0.0 collective-permute-done.3.l1
  15.0 2.3 %collective-permute-start.5 = (bf16[512,128]{1,0:T(8,128)(2,1)S(1)}, bf16[512,128]{1,0:T(8,128)(2,1)S(1)}, u32[]{:S(2)}, u32[]{:S(2)}) collective-permute-start(bf16[512,128]{1,0:T(8,128)(2,1)S(1)} %bitcast.14), channel_id=1, source_target_pairs={{0,4},{1,5},{2,6},{3,7},{8,12},{9,13},{10,14},{11,15},{16,20},{17,... | collective-permute-start | bytes 393224 | tf_op jit(solution)/shard_map/ppermute | solution.py:227
  17.3 0.1 pad_add_fusion.panel.refs_0_
  17.4 0.0 collective-permute-done.q1
  17.4 0.7 collective-permute-start.4
  18.1 0.0 collective-permute-done.2.o1
  18.1 0.0 collective-permute-done.1.g1
  18.1 1.2 %prep.1 = (bf16[2,512,256]{2,1,0:T(8,128)(2,1)S(1)}, bf16[2,512,256]{2,1,0:T(8,128)(2,1)S(1)}, bf16[2,256,512]{2,1,0:T(8,128)(2,1)S(1)}, bf16[2,256,512]{2,1,0:T(8,128)(2,1)S(1)}, f32[2,512,128]{2,1,0:T(8,128)S(1)}) custom-call(s32[2]{0:T(128)S(1)} %pad_add_fusion.panel.refs_0_, bf16[512,256]{1,0:T(8,128)(2,1)S(1)} %copy-done.1, ...), custom_call_target="tpu_custom_call" | custom-call | tf_op jit(solution)/shard_map/prep/pallas_call | solution.py:186
  19.3 5.0 %collective-permute-done.6.refs_9_ = bf16[512,128]{1,0:T(8,128)(2,1)S(1)} collective-permute-done((bf16[512,128]{1,0:T(8,128)(2,1)S(1)}, bf16[512,128]{1,0:T(8,128)(2,1)S(1)}, u32[]{:S(2)}, u32[]{:S(2)}) %collective-permute-start.6) | collective-permute-done | bytes 131104 | tf_op jit(solution)/shard_map/ppermute | solution.py:227
  24.3 6.2 %band1.1 = (f32[2,512,256]{2,1,0:T(8,128)S(1)}, bf16[128,512]{1,0:T(8,128)(2,1)S(1)}) custom-call(s32[2]{0:T(128)S(1)} %pad_add_fusion.panel.refs_0_, s32[8]{0:T(128)S(1)} %get-tuple-element.34.refs_1_, s32[8]{0:T(128)S(1)} %get-tuple-element.33.refs_2_, bf16[2,512,256]{2,1,0:T(8,128)(2,1)S(1)} %get-tuple-element.18.refs_3_, ...), custom_call_target="tpu_custom_call" | custom-call | flops 1342177280 | bytes 6291456 | tf_op jit(solution)/shard_map/band1/pallas_call | solution.py:204
  30.4 0.0 collective-permute-done.5.refs_9_
  30.4 0.8 %band2.1 = (f32[2,512,256]{2,1,0:T(8,128)S(1)}, bf16[128,512]{1,0:T(8,128)(2,1)S(1)}) custom-call(s32[2]{0:T(128)S(1)} %pad_add_fusion.panel.refs_0_, s32[8]{0:T(128)S(1)} %get-tuple-element.34.refs_1_, s32[8]{0:T(128)S(1)} %get-tuple-element.33.refs_2_, bf16[2,512,256]{2,1,0:T(8,128)(2,1)S(1)} %get-tuple-element.18.refs_3_, ...), custom_call_target="tpu_custom_call", output_to_operand_aliasing={{0}: (10, {})} | custom-call | flops 1342177280 | bytes 6291456 | tf_op jit(solution)/shard_map/band2/pallas_call | solution.py:204
  31.2 0.0 collective-permute-done.4.refs_9_
  31.2 0.6 band3.1
  31.8 6.7 %band0.1 = (f32[2,512,256]{2,1,0:T(8,128)S(1)}, f32[128,512]{1,0:T(8,128)S(1)}) custom-call(s32[2]{0:T(128)S(1)} %pad_add_fusion.panel.refs_0_, s32[8]{0:T(128)S(1)} %get-tuple-element.34.refs_1_, s32[8]{0:T(128)S(1)} %get-tuple-element.33.refs_2_, bf16[2,512,256]{2,1,0:T(8,128)(2,1)S(1)} %get-tuple-element.18.refs_3_, ...), custom_call_target="tpu_custom_call", output_to_operand_aliasing={{0}: (10, {})} | custom-call | flops 1342177280 | bytes 6291456 | tf_op jit(solution)/shard_map/band0/pallas_call | solution.py:204
  38.5 0.0 copy-start
  38.6 0.6 copy-done
  39.2 0.0 collective-permute-start.7
  39.2 0.7 collective-permute-start.10
  39.9 1.3 %collective-permute-start.9 = (bf16[128,512]{1,0:T(8,128)(2,1)S(1)}, bf16[128,512]{1,0:T(8,128)(2,1)S(1)}, u32[]{:S(2)}, u32[]{:S(2)}) collective-permute-start(bf16[128,512]{1,0:T(8,128)(2,1)S(1)} %get-tuple-element.29), channel_id=1, source_target_pairs={{4,0},{5,1},{6,2},{7,3},{12,8},{13,9},{14,10},{15,11},{20,16},{21,... | collective-permute-start | bytes 393224 | tf_op jit(solution)/shard_map/ppermute | solution.py:233
  41.2 1.9 %collective-permute-start.8 = (bf16[128,512]{1,0:T(8,128)(2,1)S(1)}, bf16[128,512]{1,0:T(8,128)(2,1)S(1)}, u32[]{:S(2)}, u32[]{:S(2)}) collective-permute-start(bf16[128,512]{1,0:T(8,128)(2,1)S(1)} %get-tuple-element.28), channel_id=1, source_target_pairs={{2,0},{3,1},{4,2},{5,3},{6,4},{7,5},{10,8},{11,9},{12,10},{13,11},... | collective-permute-start | bytes 393224 | tf_op jit(solution)/shard_map/ppermute | solution.py:233
  43.1 0.0 collective-permute-done.10.refs_2_
  43.1 5.5 %collective-permute-done.9.refs_1_ = bf16[128,512]{1,0:T(8,128)(2,1)S(1)} collective-permute-done((bf16[128,512]{1,0:T(8,128)(2,1)S(1)}, bf16[128,512]{1,0:T(8,128)(2,1)S(1)}, u32[]{:S(2)}, u32[]{:S(2)}) %collective-permute-start.9) | collective-permute-done | bytes 131104 | tf_op jit(solution)/shard_map/ppermute | solution.py:233
  48.6 7.5 %collective-permute-done.8.refs_0_ = bf16[128,512]{1,0:T(8,128)(2,1)S(1)} collective-permute-done((bf16[128,512]{1,0:T(8,128)(2,1)S(1)}, bf16[128,512]{1,0:T(8,128)(2,1)S(1)}, u32[]{:S(2)}, u32[]{:S(2)}) %collective-permute-start.8) | collective-permute-done | bytes 131104 | tf_op jit(solution)/shard_map/ppermute | solution.py:233
  56.1 0.6 copy-done.8
  56.8 1.9 %collect.1 = f32[4,128,128]{2,1,0:T(8,128)} custom-call(f32[128,512]{1,0:T(8,128)} %copy-done, bf16[128,512]{1,0:T(8,128)(2,1)} %copy-done.8, bf16[128,512]{1,0:T(8,128)(2,1)} %copy-done.7, bf16[128,512]{1,0:T(8,128)(2,1)} %copy-done.6), custom_call_target="tpu_custom_call" | custom-call | tf_op jit(solution)/shard_map/collect/pallas_call | solution.py:239
  58.7 10.2 %all_to_all.10.got = f32[4,128,128]{2,1,0:T(8,128)} all-to-all(f32[4,128,128]{2,1,0:T(8,128)} %collect.1), channel_id=1, replica_groups=mesh['qrow'=4,'kcol'=8] {'qrow'}, dimensions={0} | all-to-all | bytes 524288 | tf_op jit(solution)/shard_map/all_to_all | solution.py:246
  68.8 1.7 %finish.1 = (f32[128,256]{1,0:T(8,128)}, f32[128,256]{1,0:T(8,128)}) custom-call(f32[4,128,128]{2,1,0:T(8,128)} %all_to_all.10.got), custom_call_target="tpu_custom_call" | custom-call | tf_op jit(solution)/shard_map/finish/pallas_call | solution.py:247
  70.6 0.0 collective-permute-done.7
  70.6 0.9 %add_bitcast_fusion = f32[512,256]{1,0:T(8,128)} fusion(f32[1,512,256]{2,1,0:T(8,128)S(1)} %collective-permute-done.7, f32[2,512,256]{2,1,0:T(8,128)S(1)} %get-tuple-element.26), kind=kLoop, calls=%fused_computation | loop fusion | flops 131072 | bytes 1572864 | tf_op jit(solution)/shard_map/reshape | solution.py:237
  (15 shorter events, 0.1 us)
Async XLA Ops:
  0.6 0.9 %copy-start.5 = (bf16[128,256]{1,0:T(8,128)(2,1)S(1)}, bf16[128,256]{1,0:T(8,128)(2,1)}, u32[]{:S(2)}) copy-start(bf16[128,256]{1,0:T(8,128)(2,1)} %param.9) | copy-start | bytes 196612
  1.7 4.7 %copy-start.3 = (bf16[512,256]{1,0:T(8,128)(2,1)S(1)}, bf16[512,256]{1,0:T(8,128)(2,1)}, u32[]{:S(2)}) copy-start(bf16[512,256]{1,0:T(8,128)(2,1)} %o0.1) | copy-start | bytes 786436
  1.8 5.1 %copy-start.4 = (f32[4,512]{1,0:T(4,128)S(1)}, f32[4,512]{1,0:T(4,128)}, u32[]{:S(2)}) copy-start(f32[4,512]{1,0:T(4,128)} %l0.1) | copy-start | bytes 24580
  1.8 5.6 %copy-start.9 = (s32[4096]{0:T(1024)S(1)}, s32[4096]{0:T(1024)}, u32[]{:S(2)}) copy-start(s32[4096]{0:T(1024)} %param.13) | copy-start | bytes 49156
  1.9 4.4 %copy-start.1 = (bf16[512,256]{1,0:T(8,128)(2,1)S(1)}, bf16[512,256]{1,0:T(8,128)(2,1)}, u32[]{:S(2)}) copy-start(bf16[512,256]{1,0:T(8,128)(2,1)} %q0.1) | copy-start | bytes 786436
  1.9 4.9 %copy-start.2 = (bf16[512,256]{1,0:T(8,128)(2,1)S(1)}, bf16[512,256]{1,0:T(8,128)(2,1)}, u32[]{:S(2)}) copy-start(bf16[512,256]{1,0:T(8,128)(2,1)} %g0.1) | copy-start | bytes 786436
  2.6 8.7 %all-to-all-start = ((bf16[4,128,128]{2,1,0:T(8,128)(2,1)}), bf16[4,128,128]{2,1,0:T(8,128)(2,1)S(1)}, u32[]{:S(2)}, u32[]{:S(2)}) async-start(bf16[4,128,128]{2,1,0:T(8,128)(2,1)} %pad_maximum_fusion), calls=%async_computation | async-start | bytes 262144 | tf_op jit(solution)/shard_map/all_to_all | solution.py:178
  6.3 11.1 %collective-permute-start = (bf16[512,256]{1,0:T(8,128)(2,1)S(1)}, bf16[512,256]{1,0:T(8,128)(2,1)S(1)}, u32[]{:S(2)}, u32[]{:S(2)}) collective-permute-start(bf16[512,256]{1,0:T(8,128)(2,1)S(1)} %copy-done.1), channel_id=1, source_target_pairs={{0,1},{1,0},{2,3},{3,2},{4,5},{5,4},{6,7},{7,6},{8,9},{9,8},{10,11... | collective-permute-start | bytes 786440 | tf_op jit(solution)/shard_map/ppermute | solution.py:169
  6.3 11.7 %collective-permute-start.2 = (bf16[512,256]{1,0:T(8,128)(2,1)S(1)}, bf16[512,256]{1,0:T(8,128)(2,1)S(1)}, u32[]{:S(2)}, u32[]{:S(2)}) collective-permute-start(bf16[512,256]{1,0:T(8,128)(2,1)S(1)} %copy-done.3), channel_id=1, source_target_pairs={{0,1},{1,0},{2,3},{3,2},{4,5},{5,4},{6,7},{7,6},{8,9},{9,8},{10,11... | collective-permute-start | bytes 786440 | tf_op jit(solution)/shard_map/ppermute | solution.py:169
  6.8 11.3 %collective-permute-start.1 = (bf16[512,256]{1,0:T(8,128)(2,1)S(1)}, bf16[512,256]{1,0:T(8,128)(2,1)S(1)}, u32[]{:S(2)}, u32[]{:S(2)}) collective-permute-start(bf16[512,256]{1,0:T(8,128)(2,1)S(1)} %copy-done.2), channel_id=1, source_target_pairs={{0,1},{1,0},{2,3},{3,2},{4,5},{5,4},{6,7},{7,6},{8,9},{9,8},{10,11... | collective-permute-start | bytes 786440 | tf_op jit(solution)/shard_map/ppermute | solution.py:169
  6.9 8.1 %collective-permute-start.3 = (f32[4,512]{1,0:T(4,128)S(1)}, f32[4,512]{1,0:T(4,128)S(1)}, u32[]{:S(2)}, u32[]{:S(2)}) collective-permute-start(f32[4,512]{1,0:T(4,128)S(1)} %copy-done.4), channel_id=1, source_target_pairs={{0,1},{1,0},{2,3},{3,2},{4,5},{5,4},{6,7},{7,6},{8,9},{9,8},{10,11... | collective-permute-start | bytes 24584 | tf_op jit(solution)/shard_map/ppermute | solution.py:169
  11.3 12.9 %collective-permute-start.6 = (bf16[512,128]{1,0:T(8,128)(2,1)S(1)}, bf16[512,128]{1,0:T(8,128)(2,1)S(1)}, u32[]{:S(2)}, u32[]{:S(2)}) collective-permute-start(bf16[512,128]{1,0:T(8,128)(2,1)S(1)} %bitcast.13), channel_id=1, source_target_pairs={{0,2},{1,3},{2,4},{3,5},{4,6},{5,7},{8,10},{9,11},{10,12},{11,13},... | collective-permute-start | bytes 393224 | tf_op jit(solution)/shard_map/ppermute | solution.py:227
  15.0 15.4 %collective-permute-start.5 = (bf16[512,128]{1,0:T(8,128)(2,1)S(1)}, bf16[512,128]{1,0:T(8,128)(2,1)S(1)}, u32[]{:S(2)}, u32[]{:S(2)}) collective-permute-start(bf16[512,128]{1,0:T(8,128)(2,1)S(1)} %bitcast.14), channel_id=1, source_target_pairs={{0,4},{1,5},{2,6},{3,7},{8,12},{9,13},{10,14},{11,15},{16,20},{17,... | collective-permute-start | bytes 393224 | tf_op jit(solution)/shard_map/ppermute | solution.py:227
  17.4 13.8 %collective-permute-start.4 = (bf16[512,128]{1,0:T(8,128)(2,1)S(1)}, bf16[512,128]{1,0:T(8,128)(2,1)S(1)}, u32[]{:S(2)}, u32[]{:S(2)}) collective-permute-start(bf16[512,128]{1,0:T(8,128)(2,1)S(1)} %bitcast.15), channel_id=1, source_target_pairs={{0,6},{1,7},{8,14},{9,15},{16,22},{17,23},{24,30},{25,31}} | collective-permute-start | bytes 393224 | tf_op jit(solution)/shard_map/ppermute | solution.py:227
  38.5 0.7 copy-start
  39.2 31.4 %collective-permute-start.7 = (f32[1,512,256]{2,1,0:T(8,128)S(1)}, f32[1,512,256]{2,1,0:T(8,128)S(1)}, u32[]{:S(2)}, u32[]{:S(2)}) collective-permute-start(f32[1,512,256]{2,1,0:T(8,128)S(1)} %slice.47), channel_id=1, source_target_pairs={{0,1},{1,0},{2,3},{3,2},{4,5},{5,4},{6,7},{7,6},{8,9},{9,8},{10,11... | collective-permute-start | bytes 1572872 | tf_op jit(solution)/shard_map/ppermute | solution.py:169
  39.2 3.9 %collective-permute-start.10 = (bf16[128,512]{1,0:T(8,128)(2,1)S(1)}, bf16[128,512]{1,0:T(8,128)(2,1)S(1)}, u32[]{:S(2)}, u32[]{:S(2)}) collective-permute-start(bf16[128,512]{1,0:T(8,128)(2,1)S(1)} %get-tuple-element.30), channel_id=1, source_target_pairs={{6,0},{7,1},{14,8},{15,9},{22,16},{23,17},{30,24},{31,25}} | collective-permute-start | bytes 393224 | tf_op jit(solution)/shard_map/ppermute | solution.py:233
  39.9 8.7 %collective-permute-start.9 = (bf16[128,512]{1,0:T(8,128)(2,1)S(1)}, bf16[128,512]{1,0:T(8,128)(2,1)S(1)}, u32[]{:S(2)}, u32[]{:S(2)}) collective-permute-start(bf16[128,512]{1,0:T(8,128)(2,1)S(1)} %get-tuple-element.29), channel_id=1, source_target_pairs={{4,0},{5,1},{6,2},{7,3},{12,8},{13,9},{14,10},{15,11},{20,16},{21,... | collective-permute-start | bytes 393224 | tf_op jit(solution)/shard_map/ppermute | solution.py:233
  41.2 14.9 %collective-permute-start.8 = (bf16[128,512]{1,0:T(8,128)(2,1)S(1)}, bf16[128,512]{1,0:T(8,128)(2,1)S(1)}, u32[]{:S(2)}, u32[]{:S(2)}) collective-permute-start(bf16[128,512]{1,0:T(8,128)(2,1)S(1)} %get-tuple-element.28), channel_id=1, source_target_pairs={{2,0},{3,1},{4,2},{5,3},{6,4},{7,5},{10,8},{11,9},{12,10},{13,11},... | collective-permute-start | bytes 393224 | tf_op jit(solution)/shard_map/ppermute | solution.py:233
  43.1 13.0 %copy-start.6 = (bf16[128,512]{1,0:T(8,128)(2,1)}, bf16[128,512]{1,0:T(8,128)(2,1)S(1)}, u32[]{:S(2)}) copy-start(bf16[128,512]{1,0:T(8,128)(2,1)S(1)} %collective-permute-done.10.refs_2_) | copy-start | bytes 393220
  48.6 7.5 %copy-start.7 = (bf16[128,512]{1,0:T(8,128)(2,1)}, bf16[128,512]{1,0:T(8,128)(2,1)S(1)}, u32[]{:S(2)}) copy-start(bf16[128,512]{1,0:T(8,128)(2,1)S(1)} %collective-permute-done.9.refs_1_) | copy-start | bytes 393220
  56.1 0.7 copy-start.8

commit v2 on v1

v2 whole, which is shorter than its diff:
```python
import functools
import jax
import jax.numpy as jnp
from jax import lax
from jax.experimental import pallas as pl
from jax.experimental.pallas import tpu as pltpu
from jax.sharding import PartitionSpec as P

HEAD_DIM = 64
GROUP = 4
DOCS = 16
FAR = 512.0
SUB = 256
LOG2E = 1.4426950408889634
SCORE_SCALE = 0.125

f32, bf16 = jnp.float32, jnp.bfloat16
VMEM_SPEC = pl.BlockSpec(memory_space=pltpu.VMEM)
SMEM_SPEC = pl.BlockSpec(memory_space=pltpu.SMEM)


def small(mib=4):
    return pltpu.CompilerParams(vmem_limit_bytes=mib << 20)


def nt(a, b):
    return lax.dot_general(a, b, (((1,), (1,)), ((), ())), preferred_element_type=f32)


def nn(a, b):
    return lax.dot_general(a, b, (((1,), (0,)), ((), ())), preferred_element_type=f32)


def halves_swapped(x):
    return jnp.concatenate([x[:, HEAD_DIM:], x[:, :HEAD_DIM]], axis=1)


def three(x):
    high = x.astype(bf16).astype(f32)
    rest = x - high
    middle = rest.astype(bf16).astype(f32)
    return high, middle, rest - middle


def one_hot_rows(doc_row, value):
    length = doc_row.shape[1]
    ids = lax.broadcasted_iota(jnp.int32, (DOCS, length), 0).astype(f32)
    return jnp.where(ids == doc_row, value, 0.0)


def pack_kernel(heads, key, value, out):
    for r in range(out.shape[0]):
        g = r * heads // GROUP
        at = slice(g * HEAD_DIM, (g + 1) * HEAD_DIM)
        out[r] = jnp.concatenate([key[:, at], value[:, at]], axis=1)


def prep_kernel(panel, q0, q1, g0, g1, o0, o1, l0, l1, docs, q_ext, g_ext, q_t, g_t):
    rows, feats = q0.shape
    heads = feats // HEAD_DIM
    lane = lax.broadcasted_iota(jnp.int32, (rows, 128), 1)
    low_half = lane < HEAD_DIM
    for side, (q, g, o, l) in enumerate(((q0, g0, o0, l0), (q1, g1, o1, l1))):
        dst = slice(side * rows, (side + 1) * rows)
        q_t[:, dst] = (q[...].astype(f32) * SCORE_SCALE).T.astype(bf16)
        g_t[:, dst] = g[...].astype(f32).T.astype(bf16)
        product = g[...].astype(f32) * o[...].astype(f32)
        high = product.astype(bf16)
        low = (product - high.astype(f32)).astype(bf16)
        doc_row = docs[pl.ds(panel[side], 1), :]
        tail = [one_hot_rows(doc_row, FAR), jnp.zeros((HEAD_DIM - 3 - DOCS, rows), f32)]
        for p in range(heads // 2):
            at = slice(p * 128, (p + 1) * 128)
            table = []
            for h in (2 * p + 1, 2 * p):
                table += list(three(-FAR - l[h : h + 1, :])) + tail
            extra = jnp.concatenate(table, axis=0).T
            q_pair = q[:, at].astype(f32) * SCORE_SCALE
            q_ext[2 * p, dst, :] = jnp.where(low_half, q_pair, extra).astype(bf16)
            q_ext[2 * p + 1, dst, :] = jnp.where(low_half, extra, q_pair).astype(bf16)
            col = lax.broadcasted_iota(jnp.int32, (feats, 128), 0) // HEAD_DIM
            spot = lax.broadcasted_iota(jnp.int32, (feats, 128), 1)
            even = (col == 2 * p) & (spot >= HEAD_DIM) & (spot < HEAD_DIM + 3)
            odd = (col == 2 * p + 1) & (spot < 3)
            pick = jnp.where(even | odd, -1.0, 0.0).astype(bf16)
            d0, d1, d2 = three(nn(high, pick) + nn(low, pick))
            place = lane % HEAD_DIM
            extra = jnp.where(place == 0, d0, jnp.where(place == 1, d1, d2))
            g_pair = g[:, at].astype(f32)
            g_ext[2 * p, dst, :] = jnp.where(low_half, g_pair, extra).astype(bf16)
            g_ext[2 * p + 1, dst, :] = jnp.where(low_half, extra, g_pair).astype(bf16)


def band_kernel(shift, q_tile, first_call, *refs):
    panel, first, last, q_ext, g_ext, q_t, g_t, docs, pair = refs[:9]
    dq, grads, acc, k_ext, v_ext, k_lone = refs[9 if first_call else 10 :]
    heads, q_rows, _ = q_ext.shape
    rows = pair.shape[0]
    subs = rows // SUB
    q_subs = q_tile // SUB
    q_tiles = q_rows // q_tile
    if first_call:
        dq[...] = jnp.zeros_like(dq)
    acc[...] = jnp.zeros_like(acc)
    key_panel = panel[0] - shift

    def one(qt, kt, masked):
        at_q = pl.ds(pl.multiple_of(qt * q_tile, q_tile), q_tile)
        at_k = pl.ds(pl.multiple_of(kt * SUB, SUB), SUB)
        weights, score_grads = [], []
        if masked:
            ahead = (qt % (rows // q_tile)) * q_tile - kt * SUB
            q_pos = lax.broadcasted_iota(jnp.int32, (q_tile, SUB), 0) + ahead
            live = lax.broadcasted_iota(jnp.int32, (q_tile, SUB), 1) <= q_pos
        for h in range(heads):
            weight = jnp.exp2(nt(q_ext[h, at_q, :], k_ext[h % 2, at_k, :]) * LOG2E)
            if masked:
                weight = jnp.where(live, weight, 0.0)
            grad = nt(g_ext[h, at_q, :], v_ext[h % 2, at_k, :])
            weights.append(weight.astype(bf16))
            score_grads.append((weight * grad).astype(bf16))
        key_sum = value_sum = 0.0
        for h in range(heads):
            at = slice(h * HEAD_DIM, (h + 1) * HEAD_DIM)
            key_sum += nn(q_t[at, at_q], score_grads[h])
            value_sum += nn(g_t[at, at_q], weights[h])
        for p in range(heads // 2):
            dq[at_q, p * 128 : (p + 1) * 128] += nn(score_grads[2 * p], k_lone[0, at_k, :]) + nn(
                score_grads[2 * p + 1], k_lone[1, at_k, :]
            )
        acc[:HEAD_DIM, at_k] += key_sum
        acc[HEAD_DIM:, at_k] += value_sum

    @pl.when(key_panel >= 0)
    def _():
        lane = lax.broadcasted_iota(jnp.int32, (rows, 128), 1)
        low_half = lane < HEAD_DIM
        doc_row = docs[pl.ds(key_panel, 1), :]
        half = [jnp.ones((3, rows), f32), one_hot_rows(doc_row, 1.0), jnp.zeros((HEAD_DIM - 3 - DOCS, rows), f32)]
        extra = jnp.concatenate(half + half, axis=0).T
        ones = jnp.where(lane % HEAD_DIM < 3, 1.0, 0.0)
        straight = pair[...].astype(f32)
        turned = halves_swapped(pair[...]).astype(f32)
        k_ext[0] = jnp.where(low_half, straight, extra).astype(bf16)
        k_ext[1] = jnp.where(low_half, extra, turned).astype(bf16)
        v_ext[0] = jnp.where(low_half, turned, ones).astype(bf16)
        v_ext[1] = jnp.where(low_half, ones, straight).astype(bf16)
        k_lone[0] = jnp.where(low_half, straight * SCORE_SCALE, 0.0).astype(bf16)
        k_lone[1] = jnp.where(low_half, 0.0, turned * SCORE_SCALE).astype(bf16)

        def step(index, carry):
            qt, kt = index // subs, index % subs
            side = qt // (rows // q_tile)
            q_at = panel[side] * subs + (qt % (rows // q_tile)) * q_subs
            k_at = key_panel * subs + kt
            live = first[q_at] <= last[k_at]
            if shift > 0:
                pl.when(live)(functools.partial(one, qt, kt, False))
            else:
                live = live & (k_at < q_at + q_subs)
                below = k_at < q_at
                pl.when(live & below)(functools.partial(one, qt, kt, False))
                pl.when(live & jnp.logical_not(below))(functools.partial(one, qt, kt, True))
            return carry

        lax.fori_loop(0, q_tiles * subs, step, 0)

    grads[...] = acc[...].astype(grads.dtype)


def collect_kernel(own, *refs):
    parts, out = refs[:-1], refs[-1]
    total = own[...]
    for part in parts:
        total = total + part[...].astype(f32)
    chunk = out.shape[2]
    for i in range(out.shape[0]):
        out[i] = total[:, i * chunk : (i + 1) * chunk]


def finish_kernel(ways, got, grad_key, grad_value):
    groups = got.shape[0] // ways
    keys, values = [], []
    for g in range(groups):
        block = got[g * ways]
        for w in range(1, ways):
            block = block + got[g * ways + w]
        keys.append(block[:HEAD_DIM])
        values.append(block[HEAD_DIM:])
    grad_key[...] = jnp.concatenate(keys, axis=0).T
    grad_value[...] = jnp.concatenate(values, axis=0).T


def per_device(query, key, value, output, grad_out, lse, doc_ids):
    row_count, col_count = lax.axis_size("qrow"), lax.axis_size("kcol")
    col = lax.axis_index("kcol")
    rows, feats = query.shape
    heads = feats // HEAD_DIM
    key_rows, key_feats = key.shape
    pair_feats = 2 * HEAD_DIM
    core_swap = [(i, i ^ 1) for i in range(col_count)]

    def swap(x):
        return lax.ppermute(x, "kcol", core_swap)

    q_other, g_other, o_other, l_other = swap(query), swap(grad_out), swap(output), swap(lse)

    pieces = pl.pallas_call(
        functools.partial(pack_kernel, heads),
        in_specs=[VMEM_SPEC] * 2,
        out_specs=VMEM_SPEC,
        out_shape=jax.ShapeDtypeStruct((row_count, key_rows, pair_feats), bf16),
        compiler_params=small(),
        name="pack",
    )(key, value)
    pair = lax.all_to_all(pieces, "qrow", 0, 0).reshape(rows, pair_feats)

    doc_subs = doc_ids.reshape(-1, SUB)
    first, last = doc_subs[:, 0], doc_subs[:, SUB - 1]
    docs = doc_ids.reshape(col_count, rows).astype(f32)
    panel = jnp.stack([col, col ^ 1]).astype(jnp.int32)

    q_ext, g_ext, q_t, g_t = pl.pallas_call(
        prep_kernel,
        in_specs=[SMEM_SPEC] + [VMEM_SPEC] * 9,
        out_specs=[VMEM_SPEC] * 4,
        out_shape=[jax.ShapeDtypeStruct((heads, 2 * rows, 128), bf16)] * 2
        + [jax.ShapeDtypeStruct((feats, 2 * rows), bf16)] * 2,
        compiler_params=small(16),
        name="prep",
    )(panel, query, q_other, grad_out, g_other, output, o_other, lse, l_other, docs)

    def band(distance, block, dq):
        own = distance == 0
        extra = [] if dq is None else [dq]
        return pl.pallas_call(
            functools.partial(band_kernel, 2 * distance, SUB if own else 2 * SUB, dq is None),
            in_specs=[SMEM_SPEC] * 3 + [VMEM_SPEC] * (6 + len(extra)),
            out_specs=[VMEM_SPEC] * 2,
            out_shape=[
                jax.ShapeDtypeStruct((2 * rows, feats), f32),
                jax.ShapeDtypeStruct((pair_feats, rows), f32 if own else bf16),
            ],
            scratch_shapes=[pltpu.VMEM((pair_feats, rows), f32)] + [pltpu.VMEM((2, rows, 128), bf16)] * 3,
            input_output_aliases={} if dq is None else {9: 0},
            compiler_params=small(24),
            cost_estimate=pl.CostEstimate(
                flops=20 * rows * rows * feats,
                bytes_accessed=6 << 20,
                transcendentals=2 * rows * rows * heads,
            ),
            name=f"band{distance}",
        )(panel, first, last, q_ext, g_ext, q_t, g_t, docs, block, *extra)

    reach = min(col_count // 2 - 1, col_count // 4 + 1)
    blocks = {}
    for d in range(1, reach + 1):
        route = [(i, i + 2 * d) for i in range(col_count - 2 * d)]
        blocks[d] = lax.ppermute(pair, "kcol", route)
    dq = None
    returned = []
    for d in range(1, reach + 1):
        dq, grads = band(d, blocks[d], dq)
        route = [(i + 2 * d, i) for i in range(col_count - 2 * d)]
        returned.append(lax.ppermute(grads, "kcol", route))
        if d > 1:
            dq, returned[-2] = lax.optimization_barrier((dq, returned[-2]))
    dq, own_grads = band(0, pair, dq)

    dq_partner = swap(dq[rows:])
    grad_query = dq[:rows] + dq_partner

    chunks = pl.pallas_call(
        collect_kernel,
        in_specs=[VMEM_SPEC] * (1 + reach),
        out_specs=VMEM_SPEC,
        out_shape=jax.ShapeDtypeStruct((row_count, pair_feats, key_rows), f32),
        compiler_params=small(),
        name="collect",
    )(own_grads, *returned)
    got = lax.all_to_all(chunks, "qrow", 0, 0)
    grad_key, grad_value = pl.pallas_call(
        functools.partial(finish_kernel, row_count * HEAD_DIM // key_feats),
        in_specs=[VMEM_SPEC],
        out_specs=[VMEM_SPEC] * 2,
        out_shape=[jax.ShapeDtypeStruct((key_rows, key_feats), f32)] * 2,
        compiler_params=small(),
        name="finish",
    )(got)
    return grad_query, grad_key, grad_value


def solution(mesh):
    return jax.shard_map(
        per_device,
        mesh=mesh,
        in_specs=(
            P("kcol", "qrow"),
            P(("kcol", "qrow"), None),
            P(("kcol", "qrow"), None),
            P("kcol", "qrow"),
            P("kcol", "qrow"),
            P("qrow", "kcol"),
            P(),
        ),
        out_specs=(P("kcol", "qrow"), P(("kcol", "qrow"), None), P(("kcol", "qrow"), None)),
        check_vma=False,
    )
```

time: 72.1 us -> 71.5 us (level)
  the two profiles are of different devices: /device:TPU:8 before, /device:TPU:0 now
where the time goes in v2:
time: 71.5 us; the launch traced here: 70.3 us
  starting transfers between devices  28.2 us (39%)
  waiting for transfers between devices  17.7 us (25%)
  Pallas kernels  10.1 us (14%)
  blocking collectives  8.25 us (12%)
  local copies, waits for them, and re-layouts  4.27 us (6%)
  other arithmetic  0.94 us (1%)
  between operations  0.85 us (1%)
    ppermute x3, starting transfers between devices, per_device(): blocks[d] = lax.ppermute(pair, 'kcol', route)  18.1 us
    ppermute x3, waiting for transfers between devices, per_device(): returned.append(lax.ppermute(grads, 'kcol', route))  13.8 us
    all_to_all x1, blocking collectives, per_device(): got = lax.all_to_all(chunks, 'qrow', 0, 0)  8.25 us
    pallas_call x4, Pallas kernels, band(): pl.pallas_call(functools.partial(band_kernel, 2 * distance, SUB if own el...  6.67 us
    all_to_all x1, starting transfers between devices, per_device(): pair = lax.all_to_all(pieces, 'qrow', 0, 0).reshape(rows, pair_feats)  5.16 us
    ppermute x3, starting transfers between devices, per_device(): returned.append(lax.ppermute(grads, 'kcol', route))  3.88 us
    unnamed x14, local copies, waits for them, and re-layouts  3.34 us
    all_to_all x1, waiting for transfers between devices, per_device(): pair = lax.all_to_all(pieces, 'qrow', 0, 0).reshape(rows, pair_feats)  3.27 us
  transfers between devices with their start and end apart: 12, of which 4 were waited for; matrix products, arithmetic and copies ran while one was open for 1% of the time, Pallas kernels for 6%

profile of v2, /device:TPU:0, one launch (start us, length us, event | category | flops | bytes accessed | tf_op | source)
XLA Modules:
  0.0 70.3 jit_solution(8833456079150038414)
XLA Ops:
  0.6 0.0 copy-start
  0.6 0.0 copy-start.1
  0.7 0.0 copy-start.3
  0.7 0.9 %copy-done.3 = bf16[128,256]{1,0:T(8,128)(2,1)S(1)} copy-done((bf16[128,256]{1,0:T(8,128)(2,1)S(1)}, bf16[128,256]{1,0:T(8,128)(2,1)}, u32[]{:S(2)}) %copy-start.3) | copy-done | bytes 65560
  1.5 0.0 copy-start.4
  1.5 0.8 %copy-done.4 = bf16[128,256]{1,0:T(8,128)(2,1)S(1)} copy-done((bf16[128,256]{1,0:T(8,128)(2,1)S(1)}, bf16[128,256]{1,0:T(8,128)(2,1)}, u32[]{:S(2)}) %copy-start.4) | copy-done | bytes 65560
  2.4 0.8 %pack.1 = bf16[4,128,128]{2,1,0:T(8,128)(2,1)} custom-call(bf16[128,256]{1,0:T(8,128)(2,1)S(1)} %copy-done.3, bf16[128,256]{1,0:T(8,128)(2,1)S(1)} %copy-done.4), custom_call_target="tpu_custom_call" | custom-call | tf_op jit(solution)/shard_map/pack/pallas_call | solution.py:208
  3.1 5.2 %all-to-all-start = ((bf16[4,128,128]{2,1,0:T(8,128)(2,1)}), bf16[4,128,128]{2,1,0:T(8,128)(2,1)S(1)}, u32[]{:S(2)}, u32[]{:S(2)}) async-start(bf16[4,128,128]{2,1,0:T(8,128)(2,1)} %pack.1), calls=%async_computation | async-start | bytes 262144 | tf_op jit(solution)/shard_map/all_to_all | solution.py:216
  8.3 0.0 copy-done
  8.3 0.0 collective-permute-start
  8.3 0.5 collective-permute-start.2
  8.8 0.0 copy-done.1
  8.8 0.1 collective-permute-start.1
  8.9 0.4 collective-permute-start.3
  9.3 0.7 %reshape.14 = s32[16,256]{1,0:T(8,128)S(1)} reshape(s32[4096]{0:T(1024)} %param.13) | data formatting | bytes 32768 | tf_op jit(solution)/shard_map/reshape | solution.py:218
  10.1 3.3 %all-to-all-done = bf16[4,128,128]{2,1,0:T(8,128)(2,1)S(1)} async-done(((bf16[4,128,128]{2,1,0:T(8,128)(2,1)}), bf16[4,128,128]{2,1,0:T(8,128)(2,1)S(1)}, u32[]{:S(2)}, u32[]{:S(2)}) %all-to-all-start) | async-done | bytes 131104 | tf_op jit(solution)/shard_map/all_to_all | solution.py:216
  13.3 3.5 %collective-permute-start.6 = (bf16[512,128]{1,0:T(8,128)(2,1)S(1)}, bf16[512,128]{1,0:T(8,128)(2,1)S(1)}, u32[]{:S(2)}, u32[]{:S(2)}) collective-permute-start(bf16[512,128]{1,0:T(8,128)(2,1)S(1)} %bitcast.3), channel_id=1, source_target_pairs={{0,2},{1,3},{2,4},{3,5},{4,6},{5,7},{8,10},{9,11},{10,12},{11,13},... | collective-permute-start | bytes 393224 | tf_op jit(solution)/shard_map/ppermute | solution.py:259
  16.8 0.2 slice_reduce_fusion
  17.0 0.0 collective-permute-done.3.l1
  17.0 4.5 %collective-permute-start.5 = (bf16[512,128]{1,0:T(8,128)(2,1)S(1)}, bf16[512,128]{1,0:T(8,128)(2,1)S(1)}, u32[]{:S(2)}, u32[]{:S(2)}) collective-permute-start(bf16[512,128]{1,0:T(8,128)(2,1)S(1)} %bitcast.4), channel_id=1, source_target_pairs={{0,4},{1,5},{2,6},{3,7},{8,12},{9,13},{10,14},{11,15},{16,20},{17,... | collective-permute-start | bytes 393224 | tf_op jit(solution)/shard_map/ppermute | solution.py:259
  21.5 0.1 pad_add_fusion.panel.refs_0_
  21.6 0.0 copy-done.6
  21.6 0.0 collective-permute-done.q1
  21.6 0.0 collective-permute-done.2.o1
  21.6 0.0 collective-permute-done.1.g1
  21.6 0.6 copy-done.5
  22.3 0.9 %copy-done.2 = bf16[512,256]{1,0:T(8,128)(2,1)S(1)} copy-done((bf16[512,256]{1,0:T(8,128)(2,1)S(1)}, bf16[512,256]{1,0:T(8,128)(2,1)}, u32[]{:S(2)}) %copy-start.2) | copy-done | bytes 262168
  23.2 1.8 %prep.1 = (bf16[4,1024,128]{2,1,0:T(8,128)(2,1)S(1)}, bf16[4,1024,128]{2,1,0:T(8,128)(2,1)S(1)}, bf16[256,1024]{1,0:T(8,128)(2,1)S(1)}, bf16[256,1024]{1,0:T(8,128)(2,1)S(1)}) custom-call(s32[2]{0:T(128)S(1)} %pad_add_fusion.panel.refs_0_, bf16[512,256]{1,0:T(8,128)(2,1)S(1)} %copy-done, bf16[512,256]{1,0:T(8,128)(2,1)S(1)} %collective-permute-done.q1, ...), custom_call_target="tpu_custom_call" | custom-call | tf_op jit(solution)/shard_map/prep/pallas_call | solution.py:223
  25.1 0.0 collective-permute-done.6.refs_8_
  25.1 0.7 band1.1
  25.8 1.3 %collective-permute-start.7 = (bf16[128,512]{1,0:T(8,128)(2,1)S(1)}, bf16[128,512]{1,0:T(8,128)(2,1)S(1)}, u32[]{:S(2)}, u32[]{:S(2)}) collective-permute-start(bf16[128,512]{1,0:T(8,128)(2,1)S(1)} %get-tuple-element.27), channel_id=1, source_target_pairs={{2,0},{3,1},{4,2},{5,3},{6,4},{7,5},{10,8},{11,9},{12,10},{13,11},... | collective-permute-start | bytes 393224 | tf_op jit(solution)/shard_map/ppermute | solution.py:265
  27.1 10.1 %collective-permute-start.4 = (bf16[512,128]{1,0:T(8,128)(2,1)S(1)}, bf16[512,128]{1,0:T(8,128)(2,1)S(1)}, u32[]{:S(2)}, u32[]{:S(2)}) collective-permute-start(bf16[512,128]{1,0:T(8,128)(2,1)S(1)} %bitcast.5), channel_id=1, source_target_pairs={{0,6},{1,7},{8,14},{9,15},{16,22},{17,23},{24,30},{25,31}} | collective-permute-start | bytes 393224 | tf_op jit(solution)/shard_map/ppermute | solution.py:259
  37.2 0.0 collective-permute-done.5.refs_8_
  37.2 0.6 band2.1
  37.8 1.3 %collective-permute-start.8 = (bf16[128,512]{1,0:T(8,128)(2,1)S(1)}, bf16[128,512]{1,0:T(8,128)(2,1)S(1)}, u32[]{:S(2)}, u32[]{:S(2)}) collective-permute-start(bf16[128,512]{1,0:T(8,128)(2,1)S(1)} %get-tuple-element.30), channel_id=1, source_target_pairs={{4,0},{5,1},{6,2},{7,3},{12,8},{13,9},{14,10},{15,11},{20,16},{21,... | collective-permute-start | bytes 393224 | tf_op jit(solution)/shard_map/ppermute | solution.py:265
  39.1 0.0 collective-permute-done.7.refs_0_
  39.1 0.6 collective-permute-done.4.refs_8_
  39.7 0.6 band3.1
  40.3 5.5 %collective-permute-done.8.refs_1_ = bf16[128,512]{1,0:T(8,128)(2,1)S(1)} collective-permute-done((bf16[128,512]{1,0:T(8,128)(2,1)S(1)}, bf16[128,512]{1,0:T(8,128)(2,1)S(1)}, u32[]{:S(2)}, u32[]{:S(2)}) %collective-permute-start.8) | collective-permute-done | bytes 131104 | tf_op jit(solution)/shard_map/ppermute | solution.py:265
  45.8 4.8 %band0.1 = (f32[1024,256]{1,0:T(8,128)S(1)}, f32[128,512]{1,0:T(8,128)S(1)}) custom-call(s32[2]{0:T(128)S(1)} %pad_add_fusion.panel.refs_0_, s32[16]{0:T(128)S(1)} %get-tuple-element.40.refs_1_, s32[16]{0:T(128)S(1)} %get-tuple-element.39.refs_2_, bf16[4,1024,128]{2,1,0:T(8,128)(2,1)S(1)} %get-tuple-element.21.refs_3_, ...), custom_call_target="tpu_custom_call", output_to_operand_aliasing={{0}: (9, {})} | custom-call | flops 1342177280 | bytes 6291456 | tf_op jit(solution)/shard_map/band0/pallas_call | solution.py:236
  50.7 0.1 collective-permute-start.9
  50.8 1.3 %collective-permute-start.10 = (bf16[128,512]{1,0:T(8,128)(2,1)S(1)}, bf16[128,512]{1,0:T(8,128)(2,1)S(1)}, u32[]{:S(2)}, u32[]{:S(2)}) collective-permute-start(bf16[128,512]{1,0:T(8,128)(2,1)S(1)} %get-tuple-element.36), channel_id=1, source_target_pairs={{6,0},{7,1},{14,8},{15,9},{22,16},{23,17},{30,24},{31,25}} | collective-permute-start | bytes 393224 | tf_op jit(solution)/shard_map/ppermute | solution.py:265
  52.1 8.3 %collective-permute-done.10.refs_2_ = bf16[128,512]{1,0:T(8,128)(2,1)S(1)} collective-permute-done((bf16[128,512]{1,0:T(8,128)(2,1)S(1)}, bf16[128,512]{1,0:T(8,128)(2,1)S(1)}, u32[]{:S(2)}, u32[]{:S(2)}) %collective-permute-start.10) | collective-permute-done | bytes 131104 | tf_op jit(solution)/shard_map/ppermute | solution.py:265
  60.3 0.1 collect.1
  60.4 8.2 %all_to_all.10.got = f32[4,128,128]{2,1,0:T(8,128)S(1)} all-to-all(f32[4,128,128]{2,1,0:T(8,128)S(1)} %collect.1), channel_id=1, replica_groups=mesh['qrow'=4,'kcol'=8] {'qrow'}, dimensions={0} | all-to-all | bytes 524288 | tf_op jit(solution)/shard_map/all_to_all | solution.py:281
  68.7 0.8 %finish.1 = (f32[128,256]{1,0:T(8,128)}, f32[128,256]{1,0:T(8,128)}) custom-call(f32[4,128,128]{2,1,0:T(8,128)S(1)} %all_to_all.10.got), custom_call_target="tpu_custom_call" | custom-call | tf_op jit(solution)/shard_map/finish/pallas_call | solution.py:282
  69.5 0.0 collective-permute-done.9
  69.5 0.9 %slice_add_fusion = f32[512,256]{1,0:T(8,128)} fusion(f32[512,256]{1,0:T(8,128)S(1)} %collective-permute-done.9, f32[1024,256]{1,0:T(8,128)S(1)} %get-tuple-element.32), kind=kLoop, calls=%fused_computation | loop fusion | flops 131072 | bytes 1572864 | tf_op jit(solution)/shard_map/add | solution.py:271
  (6 shorter events, 0.0 us)
Async XLA Ops:
  0.6 7.7 %copy-start = (bf16[512,256]{1,0:T(8,128)(2,1)S(1)}, bf16[512,256]{1,0:T(8,128)(2,1)}, u32[]{:S(2)}) copy-start(bf16[512,256]{1,0:T(8,128)(2,1)} %q0.1) | copy-start | bytes 786436
  0.6 8.2 %copy-start.1 = (bf16[512,256]{1,0:T(8,128)(2,1)S(1)}, bf16[512,256]{1,0:T(8,128)(2,1)}, u32[]{:S(2)}) copy-start(bf16[512,256]{1,0:T(8,128)(2,1)} %g0.1) | copy-start | bytes 786436
  0.7 0.9 %copy-start.3 = (bf16[128,256]{1,0:T(8,128)(2,1)S(1)}, bf16[128,256]{1,0:T(8,128)(2,1)}, u32[]{:S(2)}) copy-start(bf16[128,256]{1,0:T(8,128)(2,1)} %key.1) | copy-start | bytes 196612
  1.5 0.8 %copy-start.4 = (bf16[128,256]{1,0:T(8,128)(2,1)S(1)}, bf16[128,256]{1,0:T(8,128)(2,1)}, u32[]{:S(2)}) copy-start(bf16[128,256]{1,0:T(8,128)(2,1)} %value.1) | copy-start | bytes 196612
  3.1 10.2 %all-to-all-start = ((bf16[4,128,128]{2,1,0:T(8,128)(2,1)}), bf16[4,128,128]{2,1,0:T(8,128)(2,1)S(1)}, u32[]{:S(2)}, u32[]{:S(2)}) async-start(bf16[4,128,128]{2,1,0:T(8,128)(2,1)} %pack.1), calls=%async_computation | async-start | bytes 262144 | tf_op jit(solution)/shard_map/all_to_all | solution.py:216
  8.3 13.3 %collective-permute-start = (bf16[512,256]{1,0:T(8,128)(2,1)S(1)}, bf16[512,256]{1,0:T(8,128)(2,1)S(1)}, u32[]{:S(2)}, u32[]{:S(2)}) collective-permute-start(bf16[512,256]{1,0:T(8,128)(2,1)S(1)} %copy-done), channel_id=1, source_target_pairs={{0,1},{1,0},{2,3},{3,2},{4,5},{5,4},{6,7},{7,6},{8,9},{9,8},{10,11... | collective-permute-start | bytes 786440 | tf_op jit(solution)/shard_map/ppermute | solution.py:204
  8.3 13.3 %collective-permute-start.2 = (bf16[512,256]{1,0:T(8,128)(2,1)}, bf16[512,256]{1,0:T(8,128)(2,1)S(1)}, u32[]{:S(2)}, u32[]{:S(2)}) collective-permute-start(bf16[512,256]{1,0:T(8,128)(2,1)} %o0.1), channel_id=1, source_target_pairs={{0,1},{1,0},{2,3},{3,2},{4,5},{5,4},{6,7},{7,6},{8,9},{9,8},{10,11... | collective-permute-start | bytes 786440 | tf_op jit(solution)/shard_map/ppermute | solution.py:204
  8.8 12.8 %collective-permute-start.1 = (bf16[512,256]{1,0:T(8,128)(2,1)S(1)}, bf16[512,256]{1,0:T(8,128)(2,1)S(1)}, u32[]{:S(2)}, u32[]{:S(2)}) collective-permute-start(bf16[512,256]{1,0:T(8,128)(2,1)S(1)} %copy-done.1), channel_id=1, source_target_pairs={{0,1},{1,0},{2,3},{3,2},{4,5},{5,4},{6,7},{7,6},{8,9},{9,8},{10,11... | collective-permute-start | bytes 786440 | tf_op jit(solution)/shard_map/ppermute | solution.py:204
  8.9 8.1 %collective-permute-start.3 = (f32[4,512]{1,0:T(4,128)}, f32[4,512]{1,0:T(4,128)S(1)}, u32[]{:S(2)}, u32[]{:S(2)}) collective-permute-start(f32[4,512]{1,0:T(4,128)} %l0.1), channel_id=1, source_target_pairs={{0,1},{1,0},{2,3},{3,2},{4,5},{5,4},{6,7},{7,6},{8,9},{9,8},{10,11... | collective-permute-start | bytes 24584 | tf_op jit(solution)/shard_map/ppermute | solution.py:204
  10.1 11.5 %copy-start.6 = (s32[4096]{0:T(1024)S(1)}, s32[4096]{0:T(1024)}, u32[]{:S(2)}) copy-start(s32[4096]{0:T(1024)} %param.13) | copy-start | bytes 49156
  13.3 11.8 %collective-permute-start.6 = (bf16[512,128]{1,0:T(8,128)(2,1)S(1)}, bf16[512,128]{1,0:T(8,128)(2,1)S(1)}, u32[]{:S(2)}, u32[]{:S(2)}) collective-permute-start(bf16[512,128]{1,0:T(8,128)(2,1)S(1)} %bitcast.3), channel_id=1, source_target_pairs={{0,2},{1,3},{2,4},{3,5},{4,6},{5,7},{8,10},{9,11},{10,12},{11,13},... | collective-permute-start | bytes 393224 | tf_op jit(solution)/shard_map/ppermute | solution.py:259
  17.0 20.2 %collective-permute-start.5 = (bf16[512,128]{1,0:T(8,128)(2,1)S(1)}, bf16[512,128]{1,0:T(8,128)(2,1)S(1)}, u32[]{:S(2)}, u32[]{:S(2)}) collective-permute-start(bf16[512,128]{1,0:T(8,128)(2,1)S(1)} %bitcast.4), channel_id=1, source_target_pairs={{0,4},{1,5},{2,6},{3,7},{8,12},{9,13},{10,14},{11,15},{16,20},{17,... | collective-permute-start | bytes 393224 | tf_op jit(solution)/shard_map/ppermute | solution.py:259
  21.6 0.7 copy-start.5
  22.3 0.9 %copy-start.2 = (bf16[512,256]{1,0:T(8,128)(2,1)S(1)}, bf16[512,256]{1,0:T(8,128)(2,1)}, u32[]{:S(2)}) copy-start(bf16[512,256]{1,0:T(8,128)(2,1)} %o0.1) | copy-start | bytes 786436
  25.8 13.3 %collective-permute-start.7 = (bf16[128,512]{1,0:T(8,128)(2,1)S(1)}, bf16[128,512]{1,0:T(8,128)(2,1)S(1)}, u32[]{:S(2)}, u32[]{:S(2)}) collective-permute-start(bf16[128,512]{1,0:T(8,128)(2,1)S(1)} %get-tuple-element.27), channel_id=1, source_target_pairs={{2,0},{3,1},{4,2},{5,3},{6,4},{7,5},{10,8},{11,9},{12,10},{13,11},... | collective-permute-start | bytes 393224 | tf_op jit(solution)/shard_map/ppermute | solution.py:265
  27.1 12.6 %collective-permute-start.4 = (bf16[512,128]{1,0:T(8,128)(2,1)S(1)}, bf16[512,128]{1,0:T(8,128)(2,1)S(1)}, u32[]{:S(2)}, u32[]{:S(2)}) collective-permute-start(bf16[512,128]{1,0:T(8,128)(2,1)S(1)} %bitcast.5), channel_id=1, source_target_pairs={{0,6},{1,7},{8,14},{9,15},{16,22},{17,23},{24,30},{25,31}} | collective-permute-start | bytes 393224 | tf_op jit(solution)/shard_map/ppermute | solution.py:259
  37.8 8.0 %collective-permute-start.8 = (bf16[128,512]{1,0:T(8,128)(2,1)S(1)}, bf16[128,512]{1,0:T(8,128)(2,1)S(1)}, u32[]{:S(2)}, u32[]{:S(2)}) collective-permute-start(bf16[128,512]{1,0:T(8,128)(2,1)S(1)} %get-tuple-element.30), channel_id=1, source_target_pairs={{4,0},{5,1},{6,2},{7,3},{12,8},{13,9},{14,10},{15,11},{20,16},{21,... | collective-permute-start | bytes 393224 | tf_op jit(solution)/shard_map/ppermute | solution.py:265
  50.7 18.8 %collective-permute-start.9 = (f32[512,256]{1,0:T(8,128)S(1)}, f32[512,256]{1,0:T(8,128)S(1)}, u32[]{:S(2)}, u32[]{:S(2)}) collective-permute-start(f32[512,256]{1,0:T(8,128)S(1)} %slice.15), channel_id=1, source_target_pairs={{0,1},{1,0},{2,3},{3,2},{4,5},{5,4},{6,7},{7,6},{8,9},{9,8},{10,11... | collective-permute-start | bytes 1572872 | tf_op jit(solution)/shard_map/ppermute | solution.py:204
  50.8 9.6 %collective-permute-start.10 = (bf16[128,512]{1,0:T(8,128)(2,1)S(1)}, bf16[128,512]{1,0:T(8,128)(2,1)S(1)}, u32[]{:S(2)}, u32[]{:S(2)}) collective-permute-start(bf16[128,512]{1,0:T(8,128)(2,1)S(1)} %get-tuple-element.36), channel_id=1, source_target_pairs={{6,0},{7,1},{14,8},{15,9},{22,16},{23,17},{30,24},{31,25}} | collective-permute-start | bytes 393224 | tf_op jit(solution)/shard_map/ppermute | solution.py:265

commit v3 on v2

v3 whole, which is shorter than its diff:
```python
import functools
import jax
import jax.numpy as jnp
from jax import lax
from jax.experimental import pallas as pl
from jax.experimental.pallas import tpu as pltpu
from jax.sharding import PartitionSpec as P

HEAD_DIM = 64
GROUP = 4
DOCS = 16
FAR = 512.0
SUB = 256
EXTRA = 8
FAR_STEP = 2
PREP_MIB = 56
LOG2E = 1.4426950408889634
SCORE_SCALE = 0.125

f32, bf16 = jnp.float32, jnp.bfloat16
VMEM_SPEC = pl.BlockSpec(memory_space=pltpu.VMEM)
SMEM_SPEC = pl.BlockSpec(memory_space=pltpu.SMEM)


def small(mib=4):
    return pltpu.CompilerParams(vmem_limit_bytes=mib << 20)


def nt(a, b):
    return lax.dot_general(a, b, (((1,), (1,)), ((), ())), preferred_element_type=f32)


def nn(a, b):
    return lax.dot_general(a, b, (((1,), (0,)), ((), ())), preferred_element_type=f32)


def halves_swapped(x):
    return jnp.concatenate([x[:, HEAD_DIM:], x[:, :HEAD_DIM]], axis=1)


def three(x):
    high = x.astype(bf16).astype(f32)
    rest = x - high
    middle = rest.astype(bf16).astype(f32)
    return high, middle, rest - middle


def one_hot_rows(doc_row, value):
    length = doc_row.shape[1]
    ids = lax.broadcasted_iota(jnp.int32, (DOCS, length), 0).astype(f32)
    return jnp.where(ids == doc_row, value, 0.0)


def prep_kernel(key, value, query, grad_out, output, lse, pieces, packed):
    rows, feats = query.shape
    heads = feats // HEAD_DIM
    for r in range(pieces.shape[0]):
        g = r * heads // GROUP
        at = slice(g * HEAD_DIM, (g + 1) * HEAD_DIM)
        pieces[r] = jnp.concatenate([key[:, at], value[:, at]], axis=1)
    packed[:, :feats] = query[...]
    packed[:, feats : 2 * feats] = grad_out[...]
    product = grad_out[...].astype(f32) * output[...].astype(f32)
    high = product.astype(bf16)
    low = (product - high.astype(f32)).astype(bf16)
    head = lax.broadcasted_iota(jnp.int32, (feats, 128), 0) // HEAD_DIM
    spot = lax.broadcasted_iota(jnp.int32, (feats, 128), 1) - EXTRA * head
    pick = jnp.where((spot >= 3) & (spot < 6), -1.0, 0.0).astype(bf16)
    d0, d1, d2 = three(nn(high, pick) + nn(low, pick))
    table = []
    for h in range(heads):
        table += list(three(-FAR - lse[h : h + 1, :])) + [jnp.zeros((EXTRA - 3, rows), f32)]
    table.append(jnp.zeros((128 - EXTRA * heads, rows), f32))
    place = lax.broadcasted_iota(jnp.int32, (rows, 128), 1) % EXTRA
    delta = jnp.where(place == 3, d0, jnp.where(place == 4, d1, d2))
    packed[:, 2 * feats :] = (jnp.concatenate(table, axis=0).T + delta).astype(bf16)


def expand_kernel(sides, panel, *refs):
    packs, docs = refs[:sides], refs[sides]
    q_ext, g_ext, q_t, g_t = refs[sides + 1 :]
    feats = q_t.shape[0]
    heads = feats // HEAD_DIM
    rows = docs.shape[1]
    lane = lax.broadcasted_iota(jnp.int32, (rows, 128), 1)
    low_half = lane < HEAD_DIM
    source = lax.broadcasted_iota(jnp.int32, (128, 128), 0)
    target = lax.broadcasted_iota(jnp.int32, (128, 128), 1)
    offset = target % HEAD_DIM
    for side, packed in enumerate(packs):
        dst = slice(side * rows, (side + 1) * rows)
        doc_row = docs[pl.ds(panel[side], 1), :].astype(f32)
        half = [jnp.zeros((3, rows), f32), one_hot_rows(doc_row, FAR), jnp.zeros((HEAD_DIM - 3 - DOCS, rows), f32)]
        spread = jnp.concatenate(half + half, axis=0).T
        extra = packed[:, 2 * feats :]
        for p in range(heads // 2):
            at = slice(p * 128, (p + 1) * 128)
            q_pair = packed[:, at].astype(f32) * SCORE_SCALE
            g_pair = packed[:, feats + p * 128 : feats + (p + 1) * 128].astype(f32)
            q_t[at, dst] = q_pair.T.astype(bf16)
            g_t[at, dst] = g_pair.T.astype(bf16)
            base = EXTRA * jnp.where(target < HEAD_DIM, 2 * p + 1, 2 * p)
            move_q = jnp.where((source == base + offset) & (offset < 3), 1.0, 0.0).astype(bf16)
            move_g = jnp.where((source == base + 3 + offset) & (offset < 3), 1.0, 0.0).astype(bf16)
            q_more = nn(extra, move_q) + spread
            g_more = nn(extra, move_g)
            q_ext[2 * p, dst, :] = jnp.where(low_half, q_pair, q_more).astype(bf16)
            q_ext[2 * p + 1, dst, :] = jnp.where(low_half, q_more, q_pair).astype(bf16)
            g_ext[2 * p, dst, :] = jnp.where(low_half, g_pair, g_more).astype(bf16)
            g_ext[2 * p + 1, dst, :] = jnp.where(low_half, g_more, g_pair).astype(bf16)


def band_kernel(causal, q_tile, key_panels, chained, *refs):
    q_panel, k_panel, first, last, q_ext, g_ext, q_t, g_t, docs = refs[:9]
    pairs = refs[9 : 9 + key_panels]
    refs = refs[9 + key_panels + (1 if chained else 0) :]
    dq_out, grads = refs[0], refs[1 : 1 + key_panels]
    acc, k_ext, v_ext, k_lone, *more = refs[1 + key_panels :]
    dq = more[0] if more else dq_out
    heads, q_rows, _ = q_ext.shape
    rows = pairs[0].shape[0]
    subs = rows // SUB
    q_subs = q_tile // SUB
    per_panel = rows // q_tile
    q_tiles = q_rows // q_tile
    if not chained:
        dq[...] = jnp.zeros_like(dq)
    acc[...] = jnp.zeros_like(acc)

    def one(qt, kt, masked):
        at_q = pl.ds(pl.multiple_of(qt * q_tile, q_tile), q_tile)
        at_k = pl.ds(pl.multiple_of(kt * SUB, SUB), SUB)
        weights, score_grads = [], []
        if masked:
            ahead = (qt % per_panel) * q_tile - kt * SUB
            q_pos = lax.broadcasted_iota(jnp.int32, (q_tile, SUB), 0) + ahead
            live = lax.broadcasted_iota(jnp.int32, (q_tile, SUB), 1) <= q_pos
        for h in range(heads):
            weight = jnp.exp2(nt(q_ext[h, at_q, :], k_ext[h % 2, at_k, :]) * LOG2E)
            if masked:
                weight = jnp.where(live, weight, 0.0)
            grad = nt(g_ext[h, at_q, :], v_ext[h % 2, at_k, :])
            weights.append(weight.astype(bf16))
            score_grads.append((weight * grad).astype(bf16))
        key_sum = value_sum = 0.0
        for h in range(heads):
            at = slice(h * HEAD_DIM, (h + 1) * HEAD_DIM)
            key_sum += nn(q_t[at, at_q], score_grads[h])
            value_sum += nn(g_t[at, at_q], weights[h])
        for p in range(heads // 2):
            dq[at_q, p * 128 : (p + 1) * 128] += nn(score_grads[2 * p], k_lone[0, at_k, :]) + nn(
                score_grads[2 * p + 1], k_lone[1, at_k, :]
            )
        acc[:HEAD_DIM, at_k] += key_sum
        acc[HEAD_DIM:, at_k] += value_sum

    @pl.when((k_panel[0] >= 0) & (q_panel[0] >= 0))
    def _():
        lane = lax.broadcasted_iota(jnp.int32, (rows, 128), 1)
        low_half = lane < HEAD_DIM
        ones = jnp.where(lane % HEAD_DIM < 3, 1.0, 0.0)
        for j, pair in enumerate(pairs):
            dst = slice(j * rows, (j + 1) * rows)
            doc_row = docs[pl.ds(k_panel[j], 1), :].astype(f32)
            half = [
                jnp.ones((3, rows), f32),
                one_hot_rows(doc_row, 1.0),
                jnp.zeros((HEAD_DIM - 3 - DOCS, rows), f32),
            ]
            extra = jnp.concatenate(half + half, axis=0).T
            straight = pair[...].astype(f32)
            turned = halves_swapped(pair[...]).astype(f32)
            k_ext[0, dst, :] = jnp.where(low_half, straight, extra).astype(bf16)
            k_ext[1, dst, :] = jnp.where(low_half, extra, turned).astype(bf16)
            v_ext[0, dst, :] = jnp.where(low_half, turned, ones).astype(bf16)
            v_ext[1, dst, :] = jnp.where(low_half, ones, straight).astype(bf16)
            k_lone[0, dst, :] = jnp.where(low_half, straight * SCORE_SCALE, 0.0).astype(bf16)
            k_lone[1, dst, :] = jnp.where(low_half, 0.0, turned * SCORE_SCALE).astype(bf16)

        def step(index, carry):
            qt, kt = index // (subs * key_panels), index % (subs * key_panels)
            q_side, k_side = q_panel[qt // per_panel], k_panel[kt // subs]
            q_sub, k_sub = (qt % per_panel) * q_subs, kt % subs
            live = first[q_side * subs + q_sub] <= last[k_side * subs + k_sub]
            if not causal:
                pl.when(live)(functools.partial(one, qt, kt, False))
            else:
                q_at, k_at = q_side * subs + q_sub, k_side * subs + k_sub
                live = live & (k_at < q_at + q_subs)
                below = k_at < q_at
                pl.when(live & below)(functools.partial(one, qt, kt, False))
                pl.when(live & jnp.logical_not(below))(functools.partial(one, qt, kt, True))
            return carry

        lax.fori_loop(0, q_tiles * subs * key_panels, step, 0)

    for j in range(key_panels):
        grads[j][...] = acc[:, j * rows : (j + 1) * rows].astype(grads[j].dtype)
    if more:
        dq_out[...] = dq[...].astype(dq_out.dtype)


def collect_kernel(*refs):
    parts, out = refs[:-1], refs[-1]
    total = parts[0][...]
    for part in parts[1:]:
        total = total + part[...].astype(f32)
    chunk = out.shape[2]
    for i in range(out.shape[0]):
        out[i] = total[:, i * chunk : (i + 1) * chunk]


def finish_kernel(ways, count, got, dq, *refs):
    parts, (grad_query, grad_key, grad_value) = refs[:count], refs[count:]
    groups = got.shape[0] // ways
    keys, values = [], []
    for g in range(groups):
        block = got[g * ways]
        for w in range(1, ways):
            block = block + got[g * ways + w]
        keys.append(block[:HEAD_DIM])
        values.append(block[HEAD_DIM:])
    grad_key[...] = jnp.concatenate(keys, axis=0).T
    grad_value[...] = jnp.concatenate(values, axis=0).T
    total = dq[: grad_query.shape[0], :]
    for part in parts:
        total = total + part[...].astype(f32)
    grad_query[...] = total


def per_device(query, key, value, output, grad_out, lse, doc_ids):
    row_count, col_count = lax.axis_size("qrow"), lax.axis_size("kcol")
    col = lax.axis_index("kcol")
    rows, feats = query.shape
    heads = feats // HEAD_DIM
    key_rows, key_feats = key.shape
    pair_feats = 2 * HEAD_DIM
    chips = col_count // 2

    def swap(x):
        return lax.ppermute(x, "kcol", [(i, i ^ 1) for i in range(col_count)])

    def up(x, d):
        return lax.ppermute(x, "kcol", [(i, i + 2 * d) for i in range(col_count - 2 * d)])

    def down(x, d):
        return lax.ppermute(x, "kcol", [(i + 2 * d, i) for i in range(col_count - 2 * d)])

    pieces, packed = pl.pallas_call(
        prep_kernel,
        in_specs=[VMEM_SPEC] * 6,
        out_specs=[VMEM_SPEC] * 2,
        out_shape=[
            jax.ShapeDtypeStruct((row_count, key_rows, pair_feats), bf16),
            jax.ShapeDtypeStruct((rows, 2 * feats + 128), bf16),
        ],
        compiler_params=small(PREP_MIB),
        name="prep",
    )(key, value, query, grad_out, output, lse)
    pair = lax.all_to_all(pieces, "qrow", 0, 0).reshape(rows, pair_feats)
    packed_other = swap(packed)
    packed_far = down(packed, FAR_STEP)

    docs = doc_ids.reshape(col_count, rows)
    first, last = docs[:, ::SUB].reshape(-1), docs[:, SUB - 1 :: SUB].reshape(-1)

    def panels(*items):
        inside = [jnp.where((p >= 0) & (p < col_count), p, -1) for p in items]
        return jnp.stack(inside).astype(jnp.int32)

    mine = panels(col, col ^ 1)
    far = panels(col + 2 * FAR_STEP)

    def expand(panel, *packs):
        span = len(packs) * rows
        return pl.pallas_call(
            functools.partial(expand_kernel, len(packs)),
            in_specs=[SMEM_SPEC] + [VMEM_SPEC] * (len(packs) + 1),
            out_specs=[VMEM_SPEC] * 4,
            out_shape=[jax.ShapeDtypeStruct((heads, span, 128), bf16)] * 2
            + [jax.ShapeDtypeStruct((feats, span), bf16)] * 2,
            compiler_params=small(16),
            name=f"expand{len(packs)}",
        )(panel, *packs, docs)

    def band(name, q_panel, k_panel, queries, pairs, dq, q_tile, causal, out_types, dq_type=f32):
        chained = dq is not None
        extra = [dq] if chained else []
        count = len(pairs)
        q_rows = queries[0].shape[1]
        scratch = [pltpu.VMEM((pair_feats, count * rows), f32)] + [pltpu.VMEM((2, count * rows, 128), bf16)] * 3
        if dq_type != f32:
            scratch.append(pltpu.VMEM((q_rows, feats), f32))
        return pl.pallas_call(
            functools.partial(band_kernel, causal, q_tile, count, chained),
            in_specs=[SMEM_SPEC] * 4 + [VMEM_SPEC] * (5 + count + len(extra)),
            out_specs=[VMEM_SPEC] * (1 + count),
            out_shape=[jax.ShapeDtypeStruct((q_rows, feats), dq_type)]
            + [jax.ShapeDtypeStruct((pair_feats, rows), t) for t in out_types],
            scratch_shapes=scratch,
            input_output_aliases={9 + count: 0} if chained else {},
            compiler_params=small(24),
            cost_estimate=pl.CostEstimate(
                flops=10 * q_rows * count * rows * feats,
                bytes_accessed=6 << 20,
                transcendentals=q_rows * count * rows * heads,
            ),
            name=name,
        )(q_panel, k_panel, first, last, *queries, docs, *pairs, *extra)

    reach = min(chips - 1, chips // 2 + 1)
    steps = [d for d in range(1, reach + 1) if d != FAR_STEP]
    blocks = {d: up(pair, d) for d in steps}
    pair_other = swap(pair)

    queries = expand(mine, packed, packed_other)
    dq, own_grads = band("own", mine, panels(col), queries, [pair], None, SUB, True, [f32])
    grads = {}
    for d in steps:
        dq, grads[d] = band(
            f"band{d}", mine, panels(col - 2 * d), queries, [blocks[d]], dq, 2 * SUB, False, [bf16]
        )
    far_queries = expand(jnp.maximum(far, 0), packed_far)
    far_dq, far_own, far_other = band(
        "far", far, mine, far_queries, [pair, pair_other], None, 2 * SUB, False, [f32, bf16], bf16
    )
    dq, far_dq, far_other, *sent = lax.optimization_barrier((dq, far_dq, far_other, *[grads[d] for d in steps]))
    returned = [down(x, d) for x, d in zip(sent, steps)]
    returned.append(swap(far_other))
    dq_parts = [swap(dq[rows:]), up(far_dq, FAR_STEP)]

    chunks = pl.pallas_call(
        collect_kernel,
        in_specs=[VMEM_SPEC] * (2 + len(returned)),
        out_specs=VMEM_SPEC,
        out_shape=jax.ShapeDtypeStruct((row_count, pair_feats, key_rows), f32),
        compiler_params=small(),
        name="collect",
    )(own_grads, far_own, *returned)
    got = lax.all_to_all(chunks, "qrow", 0, 0)
    return pl.pallas_call(
        functools.partial(finish_kernel, row_count * HEAD_DIM // key_feats, len(dq_parts)),
        in_specs=[VMEM_SPEC] * (2 + len(dq_parts)),
        out_specs=[VMEM_SPEC] * 3,
        out_shape=[jax.ShapeDtypeStruct((rows, feats), f32)]
        + [jax.ShapeDtypeStruct((key_rows, key_feats), f32)] * 2,
        compiler_params=small(8),
        name="finish",
    )(got, dq, *dq_parts)


def solution(mesh):
    return jax.shard_map(
        per_device,
        mesh=mesh,
        in_specs=(
            P("kcol", "qrow"),
            P(("kcol", "qrow"), None),
            P(("kcol", "qrow"), None),
            P("kcol", "qrow"),
            P("kcol", "qrow"),
            P("qrow", "kcol"),
            P(),
        ),
        out_specs=(P("kcol", "qrow"), P(("kcol", "qrow"), None), P(("kcol", "qrow"), None)),
        check_vma=False,
    )
```

time: 71.5 us -> 63.2 us (0.88); the launches traced: 70.3 us -> 62.7 us
  blocking collectives: 8.25 us -> 0 us
  waiting for transfers between devices: 17.7 us -> 24 us
  starting transfers between devices: 28.2 us -> 23.9 us
  local copies, waits for them, and re-layouts: 4.27 us -> 1.43 us
  Pallas kernels: 10.1 us -> 12.5 us
  other arithmetic: 0.94 us -> 0.08 us
    all_to_all x1 -> x0, blocking collectives: 8.25 us -> none  [per_device(): got = lax.all_to_all(chunks, 'qrow', 0, 0)]
    ppermute x11 -> x10, starting transfers between devices: 23.1 us -> 14.8 us  [the longest x3 9.82 us: up(): lax.ppermute(x, 'kcol', [(i, i + 2 * d) for i in range(col_count - 2 * d)])]
    all_to_all x0 -> x1, waiting for transfers between devices: none -> 5.37 us  [per_device(): got = lax.all_to_all(chunks, 'qrow', 0, 0)]
    all_to_all x0 -> x1, starting transfers between devices: none -> 4.39 us  [per_device(): got = lax.all_to_all(chunks, 'qrow', 0, 0)]
    unnamed x14 -> x4, local copies, waits for them, and re-layouts: 3.34 us -> 1.08 us
    pallas_call x7 -> x8, Pallas kernels: 9.32 us -> 11.5 us  [the longest x4 6.45 us: band(): pl.pallas_call(functools.partial(band_kernel, causal, q_tile, count, chai...]
    all_to_all x1, waiting for transfers between devices: 3.27 us -> 5.02 us  [per_device(): pair = lax.all_to_all(pieces, 'qrow', 0, 0).reshape(rows, pair_feats)]
    add x1 -> x0, other arithmetic: 0.86 us -> none  [per_device(): grad_query = dq[:rows] + dq_partner]
  transfers between devices with their start and end apart: 12 -> 12, of which waited for: 4 -> 5; matrix products, arithmetic and copies ran while one was open for 1% -> 1% of each run, Pallas kernels for 6% -> 13%
where the time goes in v3:
time: 63.2 us; the launch traced here: 62.7 us
  waiting for transfers between devices  24 us (38%)
  starting transfers between devices  23.9 us (38%)
  Pallas kernels  12.5 us (20%)
  local copies, waits for them, and re-layouts  1.43 us (2%)
  between operations  0.8 us (1%)
    ppermute x3, waiting for transfers between devices, down(): lax.ppermute(x, 'kcol', [(i + 2 * d, i) for i in range(col_count - 2 * d)])  13.6 us
    ppermute x3, starting transfers between devices, up(): lax.ppermute(x, 'kcol', [(i, i + 2 * d) for i in range(col_count - 2 * d)])  9.82 us
    pallas_call x4, Pallas kernels, band(): pl.pallas_call(functools.partial(band_kernel, causal, q_tile, count, chai...  6.45 us
    all_to_all x1, waiting for transfers between devices, per_device(): got = lax.all_to_all(chunks, 'qrow', 0, 0)  5.37 us
    all_to_all x1, waiting for transfers between devices, per_device(): pair = lax.all_to_all(pieces, 'qrow', 0, 0).reshape(rows, pair_feats)  5.02 us
    all_to_all x1, starting transfers between devices, per_device(): pair = lax.all_to_all(pieces, 'qrow', 0, 0).reshape(rows, pair_feats)  4.73 us
    all_to_all x1, starting transfers between devices, per_device(): got = lax.all_to_all(chunks, 'qrow', 0, 0)  4.39 us
    ppermute x3, starting transfers between devices, down(): lax.ppermute(x, 'kcol', [(i + 2 * d, i) for i in range(col_count - 2 * d)])  3.86 us
  transfers between devices with their start and end apart: 12, of which 5 were waited for; matrix products, arithmetic and copies ran while one was open for 1% of the time, Pallas kernels for 13%

profile of v3, /device:TPU:0, one launch (start us, length us, event | category | flops | bytes accessed | tf_op | source)
XLA Modules:
  0.0 62.7 jit_solution(6011770509063433197)
XLA Ops:
  0.6 2.4 %prep.1 = (bf16[4,128,128]{2,1,0:T(8,128)(2,1)}, bf16[512,640]{1,0:T(8,128)(2,1)}) custom-call(bf16[128,256]{1,0:T(8,128)(2,1)} %key.1, bf16[128,256]{1,0:T(8,128)(2,1)} %value.1, bf16[512,256]{1,0:T(8,128)(2,1)} %query.1, bf16[512,256]{1,0:T(8,128)(2,1)} %grad_out.1, bf16[512,256]{1,0:T(8,128)(2,1)} %output.1, f32[4,512]{1,0:T(4,128)} %lse.1), custom_call_target="tpu_custom_call" | custom-call | tf_op jit(solution)/shard_map/prep/pallas_call | solution.py:249
  3.0 0.5 collective-permute-start
  3.5 1.3 %collective-permute-start.1 = (bf16[512,640]{1,0:T(8,128)(2,1)}, bf16[512,640]{1,0:T(8,128)(2,1)S(1)}, u32[]{:S(2)}, u32[]{:S(2)}) collective-permute-start(bf16[512,640]{1,0:T(8,128)(2,1)} %get-tuple-element.27.refs_0_), channel_id=1, source_target_pairs={{4,0},{5,1},{6,2},{7,3},{12,8},{13,9},{14,10},{15,11},{20,16},{21,... | collective-permute-start | bytes 1966088 | tf_op jit(solution)/shard_map/ppermute | solution.py:247
  4.8 4.7 %all-to-all-start = ((bf16[4,128,128]{2,1,0:T(8,128)(2,1)}), bf16[4,128,128]{2,1,0:T(8,128)(2,1)S(1)}, u32[]{:S(2)}, u32[]{:S(2)}) async-start(bf16[4,128,128]{2,1,0:T(8,128)(2,1)} %get-tuple-element.32), calls=%async_computation | async-start | bytes 262144 | tf_op jit(solution)/shard_map/all_to_all | solution.py:260
  9.5 0.0 copy-start.1
  9.5 5.0 %all-to-all-done = bf16[4,128,128]{2,1,0:T(8,128)(2,1)S(1)} async-done(((bf16[4,128,128]{2,1,0:T(8,128)(2,1)}), bf16[4,128,128]{2,1,0:T(8,128)(2,1)S(1)}, u32[]{:S(2)}, u32[]{:S(2)}) %all-to-all-start) | async-done | bytes 131104 | tf_op jit(solution)/shard_map/all_to_all | solution.py:260
  14.5 3.5 %collective-permute-start.4 = (bf16[512,128]{1,0:T(8,128)(2,1)S(1)}, bf16[512,128]{1,0:T(8,128)(2,1)S(1)}, u32[]{:S(2)}, u32[]{:S(2)}) collective-permute-start(bf16[512,128]{1,0:T(8,128)(2,1)S(1)} %bitcast.6), channel_id=1, source_target_pairs={{0,2},{1,3},{2,4},{3,5},{4,6},{5,7},{8,10},{9,11},{10,12},{11,13},... | collective-permute-start | bytes 393224 | tf_op jit(solution)/shard_map/ppermute | solution.py:244
  18.0 0.1 pad_add_fusion.panel.refs_0_.refs_1_
  18.1 0.0 copy-done.1
  18.1 0.1 slice.10
  18.2 0.1 slice.9
  18.2 0.1 reshape.20.refs_3_
  18.3 0.1 reshape.19.refs_2_
  18.4 4.3 %collective-permute-start.3 = (bf16[512,128]{1,0:T(8,128)(2,1)S(1)}, bf16[512,128]{1,0:T(8,128)(2,1)S(1)}, u32[]{:S(2)}, u32[]{:S(2)}) collective-permute-start(bf16[512,128]{1,0:T(8,128)(2,1)S(1)} %bitcast.7), channel_id=1, source_target_pairs={{0,6},{1,7},{8,14},{9,15},{16,22},{17,23},{24,30},{25,31}} | collective-permute-start | bytes 393224 | tf_op jit(solution)/shard_map/ppermute | solution.py:244
  22.7 0.1 collective-permute-start.2
  22.8 0.0 collective-permute-done.refs_1_
  22.8 0.0 copy-start
  22.8 1.1 %copy-done = bf16[512,640]{1,0:T(8,128)(2,1)S(1)} copy-done((bf16[512,640]{1,0:T(8,128)(2,1)S(1)}, bf16[512,640]{1,0:T(8,128)(2,1)}, u32[]{:S(2)}) %copy-start) | copy-done | bytes 655384
  23.9 1.4 %expand2.1 = (bf16[4,1024,128]{2,1,0:T(8,128)(2,1)S(1)}, bf16[4,1024,128]{2,1,0:T(8,128)(2,1)S(1)}, bf16[256,1024]{1,0:T(8,128)(2,1)S(1)}, bf16[256,1024]{1,0:T(8,128)(2,1)S(1)}) custom-call(s32[2]{0:T(128)S(1)} %pad_add_fusion.panel.refs_0_.refs_1_, bf16[512,640]{1,0:T(8,128)(2,1)S(1)} %copy-done, bf16[512,640]{1,0:T(8,128)(2,1)S(1)} %collective-permute-done.refs_1_, ...), custom_call_target="tpu_custom_call" | custom-call | tf_op jit(solution)/shard_map/expand2/pallas_call | solution.py:276
  25.3 4.2 %own.1 = (f32[1024,256]{1,0:T(8,128)S(1)}, f32[128,512]{1,0:T(8,128)S(1)}) custom-call(s32[2]{0:T(128)S(1)} %pad_add_fusion.panel.refs_0_.refs_1_, s32[1]{0:T(128)} %bitcast.refs_1_, s32[16]{0:T(128)S(1)} %reshape.19.refs_2_, s32[16]{0:T(128)S(1)} %reshape.20.refs_3_, bf16[4,1024,128]{2,1,0:T(8,128)(2,1)S(1)} %get-tuple-element.28.refs_4_, ...), custom_call_target="tpu_custom_call" | custom-call | flops 1342177280 | bytes 6291456 | tf_op jit(solution)/shard_map/own/pallas_call | solution.py:294
  29.4 0.0 collective-permute-done.4.refs_9_
  29.5 0.6 band1.1
  30.1 7.9 %collective-permute-done.1.refs_0_ = bf16[512,640]{1,0:T(8,128)(2,1)S(1)} collective-permute-done((bf16[512,640]{1,0:T(8,128)(2,1)}, bf16[512,640]{1,0:T(8,128)(2,1)S(1)}, u32[]{:S(2)}, u32[]{:S(2)}) %collective-permute-start.1) | collective-permute-done | bytes 655392 | tf_op jit(solution)/shard_map/ppermute | solution.py:247
  38.0 0.5 expand1.1
  38.5 0.0 collective-permute-done.3.refs_9_
  38.5 0.6 band3.1
  39.1 0.0 collective-permute-done.2.refs_10_
  39.1 1.1 %far.1 = (bf16[512,256]{1,0:T(8,128)(2,1)S(1)}, f32[128,512]{1,0:T(8,128)S(1)}, bf16[128,512]{1,0:T(8,128)(2,1)S(1)}) custom-call(s32[1]{0:T(128)} %bitcast.3.refs_0_, s32[2]{0:T(128)S(1)} %pad_add_fusion.panel.refs_0_.refs_1_, s32[16]{0:T(128)S(1)} %reshape.19.refs_2_, s32[16]{0:T(128)S(1)} %reshape.20.refs_3_, ...), custom_call_target="tpu_custom_call" | custom-call | flops 1342177280 | bytes 6291456 | tf_op jit(solution)/shard_map/far/pallas_call | solution.py:294
  40.2 0.1 collective-permute-start.8
  40.3 1.3 %collective-permute-start.5 = (bf16[128,512]{1,0:T(8,128)(2,1)S(1)}, bf16[128,512]{1,0:T(8,128)(2,1)S(1)}, u32[]{:S(2)}, u32[]{:S(2)}) collective-permute-start(bf16[128,512]{1,0:T(8,128)(2,1)S(1)} %get-tuple-element.46), channel_id=1, source_target_pairs={{2,0},{3,1},{4,2},{5,3},{6,4},{7,5},{10,8},{11,9},{12,10},{13,11},... | collective-permute-start | bytes 393224 | tf_op jit(solution)/shard_map/ppermute | solution.py:247
  41.6 1.3 %collective-permute-start.6 = (bf16[128,512]{1,0:T(8,128)(2,1)S(1)}, bf16[128,512]{1,0:T(8,128)(2,1)S(1)}, u32[]{:S(2)}, u32[]{:S(2)}) collective-permute-start(bf16[128,512]{1,0:T(8,128)(2,1)S(1)} %get-tuple-element.47), channel_id=1, source_target_pairs={{6,0},{7,1},{14,8},{15,9},{22,16},{23,17},{30,24},{31,25}} | collective-permute-start | bytes 393224 | tf_op jit(solution)/shard_map/ppermute | solution.py:247
  42.9 0.6 collective-permute-start.7
  43.5 2.0 %collective-permute-start.9 = (bf16[512,256]{1,0:T(8,128)(2,1)S(1)}, bf16[512,256]{1,0:T(8,128)(2,1)S(1)}, u32[]{:S(2)}, u32[]{:S(2)}) collective-permute-start(bf16[512,256]{1,0:T(8,128)(2,1)S(1)} %get-tuple-element.50), channel_id=1, source_target_pairs={{0,4},{1,5},{2,6},{3,7},{8,12},{9,13},{10,14},{11,15},{16,20},{17,... | collective-permute-start | bytes 786440 | tf_op jit(solution)/shard_map/ppermute | solution.py:244
  45.5 2.6 %collective-permute-done.5.refs_2_ = bf16[128,512]{1,0:T(8,128)(2,1)S(1)} collective-permute-done((bf16[128,512]{1,0:T(8,128)(2,1)S(1)}, bf16[128,512]{1,0:T(8,128)(2,1)S(1)}, u32[]{:S(2)}, u32[]{:S(2)}) %collective-permute-start.5) | collective-permute-done | bytes 131104 | tf_op jit(solution)/shard_map/ppermute | solution.py:247
  48.1 3.1 %collective-permute-done.6.refs_3_ = bf16[128,512]{1,0:T(8,128)(2,1)S(1)} collective-permute-done((bf16[128,512]{1,0:T(8,128)(2,1)S(1)}, bf16[128,512]{1,0:T(8,128)(2,1)S(1)}, u32[]{:S(2)}, u32[]{:S(2)}) %collective-permute-start.6) | collective-permute-done | bytes 131104 | tf_op jit(solution)/shard_map/ppermute | solution.py:247
  51.2 0.0 collective-permute-done.7.refs_4_
  51.2 0.8 %collect.1 = f32[4,128,128]{2,1,0:T(8,128)} custom-call(f32[128,512]{1,0:T(8,128)S(1)} %get-tuple-element.33.refs_0_, f32[128,512]{1,0:T(8,128)S(1)} %get-tuple-element.38.refs_1_, bf16[128,512]{1,0:T(8,128)(2,1)S(1)} %collective-permute-done.5.refs_2_, bf16[128,512]{1,0:T(8,128)(2,1)S(1)} %collective-permute-done.6.refs_3_, ...), custom_call_target="tpu_custom_call" | custom-call | tf_op jit(solution)/shard_map/collect/pallas_call | solution.py:332
  52.0 4.4 %all-to-all-start.1 = ((f32[4,128,128]{2,1,0:T(8,128)}), f32[4,128,128]{2,1,0:T(8,128)S(1)}, u32[]{:S(2)}, u32[]{:S(2)}) async-start(f32[4,128,128]{2,1,0:T(8,128)} %collect.1), calls=%async_computation.1 | async-start | bytes 524288 | tf_op jit(solution)/shard_map/all_to_all | solution.py:340
  56.4 0.0 collective-permute-done.9.refs_1_
  56.4 5.4 %all-to-all-done.1.got = f32[4,128,128]{2,1,0:T(8,128)S(1)} async-done(((f32[4,128,128]{2,1,0:T(8,128)}), f32[4,128,128]{2,1,0:T(8,128)S(1)}, u32[]{:S(2)}, u32[]{:S(2)}) %all-to-all-start.1) | async-done | bytes 262176 | tf_op jit(solution)/shard_map/all_to_all | solution.py:340
  61.7 0.0 collective-permute-done.8.refs_0_
  61.7 1.0 %finish.1 = (f32[512,256]{1,0:T(8,128)}, f32[128,256]{1,0:T(8,128)}, f32[128,256]{1,0:T(8,128)}) custom-call(f32[4,128,128]{2,1,0:T(8,128)S(1)} %all-to-all-done.1.got, f32[1024,256]{1,0:T(8,128)S(1)} %get-tuple-element.49.dq, f32[512,256]{1,0:T(8,128)S(1)} %collective-permute-done.8.refs_0_, bf16[512,256]{1,0:T(8,128)(2,1)S(1)} %collective-permute-done.9.refs_1_), custom_call_target="tpu_custom_call" | custom-call | tf_op jit(solution)/shard_map/finish/pallas_call | solution.py:341
  (2 shorter events, 0.0 us)
Async XLA Ops:
  3.0 19.8 %collective-permute-start = (bf16[512,640]{1,0:T(8,128)(2,1)}, bf16[512,640]{1,0:T(8,128)(2,1)S(1)}, u32[]{:S(2)}, u32[]{:S(2)}) collective-permute-start(bf16[512,640]{1,0:T(8,128)(2,1)} %get-tuple-element.27.refs_0_), channel_id=1, source_target_pairs={{0,1},{1,0},{2,3},{3,2},{4,5},{5,4},{6,7},{7,6},{8,9},{9,8},{10,11... | collective-permute-start | bytes 1966088 | tf_op jit(solution)/shard_map/ppermute | solution.py:241
  3.5 34.5 %collective-permute-start.1 = (bf16[512,640]{1,0:T(8,128)(2,1)}, bf16[512,640]{1,0:T(8,128)(2,1)S(1)}, u32[]{:S(2)}, u32[]{:S(2)}) collective-permute-start(bf16[512,640]{1,0:T(8,128)(2,1)} %get-tuple-element.27.refs_0_), channel_id=1, source_target_pairs={{4,0},{5,1},{6,2},{7,3},{12,8},{13,9},{14,10},{15,11},{20,16},{21,... | collective-permute-start | bytes 1966088 | tf_op jit(solution)/shard_map/ppermute | solution.py:247
  4.8 9.7 %all-to-all-start = ((bf16[4,128,128]{2,1,0:T(8,128)(2,1)}), bf16[4,128,128]{2,1,0:T(8,128)(2,1)S(1)}, u32[]{:S(2)}, u32[]{:S(2)}) async-start(bf16[4,128,128]{2,1,0:T(8,128)(2,1)} %get-tuple-element.32), calls=%async_computation | async-start | bytes 262144 | tf_op jit(solution)/shard_map/all_to_all | solution.py:260
  9.5 8.6 %copy-start.1 = (s32[4096]{0:T(1024)S(1)}, s32[4096]{0:T(1024)}, u32[]{:S(2)}) copy-start(s32[4096]{0:T(1024)} %param.13) | copy-start | bytes 49156
  14.5 14.9 %collective-permute-start.4 = (bf16[512,128]{1,0:T(8,128)(2,1)S(1)}, bf16[512,128]{1,0:T(8,128)(2,1)S(1)}, u32[]{:S(2)}, u32[]{:S(2)}) collective-permute-start(bf16[512,128]{1,0:T(8,128)(2,1)S(1)} %bitcast.6), channel_id=1, source_target_pairs={{0,2},{1,3},{2,4},{3,5},{4,6},{5,7},{8,10},{9,11},{10,12},{11,13},... | collective-permute-start | bytes 393224 | tf_op jit(solution)/shard_map/ppermute | solution.py:244
  18.4 20.1 %collective-permute-start.3 = (bf16[512,128]{1,0:T(8,128)(2,1)S(1)}, bf16[512,128]{1,0:T(8,128)(2,1)S(1)}, u32[]{:S(2)}, u32[]{:S(2)}) collective-permute-start(bf16[512,128]{1,0:T(8,128)(2,1)S(1)} %bitcast.7), channel_id=1, source_target_pairs={{0,6},{1,7},{8,14},{9,15},{16,22},{17,23},{24,30},{25,31}} | collective-permute-start | bytes 393224 | tf_op jit(solution)/shard_map/ppermute | solution.py:244
  22.7 16.4 %collective-permute-start.2 = (bf16[512,128]{1,0:T(8,128)(2,1)S(1)}, bf16[512,128]{1,0:T(8,128)(2,1)S(1)}, u32[]{:S(2)}, u32[]{:S(2)}) collective-permute-start(bf16[512,128]{1,0:T(8,128)(2,1)S(1)} %bitcast.8), channel_id=1, source_target_pairs={{0,1},{1,0},{2,3},{3,2},{4,5},{5,4},{6,7},{7,6},{8,9},{9,8},{10,11... | collective-permute-start | bytes 393224 | tf_op jit(solution)/shard_map/ppermute | solution.py:241
  22.8 1.1 %copy-start = (bf16[512,640]{1,0:T(8,128)(2,1)S(1)}, bf16[512,640]{1,0:T(8,128)(2,1)}, u32[]{:S(2)}) copy-start(bf16[512,640]{1,0:T(8,128)(2,1)} %get-tuple-element.27.refs_0_) | copy-start | bytes 1966084
  40.2 21.5 %collective-permute-start.8 = (f32[512,256]{1,0:T(8,128)S(1)}, f32[512,256]{1,0:T(8,128)S(1)}, u32[]{:S(2)}, u32[]{:S(2)}) collective-permute-start(f32[512,256]{1,0:T(8,128)S(1)} %slice.11), channel_id=1, source_target_pairs={{0,1},{1,0},{2,3},{3,2},{4,5},{5,4},{6,7},{7,6},{8,9},{9,8},{10,11... | collective-permute-start | bytes 1572872 | tf_op jit(solution)/shard_map/ppermute | solution.py:241
  40.3 7.8 %collective-permute-start.5 = (bf16[128,512]{1,0:T(8,128)(2,1)S(1)}, bf16[128,512]{1,0:T(8,128)(2,1)S(1)}, u32[]{:S(2)}, u32[]{:S(2)}) collective-permute-start(bf16[128,512]{1,0:T(8,128)(2,1)S(1)} %get-tuple-element.46), channel_id=1, source_target_pairs={{2,0},{3,1},{4,2},{5,3},{6,4},{7,5},{10,8},{11,9},{12,10},{13,11},... | collective-permute-start | bytes 393224 | tf_op jit(solution)/shard_map/ppermute | solution.py:247
  41.6 9.6 %collective-permute-start.6 = (bf16[128,512]{1,0:T(8,128)(2,1)S(1)}, bf16[128,512]{1,0:T(8,128)(2,1)S(1)}, u32[]{:S(2)}, u32[]{:S(2)}) collective-permute-start(bf16[128,512]{1,0:T(8,128)(2,1)S(1)} %get-tuple-element.47), channel_id=1, source_target_pairs={{6,0},{7,1},{14,8},{15,9},{22,16},{23,17},{30,24},{31,25}} | collective-permute-start | bytes 393224 | tf_op jit(solution)/shard_map/ppermute | solution.py:247
  42.9 8.3 %collective-permute-start.7 = (bf16[128,512]{1,0:T(8,128)(2,1)S(1)}, bf16[128,512]{1,0:T(8,128)(2,1)S(1)}, u32[]{:S(2)}, u32[]{:S(2)}) collective-permute-start(bf16[128,512]{1,0:T(8,128)(2,1)S(1)} %get-tuple-element.48), channel_id=1, source_target_pairs={{0,1},{1,0},{2,3},{3,2},{4,5},{5,4},{6,7},{7,6},{8,9},{9,8},{10,11... | collective-permute-start | bytes 393224 | tf_op jit(solution)/shard_map/ppermute | solution.py:241
  43.5 12.9 %collective-permute-start.9 = (bf16[512,256]{1,0:T(8,128)(2,1)S(1)}, bf16[512,256]{1,0:T(8,128)(2,1)S(1)}, u32[]{:S(2)}, u32[]{:S(2)}) collective-permute-start(bf16[512,256]{1,0:T(8,128)(2,1)S(1)} %get-tuple-element.50), channel_id=1, source_target_pairs={{0,4},{1,5},{2,6},{3,7},{8,12},{9,13},{10,14},{11,15},{16,20},{17,... | collective-permute-start | bytes 786440 | tf_op jit(solution)/shard_map/ppermute | solution.py:244
  52.0 9.8 %all-to-all-start.1 = ((f32[4,128,128]{2,1,0:T(8,128)}), f32[4,128,128]{2,1,0:T(8,128)S(1)}, u32[]{:S(2)}, u32[]{:S(2)}) async-start(f32[4,128,128]{2,1,0:T(8,128)} %collect.1), calls=%async_computation.1 | async-start | bytes 524288 | tf_op jit(solution)/shard_map/all_to_all | solution.py:340

commit v4 on v3

--- a/solution.py
+++ b/solution.py
@@ -12,8 +12,6 @@
 FAR = 512.0
 SUB = 256
 EXTRA = 8
-FAR_STEP = 2
-PREP_MIB = 56
 LOG2E = 1.4426950408889634
 SCORE_SCALE = 0.125
 
@@ -78,7 +76,8 @@
 
 def expand_kernel(sides, panel, *refs):
     packs, docs = refs[:sides], refs[sides]
-    q_ext, g_ext, q_t, g_t = refs[sides + 1 :]
+    q_ext, g_ext, q_t, g_t, docs_out = refs[sides + 1 :]
+    docs_out[...] = docs[...]
     feats = q_t.shape[0]
     heads = feats // HEAD_DIM
     rows = docs.shape[1]
@@ -110,25 +109,29 @@
             g_ext[2 * p + 1, dst, :] = jnp.where(low_half, g_more, g_pair).astype(bf16)
 
 
-def band_kernel(causal, q_tile, key_panels, chained, *refs):
-    q_panel, k_panel, first, last, q_ext, g_ext, q_t, g_t, docs = refs[:9]
-    pairs = refs[9 : 9 + key_panels]
-    refs = refs[9 + key_panels + (1 if chained else 0) :]
-    dq_out, grads = refs[0], refs[1 : 1 + key_panels]
-    acc, k_ext, v_ext, k_lone, *more = refs[1 + key_panels :]
-    dq = more[0] if more else dq_out
+def band_kernel(causal, q_tile, chained, returns, q_base, *refs):
+    q_panel, k_panel, first, last, q_ext, g_ext, q_t, g_t, docs, pair = refs[:10]
+    refs = refs[10 + (1 if chained else 0) :]
+    parts, refs = refs[:returns], refs[returns:]
+    dq, out, acc, k_ext, v_ext, k_lone = refs
     heads, q_rows, _ = q_ext.shape
-    rows = pairs[0].shape[0]
+    rows = pair.shape[0]
     subs = rows // SUB
     q_subs = q_tile // SUB
     per_panel = rows // q_tile
-    q_tiles = q_rows // q_tile
+    q_tiles = q_panel.shape[0] * per_panel
     if not chained:
         dq[...] = jnp.zeros_like(dq)
-    acc[...] = jnp.zeros_like(acc)
+    if returns:
+        total = parts[0][...].astype(f32)
+        for part in parts[1:]:
+            total = total + part[...].astype(f32)
+        acc[...] = total
+    else:
+        acc[...] = jnp.zeros_like(acc)
 
     def one(qt, kt, masked):
-        at_q = pl.ds(pl.multiple_of(qt * q_tile, q_tile), q_tile)
+        at_q = pl.ds(pl.multiple_of(q_base * rows + qt * q_tile, q_tile), q_tile)
         at_k = pl.ds(pl.multiple_of(kt * SUB, SUB), SUB)
         weights, score_grads = [], []
         if masked:
@@ -154,60 +157,56 @@
         acc[:HEAD_DIM, at_k] += key_sum
         acc[HEAD_DIM:, at_k] += value_sum
 
-    @pl.when((k_panel[0] >= 0) & (q_panel[0] >= 0))
+    key_side = k_panel[0]
+    some = first[q_panel[0] * subs] <= last[jnp.maximum(key_side, 0) * subs + subs - 1]
+    for j in range(1, q_panel.shape[0]):
+        some = some | (first[q_panel[j] * subs] <= last[jnp.maximum(key_side, 0) * subs + subs - 1])
+    some = some & (key_side >= 0)
+    if causal:
+        reach = key_side <= q_panel[0]
+        for j in range(1, q_panel.shape[0]):
+            reach = reach | (key_side <= q_panel[j])
+        some = some & reach
+
+    @pl.when(some)
     def _():
         lane = lax.broadcasted_iota(jnp.int32, (rows, 128), 1)
         low_half = lane < HEAD_DIM
         ones = jnp.where(lane % HEAD_DIM < 3, 1.0, 0.0)
-        for j, pair in enumerate(pairs):
-            dst = slice(j * rows, (j + 1) * rows)
-            doc_row = docs[pl.ds(k_panel[j], 1), :].astype(f32)
-            half = [
-                jnp.ones((3, rows), f32),
-                one_hot_rows(doc_row, 1.0),
-                jnp.zeros((HEAD_DIM - 3 - DOCS, rows), f32),
-            ]
-            extra = jnp.concatenate(half + half, axis=0).T
-            straight = pair[...].astype(f32)
-            turned = halves_swapped(pair[...]).astype(f32)
-            k_ext[0, dst, :] = jnp.where(low_half, straight, extra).astype(bf16)
-            k_ext[1, dst, :] = jnp.where(low_half, extra, turned).astype(bf16)
-            v_ext[0, dst, :] = jnp.where(low_half, turned, ones).astype(bf16)
-            v_ext[1, dst, :] = jnp.where(low_half, ones, straight).astype(bf16)
-            k_lone[0, dst, :] = jnp.where(low_half, straight * SCORE_SCALE, 0.0).astype(bf16)
-            k_lone[1, dst, :] = jnp.where(low_half, 0.0, turned * SCORE_SCALE).astype(bf16)
+        doc_row = docs[pl.ds(key_side, 1), :].astype(f32)
+        half = [jnp.ones((3, rows), f32), one_hot_rows(doc_row, 1.0), jnp.zeros((HEAD_DIM - 3 - DOCS, rows), f32)]
+        extra = jnp.concatenate(half + half, axis=0).T
+        straight = pair[...].astype(f32)
+        turned = halves_swapped(pair[...]).astype(f32)
+        k_ext[0] = jnp.where(low_half, straight, extra).astype(bf16)
+        k_ext[1] = jnp.where(low_half, extra, turned).astype(bf16)
+        v_ext[0] = jnp.where(low_half, turned, ones).astype(bf16)
+        v_ext[1] = jnp.where(low_half, ones, straight).astype(bf16)
+        k_lone[0] = jnp.where(low_half, straight * SCORE_SCALE, 0.0).astype(bf16)
+        k_lone[1] = jnp.where(low_half, 0.0, turned * SCORE_SCALE).astype(bf16)
 
         def step(index, carry):
-            qt, kt = index // (subs * key_panels), index % (subs * key_panels)
-            q_side, k_side = q_panel[qt // per_panel], k_panel[kt // subs]
-            q_sub, k_sub = (qt % per_panel) * q_subs, kt % subs
-            live = first[q_side * subs + q_sub] <= last[k_side * subs + k_sub]
+            qt, kt = index // subs, index % subs
+            q_at = q_panel[qt // per_panel] * subs + (qt % per_panel) * q_subs
+            k_at = key_side * subs + kt
+            live = first[q_at] <= last[k_at]
             if not causal:
                 pl.when(live)(functools.partial(one, qt, kt, False))
             else:
-                q_at, k_at = q_side * subs + q_sub, k_side * subs + k_sub
                 live = live & (k_at < q_at + q_subs)
                 below = k_at < q_at
                 pl.when(live & below)(functools.partial(one, qt, kt, False))
                 pl.when(live & jnp.logical_not(below))(functools.partial(one, qt, kt, True))
             return carry
 
-        lax.fori_loop(0, q_tiles * subs * key_panels, step, 0)
-
-    for j in range(key_panels):
-        grads[j][...] = acc[:, j * rows : (j + 1) * rows].astype(grads[j].dtype)
-    if more:
-        dq_out[...] = dq[...].astype(dq_out.dtype)
-
-
-def collect_kernel(*refs):
-    parts, out = refs[:-1], refs[-1]
-    total = parts[0][...]
-    for part in parts[1:]:
-        total = total + part[...].astype(f32)
-    chunk = out.shape[2]
-    for i in range(out.shape[0]):
-        out[i] = total[:, i * chunk : (i + 1) * chunk]
+        lax.fori_loop(0, q_tiles * subs, step, 0)
+
+    if len(out.shape) == 3:
+        chunk = out.shape[2]
+        for i in range(out.shape[0]):
+            out[i] = acc[:, i * chunk : (i + 1) * chunk]
+    else:
+        out[...] = acc[...].astype(out.dtype)
 
 
 def finish_kernel(ways, count, got, dq, *refs):
@@ -254,89 +253,67 @@
             jax.ShapeDtypeStruct((row_count, key_rows, pair_feats), bf16),
             jax.ShapeDtypeStruct((rows, 2 * feats + 128), bf16),
         ],
-        compiler_params=small(PREP_MIB),
+        compiler_params=small(56),
         name="prep",
     )(key, value, query, grad_out, output, lse)
+    packed_other = swap(packed)
     pair = lax.all_to_all(pieces, "qrow", 0, 0).reshape(rows, pair_feats)
-    packed_other = swap(packed)
-    packed_far = down(packed, FAR_STEP)
 
     docs = doc_ids.reshape(col_count, rows)
     first, last = docs[:, ::SUB].reshape(-1), docs[:, SUB - 1 :: SUB].reshape(-1)
-
-    def panels(*items):
-        inside = [jnp.where((p >= 0) & (p < col_count), p, -1) for p in items]
-        return jnp.stack(inside).astype(jnp.int32)
-
-    mine = panels(col, col ^ 1)
-    far = panels(col + 2 * FAR_STEP)
-
-    def expand(panel, *packs):
-        span = len(packs) * rows
-        return pl.pallas_call(
-            functools.partial(expand_kernel, len(packs)),
-            in_specs=[SMEM_SPEC] + [VMEM_SPEC] * (len(packs) + 1),
-            out_specs=[VMEM_SPEC] * 4,
-            out_shape=[jax.ShapeDtypeStruct((heads, span, 128), bf16)] * 2
-            + [jax.ShapeDtypeStruct((feats, span), bf16)] * 2,
-            compiler_params=small(16),
-            name=f"expand{len(packs)}",
-        )(panel, *packs, docs)
-
-    def band(name, q_panel, k_panel, queries, pairs, dq, q_tile, causal, out_types, dq_type=f32):
+    mine = jnp.stack([col, col ^ 1]).astype(jnp.int32)
+
+    q_ext, g_ext, q_t, g_t, docs = pl.pallas_call(
+        functools.partial(expand_kernel, 2),
+        in_specs=[SMEM_SPEC] + [VMEM_SPEC] * 3,
+        out_specs=[VMEM_SPEC] * 5,
+        out_shape=[jax.ShapeDtypeStruct((heads, 2 * rows, 128), bf16)] * 2
+        + [jax.ShapeDtypeStruct((feats, 2 * rows), bf16)] * 2
+        + [jax.ShapeDtypeStruct(docs.shape, jnp.int32)],
+        compiler_params=small(16),
+        name="expand",
+    )(mine, packed, packed_other, docs)
+    pair, docs = lax.optimization_barrier((pair, docs))
+
+    def band(name, q_panel, k_panel, block, dq, parts, q_tile, causal, q_base, out):
         chained = dq is not None
         extra = [dq] if chained else []
-        count = len(pairs)
-        q_rows = queries[0].shape[1]
-        scratch = [pltpu.VMEM((pair_feats, count * rows), f32)] + [pltpu.VMEM((2, count * rows, 128), bf16)] * 3
-        if dq_type != f32:
-            scratch.append(pltpu.VMEM((q_rows, feats), f32))
         return pl.pallas_call(
-            functools.partial(band_kernel, causal, q_tile, count, chained),
-            in_specs=[SMEM_SPEC] * 4 + [VMEM_SPEC] * (5 + count + len(extra)),
-            out_specs=[VMEM_SPEC] * (1 + count),
-            out_shape=[jax.ShapeDtypeStruct((q_rows, feats), dq_type)]
-            + [jax.ShapeDtypeStruct((pair_feats, rows), t) for t in out_types],
-            scratch_shapes=scratch,
-            input_output_aliases={9 + count: 0} if chained else {},
+            functools.partial(band_kernel, causal, q_tile, chained, len(parts), q_base),
+            in_specs=[SMEM_SPEC] * 4 + [VMEM_SPEC] * (6 + len(extra) + len(parts)),
+            out_specs=[VMEM_SPEC] * 2,
+            out_shape=[jax.ShapeDtypeStruct((2 * rows, feats), f32), out],
+            scratch_shapes=[pltpu.VMEM((pair_feats, rows), f32)] + [pltpu.VMEM((2, rows, 128), bf16)] * 3,
+            input_output_aliases={10: 0} if chained else {},
             compiler_params=small(24),
             cost_estimate=pl.CostEstimate(
-                flops=10 * q_rows * count * rows * feats,
+                flops=20 * rows * rows * feats,
                 bytes_accessed=6 << 20,
-                transcendentals=q_rows * count * rows * heads,
+                transcendentals=2 * rows * rows * heads,
             ),
             name=name,
-        )(q_panel, k_panel, first, last, *queries, docs, *pairs, *extra)
+        )(q_panel, k_panel, first, last, q_ext, g_ext, q_t, g_t, docs, block, *extra, *parts)
 
     reach = min(chips - 1, chips // 2 + 1)
-    steps = [d for d in range(1, reach + 1) if d != FAR_STEP]
-    blocks = {d: up(pair, d) for d in steps}
-    pair_other = swap(pair)
-
-    queries = expand(mine, packed, packed_other)
-    dq, own_grads = band("own", mine, panels(col), queries, [pair], None, SUB, True, [f32])
-    grads = {}
-    for d in steps:
-        dq, grads[d] = band(
-            f"band{d}", mine, panels(col - 2 * d), queries, [blocks[d]], dq, 2 * SUB, False, [bf16]
-        )
-    far_queries = expand(jnp.maximum(far, 0), packed_far)
-    far_dq, far_own, far_other = band(
-        "far", far, mine, far_queries, [pair, pair_other], None, 2 * SUB, False, [f32, bf16], bf16
+    order = [*range(2, reach + 1), 1]
+    blocks = {d: up(pair, d) for d in order}
+    wire = jax.ShapeDtypeStruct((pair_feats, rows), bf16)
+    dq = None
+    back = []
+    for d in order:
+        panel = (col - 2 * d).astype(jnp.int32)[None]
+        dq, grads = band(f"band{d}", mine, panel, blocks[d], dq, [], 2 * SUB if d < reach else SUB, False, 0, wire)
+        back.append(down(grads, d))
+    dq, *early = lax.optimization_barrier((dq, *back[:-1]))
+    here = mine[:1]
+    dq, own = band(
+        "own1", mine[1:], here, pair, dq, [], 2 * SUB, True, 1, jax.ShapeDtypeStruct((pair_feats, rows), f32)
     )
-    dq, far_dq, far_other, *sent = lax.optimization_barrier((dq, far_dq, far_other, *[grads[d] for d in steps]))
-    returned = [down(x, d) for x, d in zip(sent, steps)]
-    returned.append(swap(far_other))
-    dq_parts = [swap(dq[rows:]), up(far_dq, FAR_STEP)]
-
-    chunks = pl.pallas_call(
-        collect_kernel,
-        in_specs=[VMEM_SPEC] * (2 + len(returned)),
-        out_specs=VMEM_SPEC,
-        out_shape=jax.ShapeDtypeStruct((row_count, pair_feats, key_rows), f32),
-        compiler_params=small(),
-        name="collect",
-    )(own_grads, far_own, *returned)
+    dq, chunks = band(
+        "own0", here, here, pair, dq, [own, *early, back[-1]], SUB, True, 0,
+        jax.ShapeDtypeStruct((row_count, pair_feats, key_rows), f32),
+    )
+    dq_parts = [swap(dq[rows:])]
     got = lax.all_to_all(chunks, "qrow", 0, 0)
     return pl.pallas_call(
         functools.partial(finish_kernel, row_count * HEAD_DIM // key_feats, len(dq_parts)),

time: 63.2 us -> 65.5 us (1.036)
  the two profiles are of different devices: /device:TPU:0 before, /device:TPU:16 now
where the time goes in v4:
time: 65.5 us; the launch traced here: 65 us
  Pallas kernels  19 us (29%)
  starting transfers between devices  17.5 us (27%)
  waiting for transfers between devices  13.4 us (20%)
  blocking collectives  9.4 us (14%)
  local copies, waits for them, and re-layouts  4.83 us (7%)
  between operations  0.79 us (1%)
    pallas_call x5, Pallas kernels, band(): pl.pallas_call(functools.partial(band_kernel, causal, q_tile, chained, le...  14.2 us
    all_to_all x1, blocking collectives, per_device(): got = lax.all_to_all(chunks, 'qrow', 0, 0)  9.4 us
    ppermute x3, waiting for transfers between devices, down(): lax.ppermute(x, 'kcol', [(i + 2 * d, i) for i in range(col_count - 2 * d)])  9.39 us
    ppermute x3, starting transfers between devices, up(): lax.ppermute(x, 'kcol', [(i, i + 2 * d) for i in range(col_count - 2 * d)])  6.05 us
    ppermute x3, starting transfers between devices, down(): lax.ppermute(x, 'kcol', [(i + 2 * d, i) for i in range(col_count - 2 * d)])  5.75 us
    unnamed x12, local copies, waits for them, and re-layouts  4.48 us
    all_to_all x1, starting transfers between devices, per_device(): pair = lax.all_to_all(pieces, 'qrow', 0, 0).reshape(rows, pair_feats)  3.86 us
    pallas_call x1, Pallas kernels, per_device(): pl.pallas_call(prep_kernel, in_specs=[VMEM_SPEC] * 6, out_specs=[VMEM_SPE...  2.4 us
  transfers between devices with their start and end apart: 9, of which 3 were waited for; matrix products, arithmetic and copies ran while one was open for 1% of the time, Pallas kernels for 19%

profile of v4, /device:TPU:16, one launch (start us, length us, event | category | flops | bytes accessed | tf_op | source)
XLA Modules:
  0.0 65.0 jit_solution(15204511002175903980)
XLA Ops:
  0.6 2.4 %prep.1 = (bf16[4,128,128]{2,1,0:T(8,128)(2,1)}, bf16[512,640]{1,0:T(8,128)(2,1)}) custom-call(bf16[128,256]{1,0:T(8,128)(2,1)} %key.1, bf16[128,256]{1,0:T(8,128)(2,1)} %value.1, bf16[512,256]{1,0:T(8,128)(2,1)} %query.1, bf16[512,256]{1,0:T(8,128)(2,1)} %grad_out.1, bf16[512,256]{1,0:T(8,128)(2,1)} %output.1, f32[4,512]{1,0:T(4,128)} %lse.1), custom_call_target="tpu_custom_call" | custom-call | tf_op jit(solution)/shard_map/prep/pallas_call | solution.py:248
  3.0 0.0 collective-permute-start
  3.0 0.0 copy-start.5
  3.0 3.9 %all-to-all-start = ((bf16[4,128,128]{2,1,0:T(8,128)(2,1)}), bf16[4,128,128]{2,1,0:T(8,128)(2,1)S(1)}, u32[]{:S(2)}, u32[]{:S(2)}) async-start(bf16[4,128,128]{2,1,0:T(8,128)(2,1)} %get-tuple-element.30), calls=%async_computation | async-start | bytes 262144 | tf_op jit(solution)/shard_map/all_to_all | solution.py:260
  6.9 0.0 copy-done.5
  6.9 0.1 pad_add_fusion.panel.refs_0_
  7.0 0.0 collective-permute-done.refs_1_
  7.0 0.0 copy-start
  7.0 1.1 %copy-done = bf16[512,640]{1,0:T(8,128)(2,1)S(1)} copy-done((bf16[512,640]{1,0:T(8,128)(2,1)S(1)}, bf16[512,640]{1,0:T(8,128)(2,1)}, u32[]{:S(2)}) %copy-start) | copy-done | bytes 655384
  8.1 1.4 %expand.1 = (bf16[4,1024,128]{2,1,0:T(8,128)(2,1)S(1)}, bf16[4,1024,128]{2,1,0:T(8,128)(2,1)S(1)}, bf16[256,1024]{1,0:T(8,128)(2,1)S(1)}, bf16[256,1024]{1,0:T(8,128)(2,1)S(1)}, s32[8,512]{1,0:T(8,128)S(1)}) custom-call(s32[2]{0:T(128)S(1)} %pad_add_fusion.panel.refs_0_, bf16[512,640]{1,0:T(8,128)(2,1)S(1)} %copy-done, ...), custom_call_target="tpu_custom_call" | custom-call | tf_op jit(solution)/shard_map/expand/pallas_call | solution.py:266
  9.5 0.0 copy-start.1
  9.5 0.8 %copy-done.1 = bf16[256,1024]{1,0:T(8,128)(2,1)} copy-done((bf16[256,1024]{1,0:T(8,128)(2,1)}, bf16[256,1024]{1,0:T(8,128)(2,1)S(1)}, u32[]{:S(2)}) %copy-start.1) | copy-done | bytes 524312
  10.3 1.6 %all-to-all-done = bf16[4,128,128]{2,1,0:T(8,128)(2,1)S(1)} async-done(((bf16[4,128,128]{2,1,0:T(8,128)(2,1)}), bf16[4,128,128]{2,1,0:T(8,128)(2,1)S(1)}, u32[]{:S(2)}, u32[]{:S(2)}) %all-to-all-start) | async-done | bytes 131104 | tf_op jit(solution)/shard_map/all_to_all | solution.py:260
  11.9 1.3 %collective-permute-start.3 = (bf16[512,128]{1,0:T(8,128)(2,1)S(1)}, bf16[512,128]{1,0:T(8,128)(2,1)S(1)}, u32[]{:S(2)}, u32[]{:S(2)}) collective-permute-start(bf16[512,128]{1,0:T(8,128)(2,1)S(1)} %bitcast.6), channel_id=1, source_target_pairs={{0,4},{1,5},{2,6},{3,7},{8,12},{9,13},{10,14},{11,15},{16,20},{17,... | collective-permute-start | bytes 393224 | tf_op jit(solution)/shard_map/ppermute | solution.py:243
  13.2 0.7 %collective-permute-start.2 = (bf16[512,128]{1,0:T(8,128)(2,1)S(1)}, bf16[512,128]{1,0:T(8,128)(2,1)S(1)}, u32[]{:S(2)}, u32[]{:S(2)}) collective-permute-start(bf16[512,128]{1,0:T(8,128)(2,1)S(1)} %bitcast.7), channel_id=1, source_target_pairs={{0,6},{1,7},{8,14},{9,15},{16,22},{17,23},{24,30},{25,31}} | collective-permute-start | bytes 393224 | tf_op jit(solution)/shard_map/ppermute | solution.py:243
  13.9 0.1 slice.10
  14.0 0.1 slice.9
  14.0 0.1 reshape.20.refs_3_
  14.1 0.1 reshape.19.refs_2_
  14.2 4.1 %collective-permute-start.1 = (bf16[512,128]{1,0:T(8,128)(2,1)S(1)}, bf16[512,128]{1,0:T(8,128)(2,1)S(1)}, u32[]{:S(2)}, u32[]{:S(2)}) collective-permute-start(bf16[512,128]{1,0:T(8,128)(2,1)S(1)} %bitcast.8), channel_id=1, source_target_pairs={{0,2},{1,3},{2,4},{3,5},{4,6},{5,7},{8,10},{9,11},{10,12},{11,13},... | collective-permute-start | bytes 393224 | tf_op jit(solution)/shard_map/ppermute | solution.py:243
  18.3 2.3 %collective-permute-done.3.refs_9_ = bf16[512,128]{1,0:T(8,128)(2,1)S(1)} collective-permute-done((bf16[512,128]{1,0:T(8,128)(2,1)S(1)}, bf16[512,128]{1,0:T(8,128)(2,1)S(1)}, u32[]{:S(2)}, u32[]{:S(2)}) %collective-permute-start.3) | collective-permute-done | bytes 131104 | tf_op jit(solution)/shard_map/ppermute | solution.py:243
  20.6 0.0 copy-start.3
  20.6 0.7 %copy-done.3 = bf16[512,128]{1,0:T(8,128)(2,1)} copy-done((bf16[512,128]{1,0:T(8,128)(2,1)}, bf16[512,128]{1,0:T(8,128)(2,1)S(1)}, u32[]{:S(2)}) %copy-start.3) | copy-done | bytes 131096
  21.3 0.0 copy-start.2
  21.3 1.0 %copy-done.2 = bf16[256,1024]{1,0:T(8,128)(2,1)S(1)} copy-done((bf16[256,1024]{1,0:T(8,128)(2,1)S(1)}, bf16[256,1024]{1,0:T(8,128)(2,1)}, u32[]{:S(2)}) %copy-start.2) | copy-done | bytes 524312
  22.3 0.0 copy-start.4
  22.3 0.9 %copy-done.4 = bf16[512,128]{1,0:T(8,128)(2,1)S(1)} copy-done((bf16[512,128]{1,0:T(8,128)(2,1)S(1)}, bf16[512,128]{1,0:T(8,128)(2,1)}, u32[]{:S(2)}) %copy-start.4) | copy-done | bytes 131096
  23.2 0.6 band2.1
  23.9 0.0 collective-permute-done.2.refs_9_
  23.9 0.6 band3.1
  24.5 0.7 %collective-permute-start.5 = (bf16[128,512]{1,0:T(8,128)(2,1)S(1)}, bf16[128,512]{1,0:T(8,128)(2,1)S(1)}, u32[]{:S(2)}, u32[]{:S(2)}) collective-permute-start(bf16[128,512]{1,0:T(8,128)(2,1)S(1)} %get-tuple-element.38), channel_id=1, source_target_pairs={{6,0},{7,1},{14,8},{15,9},{22,16},{23,17},{30,24},{31,25}} | collective-permute-start | bytes 393224 | tf_op jit(solution)/shard_map/ppermute | solution.py:246
  25.2 3.2 %collective-permute-start.4 = (bf16[128,512]{1,0:T(8,128)(2,1)S(1)}, bf16[128,512]{1,0:T(8,128)(2,1)S(1)}, u32[]{:S(2)}, u32[]{:S(2)}) collective-permute-start(bf16[128,512]{1,0:T(8,128)(2,1)S(1)} %get-tuple-element.37), channel_id=1, source_target_pairs={{4,0},{5,1},{6,2},{7,3},{12,8},{13,9},{14,10},{15,11},{20,16},{21,... | collective-permute-start | bytes 393224 | tf_op jit(solution)/shard_map/ppermute | solution.py:246
  28.3 0.0 collective-permute-done.1.refs_9_
  28.3 6.3 %band1.1 = (f32[1024,256]{1,0:T(8,128)S(1)}, bf16[128,512]{1,0:T(8,128)(2,1)S(1)}) custom-call(s32[2]{0:T(128)S(1)} %pad_add_fusion.panel.refs_0_, s32[1]{0:T(128)} %bitcast.3.refs_1_, s32[16]{0:T(128)S(1)} %reshape.19.refs_2_, s32[16]{0:T(128)S(1)} %reshape.20.refs_3_, ...), custom_call_target="tpu_custom_call", output_to_operand_aliasing={{0}: (10, {})} | custom-call | flops 1342177280 | bytes 6291456 | tf_op jit(solution)/shard_map/band1/pallas_call | solution.py:281
  34.6 1.9 %collective-permute-start.6 = (bf16[128,512]{1,0:T(8,128)(2,1)S(1)}, bf16[128,512]{1,0:T(8,128)(2,1)S(1)}, u32[]{:S(2)}, u32[]{:S(2)}) collective-permute-start(bf16[128,512]{1,0:T(8,128)(2,1)S(1)} %get-tuple-element.44), channel_id=1, source_target_pairs={{2,0},{3,1},{4,2},{5,3},{6,4},{7,5},{10,8},{11,9},{12,10},{13,11},... | collective-permute-start | bytes 393224 | tf_op jit(solution)/shard_map/ppermute | solution.py:246
  36.5 0.0 collective-permute-done.5.refs_13_
  36.6 0.0 collective-permute-done.4.refs_12_
  36.6 3.5 %own1.1 = (f32[1024,256]{1,0:T(8,128)S(1)}, f32[128,512]{1,0:T(8,128)S(1)}) custom-call(s32[1]{0:T(128)} %bitcast.1.refs_0_, s32[1]{0:T(128)} %bitcast.refs_1_.refs_0_, s32[16]{0:T(128)S(1)} %reshape.19.refs_2_, s32[16]{0:T(128)S(1)} %reshape.20.refs_3_, bf16[4,1024,128]{2,1,0:T(8,128)(2,1)S(1)} %get-tuple-element.26.refs_4_, ...), custom_call_target="tpu_custom_call", output_to_operand_aliasing={{0}: (10, {})} | custom-call | flops 1342177280 | bytes 6291456 | tf_op jit(solution)/shard_map/own1/pallas_call | solution.py:281
  40.1 9.4 %collective-permute-done.6.refs_14_ = bf16[128,512]{1,0:T(8,128)(2,1)S(1)} collective-permute-done((bf16[128,512]{1,0:T(8,128)(2,1)S(1)}, bf16[128,512]{1,0:T(8,128)(2,1)S(1)}, u32[]{:S(2)}, u32[]{:S(2)}) %collective-permute-start.6) | collective-permute-done | bytes 131104 | tf_op jit(solution)/shard_map/ppermute | solution.py:246
  49.5 3.2 %own0.1 = (f32[1024,256]{1,0:T(8,128)S(1)}, f32[4,128,128]{2,1,0:T(8,128)S(1)}) custom-call(s32[1]{0:T(128)} %bitcast.refs_1_.refs_0_, s32[1]{0:T(128)} %bitcast.refs_1_.refs_0_, s32[16]{0:T(128)S(1)} %reshape.19.refs_2_, s32[16]{0:T(128)S(1)} %reshape.20.refs_3_, ...), custom_call_target="tpu_custom_call", output_to_operand_aliasing={{0}: (10, {})} | custom-call | flops 1342177280 | bytes 6291456 | tf_op jit(solution)/shard_map/own0/pallas_call | solution.py:281
  52.7 1.8 %collective-permute-start.7 = (f32[512,256]{1,0:T(8,128)S(1)}, f32[512,256]{1,0:T(8,128)S(1)}, u32[]{:S(2)}, u32[]{:S(2)}) collective-permute-start(f32[512,256]{1,0:T(8,128)S(1)} %slice.11), channel_id=1, source_target_pairs={{0,1},{1,0},{2,3},{3,2},{4,5},{5,4},{6,7},{7,6},{8,9},{9,8},{10,11... | collective-permute-start | bytes 1572872 | tf_op jit(solution)/shard_map/ppermute | solution.py:240
  54.6 9.4 %all_to_all.10.got = f32[4,128,128]{2,1,0:T(8,128)S(1)} all-to-all(f32[4,128,128]{2,1,0:T(8,128)S(1)} %get-tuple-element.45), channel_id=1, replica_groups=mesh['qrow'=4,'kcol'=8] {'qrow'}, dimensions={0} | all-to-all | bytes 524288 | tf_op jit(solution)/shard_map/all_to_all | solution.py:317
  64.0 0.0 collective-permute-done.7.refs_0_
  64.0 1.0 %finish.1 = (f32[512,256]{1,0:T(8,128)}, f32[128,256]{1,0:T(8,128)}, f32[128,256]{1,0:T(8,128)}) custom-call(f32[4,128,128]{2,1,0:T(8,128)S(1)} %all_to_all.10.got, f32[1024,256]{1,0:T(8,128)S(1)} %get-tuple-element.46.dq, f32[512,256]{1,0:T(8,128)S(1)} %collective-permute-done.7.refs_0_), custom_call_target="tpu_custom_call" | custom-call | tf_op jit(solution)/shard_map/finish/pallas_call | solution.py:318
  (2 shorter events, 0.0 us)
Async XLA Ops:
  3.0 4.0 %collective-permute-start = (bf16[512,640]{1,0:T(8,128)(2,1)}, bf16[512,640]{1,0:T(8,128)(2,1)S(1)}, u32[]{:S(2)}, u32[]{:S(2)}) collective-permute-start(bf16[512,640]{1,0:T(8,128)(2,1)} %get-tuple-element.25.refs_0_), channel_id=1, source_target_pairs={{0,1},{1,0},{2,3},{3,2},{4,5},{5,4},{6,7},{7,6},{8,9},{9,8},{10,11... | collective-permute-start | bytes 1966088 | tf_op jit(solution)/shard_map/ppermute | solution.py:240
  3.0 3.9 %copy-start.5 = (s32[4096]{0:T(1024)S(1)}, s32[4096]{0:T(1024)}, u32[]{:S(2)}) copy-start(s32[4096]{0:T(1024)} %param.13) | copy-start | bytes 49156
  3.0 8.9 %all-to-all-start = ((bf16[4,128,128]{2,1,0:T(8,128)(2,1)}), bf16[4,128,128]{2,1,0:T(8,128)(2,1)S(1)}, u32[]{:S(2)}, u32[]{:S(2)}) async-start(bf16[4,128,128]{2,1,0:T(8,128)(2,1)} %get-tuple-element.30), calls=%async_computation | async-start | bytes 262144 | tf_op jit(solution)/shard_map/all_to_all | solution.py:260
  7.0 1.1 %copy-start = (bf16[512,640]{1,0:T(8,128)(2,1)S(1)}, bf16[512,640]{1,0:T(8,128)(2,1)}, u32[]{:S(2)}) copy-start(bf16[512,640]{1,0:T(8,128)(2,1)} %get-tuple-element.25.refs_0_) | copy-start | bytes 1966084
  9.5 0.8 %copy-start.1 = (bf16[256,1024]{1,0:T(8,128)(2,1)}, bf16[256,1024]{1,0:T(8,128)(2,1)S(1)}, u32[]{:S(2)}) copy-start(bf16[256,1024]{1,0:T(8,128)(2,1)S(1)} %get-tuple-element.29.refs_7_) | copy-start | bytes 1572868
  11.9 8.7 %collective-permute-start.3 = (bf16[512,128]{1,0:T(8,128)(2,1)S(1)}, bf16[512,128]{1,0:T(8,128)(2,1)S(1)}, u32[]{:S(2)}, u32[]{:S(2)}) collective-permute-start(bf16[512,128]{1,0:T(8,128)(2,1)S(1)} %bitcast.6), channel_id=1, source_target_pairs={{0,4},{1,5},{2,6},{3,7},{8,12},{9,13},{10,14},{11,15},{16,20},{17,... | collective-permute-start | bytes 393224 | tf_op jit(solution)/shard_map/ppermute | solution.py:243
  13.2 10.7 %collective-permute-start.2 = (bf16[512,128]{1,0:T(8,128)(2,1)S(1)}, bf16[512,128]{1,0:T(8,128)(2,1)S(1)}, u32[]{:S(2)}, u32[]{:S(2)}) collective-permute-start(bf16[512,128]{1,0:T(8,128)(2,1)S(1)} %bitcast.7), channel_id=1, source_target_pairs={{0,6},{1,7},{8,14},{9,15},{16,22},{17,23},{24,30},{25,31}} | collective-permute-start | bytes 393224 | tf_op jit(solution)/shard_map/ppermute | solution.py:243
  14.2 14.1 %collective-permute-start.1 = (bf16[512,128]{1,0:T(8,128)(2,1)S(1)}, bf16[512,128]{1,0:T(8,128)(2,1)S(1)}, u32[]{:S(2)}, u32[]{:S(2)}) collective-permute-start(bf16[512,128]{1,0:T(8,128)(2,1)S(1)} %bitcast.8), channel_id=1, source_target_pairs={{0,2},{1,3},{2,4},{3,5},{4,6},{5,7},{8,10},{9,11},{10,12},{11,13},... | collective-permute-start | bytes 393224 | tf_op jit(solution)/shard_map/ppermute | solution.py:243
  20.6 0.7 %copy-start.3 = (bf16[512,128]{1,0:T(8,128)(2,1)}, bf16[512,128]{1,0:T(8,128)(2,1)S(1)}, u32[]{:S(2)}) copy-start(bf16[512,128]{1,0:T(8,128)(2,1)S(1)} %collective-permute-done.3.refs_9_) | copy-start | bytes 393220
  21.3 1.0 %copy-start.2 = (bf16[256,1024]{1,0:T(8,128)(2,1)S(1)}, bf16[256,1024]{1,0:T(8,128)(2,1)}, u32[]{:S(2)}) copy-start(bf16[256,1024]{1,0:T(8,128)(2,1)} %copy-done.1) | copy-start | bytes 1572868
  22.3 0.9 %copy-start.4 = (bf16[512,128]{1,0:T(8,128)(2,1)S(1)}, bf16[512,128]{1,0:T(8,128)(2,1)}, u32[]{:S(2)}) copy-start(bf16[512,128]{1,0:T(8,128)(2,1)} %copy-done.3) | copy-start | bytes 393220
  24.5 12.1 %collective-permute-start.5 = (bf16[128,512]{1,0:T(8,128)(2,1)S(1)}, bf16[128,512]{1,0:T(8,128)(2,1)S(1)}, u32[]{:S(2)}, u32[]{:S(2)}) collective-permute-start(bf16[128,512]{1,0:T(8,128)(2,1)S(1)} %get-tuple-element.38), channel_id=1, source_target_pairs={{6,0},{7,1},{14,8},{15,9},{22,16},{23,17},{30,24},{31,25}} | collective-permute-start | bytes 393224 | tf_op jit(solution)/shard_map/ppermute | solution.py:246
  25.2 11.4 %collective-permute-start.4 = (bf16[128,512]{1,0:T(8,128)(2,1)S(1)}, bf16[128,512]{1,0:T(8,128)(2,1)S(1)}, u32[]{:S(2)}, u32[]{:S(2)}) collective-permute-start(bf16[128,512]{1,0:T(8,128)(2,1)S(1)} %get-tuple-element.37), channel_id=1, source_target_pairs={{4,0},{5,1},{6,2},{7,3},{12,8},{13,9},{14,10},{15,11},{20,16},{21,... | collective-permute-start | bytes 393224 | tf_op jit(solution)/shard_map/ppermute | solution.py:246
  34.6 14.9 %collective-permute-start.6 = (bf16[128,512]{1,0:T(8,128)(2,1)S(1)}, bf16[128,512]{1,0:T(8,128)(2,1)S(1)}, u32[]{:S(2)}, u32[]{:S(2)}) collective-permute-start(bf16[128,512]{1,0:T(8,128)(2,1)S(1)} %get-tuple-element.44), channel_id=1, source_target_pairs={{2,0},{3,1},{4,2},{5,3},{6,4},{7,5},{10,8},{11,9},{12,10},{13,11},... | collective-permute-start | bytes 393224 | tf_op jit(solution)/shard_map/ppermute | solution.py:246
  52.7 11.2 %collective-permute-start.7 = (f32[512,256]{1,0:T(8,128)S(1)}, f32[512,256]{1,0:T(8,128)S(1)}, u32[]{:S(2)}, u32[]{:S(2)}) collective-permute-start(f32[512,256]{1,0:T(8,128)S(1)} %slice.11), channel_id=1, source_target_pairs={{0,1},{1,0},{2,3},{3,2},{4,5},{5,4},{6,7},{7,6},{8,9},{9,8},{10,11... | collective-permute-start | bytes 1572872 | tf_op jit(solution)/shard_map/ppermute | solution.py:240

commit v5 on v4

--- a/solution.py
+++ b/solution.py
@@ -49,13 +49,16 @@
     return jnp.where(ids == doc_row, value, 0.0)
 
 
-def prep_kernel(key, value, query, grad_out, output, lse, pieces, packed):
+def prep_kernel(place, key, value, query, grad_out, output, lse, *refs):
+    pieces, packed, stage = refs[:-2], refs[-2], refs[-1]
     rows, feats = query.shape
     heads = feats // HEAD_DIM
-    for r in range(pieces.shape[0]):
+    for r in range(len(pieces)):
         g = r * heads // GROUP
         at = slice(g * HEAD_DIM, (g + 1) * HEAD_DIM)
-        pieces[r] = jnp.concatenate([key[:, at], value[:, at]], axis=1)
+        stage[r] = jnp.concatenate([key[:, at], value[:, at]], axis=1)
+    for j, piece in enumerate(pieces):
+        piece[...] = stage[place[0] ^ j]
     packed[:, :feats] = query[...]
     packed[:, feats : 2 * feats] = grad_out[...]
     product = grad_out[...].astype(f32) * output[...].astype(f32)
@@ -74,7 +77,14 @@
     packed[:, 2 * feats :] = (jnp.concatenate(table, axis=0).T + delta).astype(bf16)
 
 
-def expand_kernel(sides, panel, *refs):
+def join_kernel(place, *refs):
+    parts, out = refs[:-1], refs[-1]
+    length = parts[0].shape[0]
+    for j, part in enumerate(parts):
+        out[pl.ds(pl.multiple_of((place[0] ^ j) * length, length), length), :] = part[...]
+
+
+def expand_kernel(sides, panel, first, last, *refs):
     packs, docs = refs[:sides], refs[sides]
     q_ext, g_ext, q_t, g_t, docs_out = refs[sides + 1 :]
     docs_out[...] = docs[...]
@@ -110,10 +120,10 @@
 
 
 def band_kernel(causal, q_tile, chained, returns, q_base, *refs):
-    q_panel, k_panel, first, last, q_ext, g_ext, q_t, g_t, docs, pair = refs[:10]
-    refs = refs[10 + (1 if chained else 0) :]
+    place, q_panel, k_panel, first, last, q_ext, g_ext, q_t, g_t, docs, pair = refs[:11]
+    refs = refs[11 + (1 if chained else 0) :]
     parts, refs = refs[:returns], refs[returns:]
-    dq, out, acc, k_ext, v_ext, k_lone = refs
+    dq, *outs, acc, k_ext, v_ext, k_lone = refs
     heads, q_rows, _ = q_ext.shape
     rows = pair.shape[0]
     subs = rows // SUB
@@ -201,19 +211,20 @@
 
         lax.fori_loop(0, q_tiles * subs, step, 0)
 
-    if len(out.shape) == 3:
-        chunk = out.shape[2]
-        for i in range(out.shape[0]):
-            out[i] = acc[:, i * chunk : (i + 1) * chunk]
+    if len(outs) > 1:
+        chunk = outs[0].shape[1]
+        for j, out in enumerate(outs):
+            out[...] = acc[:, pl.ds(pl.multiple_of((place[0] ^ j) * chunk, chunk), chunk)]
     else:
-        out[...] = acc[...].astype(out.dtype)
-
-
-def finish_kernel(ways, count, got, dq, *refs):
-    parts, (grad_query, grad_key, grad_value) = refs[:count], refs[count:]
-    groups = got.shape[0] // ways
+        outs[0][...] = acc[...].astype(outs[0].dtype)
+
+
+def finish_kernel(ways, count, place, dq, *refs):
+    chunks, (other,), (grad_query, grad_key, grad_value, got) = refs[:count], refs[count : count + 1], refs[count + 1 :]
+    for j, chunk in enumerate(chunks):
+        got[place[0] ^ j] = chunk[...]
     keys, values = [], []
-    for g in range(groups):
+    for g in range(count // ways):
         block = got[g * ways]
         for w in range(1, ways):
             block = block + got[g * ways + w]
@@ -221,10 +232,7 @@
         values.append(block[HEAD_DIM:])
     grad_key[...] = jnp.concatenate(keys, axis=0).T
     grad_value[...] = jnp.concatenate(values, axis=0).T
-    total = dq[: grad_query.shape[0], :]
-    for part in parts:
-        total = total + part[...].astype(f32)
-    grad_query[...] = total
+    grad_query[...] = dq[: grad_query.shape[0], :] + other[...]
 
 
 def per_device(query, key, value, output, grad_out, lse, doc_ids):
@@ -245,19 +253,22 @@
     def down(x, d):
         return lax.ppermute(x, "kcol", [(i + 2 * d, i) for i in range(col_count - 2 * d)])
 
-    pieces, packed = pl.pallas_call(
+    def across(x, j):
+        return lax.ppermute(x, "qrow", [(i, i ^ j) for i in range(row_count)]) if j else x
+
+    place = lax.axis_index("qrow").astype(jnp.int32)[None]
+    *pieces, packed = pl.pallas_call(
         prep_kernel,
-        in_specs=[VMEM_SPEC] * 6,
-        out_specs=[VMEM_SPEC] * 2,
-        out_shape=[
-            jax.ShapeDtypeStruct((row_count, key_rows, pair_feats), bf16),
-            jax.ShapeDtypeStruct((rows, 2 * feats + 128), bf16),
-        ],
+        in_specs=[SMEM_SPEC] + [VMEM_SPEC] * 6,
+        out_specs=[VMEM_SPEC] * (row_count + 1),
+        out_shape=[jax.ShapeDtypeStruct((key_rows, pair_feats), bf16)] * row_count
+        + [jax.ShapeDtypeStruct((rows, 2 * feats + 128), bf16)],
+        scratch_shapes=[pltpu.VMEM((row_count, key_rows, pair_feats), bf16)],
         compiler_params=small(56),
         name="prep",
-    )(key, value, query, grad_out, output, lse)
+    )(place, key, value, query, grad_out, output, lse)
     packed_other = swap(packed)
-    pair = lax.all_to_all(pieces, "qrow", 0, 0).reshape(rows, pair_feats)
+    pieces = [across(x, j) for j, x in enumerate(pieces)]
 
     docs = doc_ids.reshape(col_count, rows)
     first, last = docs[:, ::SUB].reshape(-1), docs[:, SUB - 1 :: SUB].reshape(-1)
@@ -265,26 +276,34 @@
 
     q_ext, g_ext, q_t, g_t, docs = pl.pallas_call(
         functools.partial(expand_kernel, 2),
-        in_specs=[SMEM_SPEC] + [VMEM_SPEC] * 3,
+        in_specs=[SMEM_SPEC] * 3 + [VMEM_SPEC] * 3,
         out_specs=[VMEM_SPEC] * 5,
         out_shape=[jax.ShapeDtypeStruct((heads, 2 * rows, 128), bf16)] * 2
         + [jax.ShapeDtypeStruct((feats, 2 * rows), bf16)] * 2
         + [jax.ShapeDtypeStruct(docs.shape, jnp.int32)],
         compiler_params=small(16),
         name="expand",
-    )(mine, packed, packed_other, docs)
-    pair, docs = lax.optimization_barrier((pair, docs))
-
-    def band(name, q_panel, k_panel, block, dq, parts, q_tile, causal, q_base, out):
+    )(mine, first, last, packed, packed_other, docs)
+    *pieces, docs = lax.optimization_barrier((*pieces, docs))
+    pair = pl.pallas_call(
+        join_kernel,
+        in_specs=[SMEM_SPEC] + [VMEM_SPEC] * row_count,
+        out_specs=VMEM_SPEC,
+        out_shape=jax.ShapeDtypeStruct((rows, pair_feats), bf16),
+        compiler_params=small(),
+        name="join",
+    )(place, *pieces)
+
+    def band(name, q_panel, k_panel, block, dq, parts, q_tile, causal, q_base, outs):
         chained = dq is not None
         extra = [dq] if chained else []
         return pl.pallas_call(
             functools.partial(band_kernel, causal, q_tile, chained, len(parts), q_base),
-            in_specs=[SMEM_SPEC] * 4 + [VMEM_SPEC] * (6 + len(extra) + len(parts)),
-            out_specs=[VMEM_SPEC] * 2,
-            out_shape=[jax.ShapeDtypeStruct((2 * rows, feats), f32), out],
+            in_specs=[SMEM_SPEC] * 5 + [VMEM_SPEC] * (6 + len(extra) + len(parts)),
+            out_specs=[VMEM_SPEC] * (1 + len(outs)),
+            out_shape=[jax.ShapeDtypeStruct((2 * rows, feats), f32), *outs],
             scratch_shapes=[pltpu.VMEM((pair_feats, rows), f32)] + [pltpu.VMEM((2, rows, 128), bf16)] * 3,
-            input_output_aliases={10: 0} if chained else {},
+            input_output_aliases={11: 0} if chained else {},
             compiler_params=small(24),
             cost_estimate=pl.CostEstimate(
                 flops=20 * rows * rows * feats,
@@ -292,38 +311,38 @@
                 transcendentals=2 * rows * rows * heads,
             ),
             name=name,
-        )(q_panel, k_panel, first, last, q_ext, g_ext, q_t, g_t, docs, block, *extra, *parts)
+        )(place, q_panel, k_panel, first, last, q_ext, g_ext, q_t, g_t, docs, block, *extra, *parts)
 
     reach = min(chips - 1, chips // 2 + 1)
     order = [*range(2, reach + 1), 1]
     blocks = {d: up(pair, d) for d in order}
     wire = jax.ShapeDtypeStruct((pair_feats, rows), bf16)
-    dq = None
+    whole = jax.ShapeDtypeStruct((pair_feats, rows), f32)
+    here = mine[:1]
+    dq, own = band("own1", mine[1:], here, pair, None, [], 2 * SUB, True, 1, [whole])
     back = []
     for d in order:
         panel = (col - 2 * d).astype(jnp.int32)[None]
-        dq, grads = band(f"band{d}", mine, panel, blocks[d], dq, [], 2 * SUB if d < reach else SUB, False, 0, wire)
+        q_tile = 2 * SUB if d < reach else SUB
+        dq, grads = band(f"band{d}", mine, panel, blocks[d], dq, [], q_tile, False, 0, [wire])
         back.append(down(grads, d))
-    dq, *early = lax.optimization_barrier((dq, *back[:-1]))
-    here = mine[:1]
-    dq, own = band(
-        "own1", mine[1:], here, pair, dq, [], 2 * SUB, True, 1, jax.ShapeDtypeStruct((pair_feats, rows), f32)
-    )
-    dq, chunks = band(
-        "own0", here, here, pair, dq, [own, *early, back[-1]], SUB, True, 0,
-        jax.ShapeDtypeStruct((row_count, pair_feats, key_rows), f32),
-    )
-    dq_parts = [swap(dq[rows:])]
-    got = lax.all_to_all(chunks, "qrow", 0, 0)
+        if d == order[-1]:
+            dq, *early = lax.optimization_barrier((dq, *back[:-1]))
+    chunk = jax.ShapeDtypeStruct((pair_feats, key_rows), f32)
+    parts = [own, *early, back[-1]]
+    dq, *chunks = band("own0", here, here, pair, dq, parts, SUB, True, 0, [chunk] * row_count)
+    chunks = [across(x, j) for j, x in enumerate(chunks)]
+    other = swap(dq[rows:])
     return pl.pallas_call(
-        functools.partial(finish_kernel, row_count * HEAD_DIM // key_feats, len(dq_parts)),
-        in_specs=[VMEM_SPEC] * (2 + len(dq_parts)),
+        functools.partial(finish_kernel, row_count * HEAD_DIM // key_feats, row_count),
+        in_specs=[SMEM_SPEC] + [VMEM_SPEC] * (2 + row_count),
         out_specs=[VMEM_SPEC] * 3,
         out_shape=[jax.ShapeDtypeStruct((rows, feats), f32)]
         + [jax.ShapeDtypeStruct((key_rows, key_feats), f32)] * 2,
+        scratch_shapes=[pltpu.VMEM((row_count, pair_feats, key_rows), f32)],
         compiler_params=small(8),
         name="finish",
-    )(got, dq, *dq_parts)
+    )(place, dq, *chunks, other)
 
 
 def solution(mesh):

time: 65.5 us -> 62.2 us (0.950)
  blocking collectives: 9.4 us -> 0 us
  starting transfers between devices: 17.5 us -> 22.5 us
  waiting for transfers between devices: 13.4 us -> 16.1 us
  local copies, waits for them, and re-layouts: 4.83 us -> 3.27 us
    all_to_all x1 -> x0, blocking collectives: 9.4 us -> none  [per_device(): got = lax.all_to_all(chunks, 'qrow', 0, 0)]
    ppermute x0 -> x6, starting transfers between devices: none -> 7.8 us  [across(): lax.ppermute(x, 'qrow', [(i, i ^ j) for i in range(row_count)])]
    ppermute x0 -> x6, waiting for transfers between devices: none -> 6.03 us  [across(): lax.ppermute(x, 'qrow', [(i, i ^ j) for i in range(row_count)])]
    all_to_all x1 -> x0, starting transfers between devices: 3.86 us -> none  [per_device(): pair = lax.all_to_all(pieces, 'qrow', 0, 0).reshape(rows, pair_feats)]
    ppermute x3, waiting for transfers between devices: 2.32 us -> 0.01 us  [up(): lax.ppermute(x, 'kcol', [(i, i + 2 * d) for i in range(col_count - 2 * d)])]
    all_to_all x1 -> x0, waiting for transfers between devices: 1.65 us -> none  [per_device(): pair = lax.all_to_all(pieces, 'qrow', 0, 0).reshape(rows, pair_feats)]
    unnamed x12, local copies, waits for them, and re-layouts: 4.48 us -> 2.92 us
    ppermute x3, starting transfers between devices: 5.75 us -> 6.69 us  [down(): lax.ppermute(x, 'kcol', [(i + 2 * d, i) for i in range(col_count - 2 * d)])]
  transfers between devices with their start and end apart: 9 -> 14, of which waited for: 3 -> 5; matrix products, arithmetic and copies ran while one was open for 1% -> 1% of each run, Pallas kernels for 19% -> 20%
where the time goes in v5:
time: 62.2 us; the launch traced here: 61.8 us
  starting transfers between devices  22.5 us (36%)
  Pallas kernels  19 us (31%)
  waiting for transfers between devices  16.1 us (26%)
  local copies, waits for them, and re-layouts  3.27 us (5%)
  between operations  0.84 us (1%)
    pallas_call x5, Pallas kernels, band(): pl.pallas_call(functools.partial(band_kernel, causal, q_tile, chained, le...  14.3 us
    ppermute x3, waiting for transfers between devices, down(): lax.ppermute(x, 'kcol', [(i + 2 * d, i) for i in range(col_count - 2 * d)])  10 us
    ppermute x6, starting transfers between devices, across(): lax.ppermute(x, 'qrow', [(i, i ^ j) for i in range(row_count)])  7.8 us
    ppermute x3, starting transfers between devices, down(): lax.ppermute(x, 'kcol', [(i + 2 * d, i) for i in range(col_count - 2 * d)])  6.69 us
    ppermute x3, starting transfers between devices, up(): lax.ppermute(x, 'kcol', [(i, i + 2 * d) for i in range(col_count - 2 * d)])  6.07 us
    ppermute x6, waiting for transfers between devices, across(): lax.ppermute(x, 'qrow', [(i, i ^ j) for i in range(row_count)])  6.03 us
    unnamed x12, local copies, waits for them, and re-layouts  2.92 us
    pallas_call x1, Pallas kernels, per_device(): pl.pallas_call(prep_kernel, in_specs=[SMEM_SPEC] + [VMEM_SPEC] * 6, out_s...  2.39 us
  transfers between devices with their start and end apart: 14, of which 5 were waited for; matrix products, arithmetic and copies ran while one was open for 1% of the time, Pallas kernels for 20%

profile of v5, /device:TPU:16, one launch (start us, length us, event | category | flops | bytes accessed | tf_op | source)
XLA Modules:
  0.0 61.8 jit_solution(9788063586904897898)
XLA Ops:
  0.6 2.4 %prep.1 = (bf16[128,128]{1,0:T(8,128)(2,1)}, bf16[128,128]{1,0:T(8,128)(2,1)}, bf16[128,128]{1,0:T(8,128)(2,1)}, bf16[128,128]{1,0:T(8,128)(2,1)}, bf16[512,640]{1,0:T(8,128)(2,1)}) custom-call(s32[1]{0:T(128)} %bitcast.place.refs_0_, bf16[128,256]{1,0:T(8,128)(2,1)} %key.1, bf16[128,256]{1,0:T(8,128)(2,1)} %value.1, bf16[512,256]{1,0:T(8,128)(2,1)} %query.1, ...), custom_call_target="tpu_custom_call" | custom-call | tf_op jit(solution)/shard_map/prep/pallas_call | solution.py:260
  3.0 0.0 collective-permute-start
  3.0 1.6 %collective-permute-start.1 = (bf16[128,128]{1,0:T(8,128)(2,1)}, bf16[128,128]{1,0:T(8,128)(2,1)S(1)}, u32[]{:S(2)}, u32[]{:S(2)}) collective-permute-start(bf16[128,128]{1,0:T(8,128)(2,1)} %get-tuple-element.40), channel_id=1, source_target_pairs={{0,8},{8,0},{16,24},{24,16},{1,9},{9,1},{17,25},{25,17},{2,10},{10... | collective-permute-start | bytes 98312 | tf_op jit(solution)/shard_map/ppermute | solution.py:257
  4.6 1.5 %collective-permute-start.2 = (bf16[128,128]{1,0:T(8,128)(2,1)}, bf16[128,128]{1,0:T(8,128)(2,1)S(1)}, u32[]{:S(2)}, u32[]{:S(2)}) collective-permute-start(bf16[128,128]{1,0:T(8,128)(2,1)} %get-tuple-element.41), channel_id=1, source_target_pairs={{0,16},{8,24},{16,0},{24,8},{1,17},{9,25},{17,1},{25,9},{2,18},{10... | collective-permute-start | bytes 98312 | tf_op jit(solution)/shard_map/ppermute | solution.py:257
  6.1 0.5 collective-permute-start.3
  6.6 0.1 pad_add_fusion.panel.refs_1_
  6.7 0.1 slice.10
  6.7 0.1 slice.9
  6.8 0.1 reshape.17.last.refs_4_
  6.9 0.1 reshape.16.first.refs_3_
  7.0 0.0 collective-permute-done.refs_1_
  7.0 0.0 copy-start
  7.0 1.1 %copy-done = bf16[512,640]{1,0:T(8,128)(2,1)S(1)} copy-done((bf16[512,640]{1,0:T(8,128)(2,1)S(1)}, bf16[512,640]{1,0:T(8,128)(2,1)}, u32[]{:S(2)}) %copy-start) | copy-done | bytes 655384
  8.1 1.4 %expand.1 = (bf16[4,1024,128]{2,1,0:T(8,128)(2,1)S(1)}, bf16[4,1024,128]{2,1,0:T(8,128)(2,1)S(1)}, bf16[256,1024]{1,0:T(8,128)(2,1)S(1)}, bf16[256,1024]{1,0:T(8,128)(2,1)S(1)}, s32[8,512]{1,0:T(8,128)S(1)}) custom-call(s32[2]{0:T(128)S(1)} %pad_add_fusion.panel.refs_1_, s32[16]{0:T(128)S(1)} %reshape.16.first.refs_3_, s32[16]{0:T(128)S(1)} %reshape.17.last.refs_4_, ...), custom_call_target="tpu_custom_call" | custom-call | tf_op jit(solution)/shard_map/expand/pallas_call | solution.py:277
  9.5 0.0 copy-start.1
  9.5 0.8 %copy-done.1 = bf16[256,1024]{1,0:T(8,128)(2,1)} copy-done((bf16[256,1024]{1,0:T(8,128)(2,1)}, bf16[256,1024]{1,0:T(8,128)(2,1)S(1)}, u32[]{:S(2)}) %copy-start.1) | copy-done | bytes 524312
  10.3 0.0 collective-permute-done.1.refs_1_
  10.3 0.0 collective-permute-done.2.refs_2_
  10.3 0.9 %collective-permute-done.3.refs_3_ = bf16[128,128]{1,0:T(8,128)(2,1)S(1)} collective-permute-done((bf16[128,128]{1,0:T(8,128)(2,1)}, bf16[128,128]{1,0:T(8,128)(2,1)S(1)}, u32[]{:S(2)}, u32[]{:S(2)}) %collective-permute-start.3) | collective-permute-done | bytes 32800 | tf_op jit(solution)/shard_map/ppermute | solution.py:257
  11.2 1.3 %collective-permute-start.6 = (bf16[512,128]{1,0:T(8,128)(2,1)S(1)}, bf16[512,128]{1,0:T(8,128)(2,1)S(1)}, u32[]{:S(2)}, u32[]{:S(2)}) collective-permute-start(bf16[512,128]{1,0:T(8,128)(2,1)S(1)} %join.1.refs_10_), channel_id=1, source_target_pairs={{0,4},{1,5},{2,6},{3,7},{8,12},{9,13},{10,14},{11,15},{16,20},{17,... | collective-permute-start | bytes 393224 | tf_op jit(solution)/shard_map/ppermute | solution.py:251
  12.5 0.7 %collective-permute-start.5 = (bf16[512,128]{1,0:T(8,128)(2,1)S(1)}, bf16[512,128]{1,0:T(8,128)(2,1)S(1)}, u32[]{:S(2)}, u32[]{:S(2)}) collective-permute-start(bf16[512,128]{1,0:T(8,128)(2,1)S(1)} %join.1.refs_10_), channel_id=1, source_target_pairs={{0,6},{1,7},{8,14},{9,15},{16,22},{17,23},{24,30},{25,31}} | collective-permute-start | bytes 393224 | tf_op jit(solution)/shard_map/ppermute | solution.py:251
  13.1 4.1 %collective-permute-start.4 = (bf16[512,128]{1,0:T(8,128)(2,1)S(1)}, bf16[512,128]{1,0:T(8,128)(2,1)S(1)}, u32[]{:S(2)}, u32[]{:S(2)}) collective-permute-start(bf16[512,128]{1,0:T(8,128)(2,1)S(1)} %join.1.refs_10_), channel_id=1, source_target_pairs={{0,2},{1,3},{2,4},{3,5},{4,6},{5,7},{8,10},{9,11},{10,12},{11,13},... | collective-permute-start | bytes 393224 | tf_op jit(solution)/shard_map/ppermute | solution.py:251
  17.2 0.0 copy-start.2
  17.3 1.0 %copy-done.2 = bf16[256,1024]{1,0:T(8,128)(2,1)S(1)} copy-done((bf16[256,1024]{1,0:T(8,128)(2,1)S(1)}, bf16[256,1024]{1,0:T(8,128)(2,1)}, u32[]{:S(2)}) %copy-start.2) | copy-done | bytes 524312
  18.3 3.6 %own1.1 = (f32[1024,256]{1,0:T(8,128)S(1)}, f32[128,512]{1,0:T(8,128)S(1)}) custom-call(s32[1]{0:T(128)} %bitcast.place.refs_0_, s32[1]{0:T(128)} %bitcast.2.refs_1_, s32[1]{0:T(128)} %bitcast.1.refs_2_.refs_1_, s32[16]{0:T(128)S(1)} %reshape.16.first.refs_3_, s32[16]{0:T(128)S(1)} %reshape.17.last.refs_4_, ...), custom_call_target="tpu_custom_call" | custom-call | flops 1342177280 | bytes 6291456 | tf_op jit(solution)/shard_map/own1/pallas_call | solution.py:300
  21.9 0.0 collective-permute-done.6.refs_10_
  21.9 0.6 band2.1
  22.5 0.0 collective-permute-done.5.refs_10_
  22.5 0.6 band3.1
  23.1 0.7 %collective-permute-start.8 = (bf16[128,512]{1,0:T(8,128)(2,1)S(1)}, bf16[128,512]{1,0:T(8,128)(2,1)S(1)}, u32[]{:S(2)}, u32[]{:S(2)}) collective-permute-start(bf16[128,512]{1,0:T(8,128)(2,1)S(1)} %get-tuple-element.54), channel_id=1, source_target_pairs={{6,0},{7,1},{14,8},{15,9},{22,16},{23,17},{30,24},{31,25}} | collective-permute-start | bytes 393224 | tf_op jit(solution)/shard_map/ppermute | solution.py:254
  23.8 4.1 %collective-permute-start.7 = (bf16[128,512]{1,0:T(8,128)(2,1)S(1)}, bf16[128,512]{1,0:T(8,128)(2,1)S(1)}, u32[]{:S(2)}, u32[]{:S(2)}) collective-permute-start(bf16[128,512]{1,0:T(8,128)(2,1)S(1)} %get-tuple-element.53), channel_id=1, source_target_pairs={{4,0},{5,1},{6,2},{7,3},{12,8},{13,9},{14,10},{15,11},{20,16},{21,... | collective-permute-start | bytes 393224 | tf_op jit(solution)/shard_map/ppermute | solution.py:254
  27.9 0.0 collective-permute-done.4.refs_10_
  27.9 0.0 copy-start.3
  27.9 6.3 %band1.1 = (f32[1024,256]{1,0:T(8,128)S(1)}, bf16[128,512]{1,0:T(8,128)(2,1)S(1)}) custom-call(s32[1]{0:T(128)} %bitcast.place.refs_0_, s32[2]{0:T(128)S(1)} %pad_add_fusion.panel.refs_1_, s32[1]{0:T(128)} %bitcast.3.refs_2_, s32[16]{0:T(128)S(1)} %reshape.16.first.refs_3_, s32[16]{0:T(128)S(1)} %reshape.17.last.refs_4_, ...), custom_call_target="tpu_custom_call", output_to_operand_aliasing={{0}: (11, {})} | custom-call | flops 1342177280 | bytes 6291456 | tf_op jit(solution)/shard_map/band1/pallas_call | solution.py:300
  34.2 1.9 %collective-permute-start.9 = (bf16[128,512]{1,0:T(8,128)(2,1)S(1)}, bf16[128,512]{1,0:T(8,128)(2,1)S(1)}, u32[]{:S(2)}, u32[]{:S(2)}) collective-permute-start(bf16[128,512]{1,0:T(8,128)(2,1)S(1)} %get-tuple-element.59), channel_id=1, source_target_pairs={{2,0},{3,1},{4,2},{5,3},{6,4},{7,5},{10,8},{11,9},{12,10},{13,11},... | collective-permute-start | bytes 393224 | tf_op jit(solution)/shard_map/ppermute | solution.py:254
  36.1 0.0 collective-permute-done.8.refs_14_
  36.1 0.0 collective-permute-done.7.refs_13_
  36.2 10.0 %collective-permute-done.9.refs_15_ = bf16[128,512]{1,0:T(8,128)(2,1)S(1)} collective-permute-done((bf16[128,512]{1,0:T(8,128)(2,1)S(1)}, bf16[128,512]{1,0:T(8,128)(2,1)S(1)}, u32[]{:S(2)}, u32[]{:S(2)}) %collective-permute-start.9) | collective-permute-done | bytes 131104 | tf_op jit(solution)/shard_map/ppermute | solution.py:254
  46.2 3.2 %own0.1 = (f32[1024,256]{1,0:T(8,128)S(1)}, f32[128,128]{1,0:T(8,128)S(1)}, f32[128,128]{1,0:T(8,128)S(1)}, f32[128,128]{1,0:T(8,128)S(1)}, f32[128,128]{1,0:T(8,128)S(1)}) custom-call(s32[1]{0:T(128)} %bitcast.place.refs_0_, s32[1]{0:T(128)} %bitcast.1.refs_2_.refs_1_, s32[1]{0:T(128)} %bitcast.1.refs_2_.refs_1_, ...), custom_call_target="tpu_custom_call", output_to_operand_aliasing={{0}: (11, {})} | custom-call | flops 1342177280 | bytes 6291456 | tf_op jit(solution)/shard_map/own0/pallas_call | solution.py:300
  49.5 1.9 %collective-permute-start.13 = (f32[512,256]{1,0:T(8,128)S(1)}, f32[512,256]{1,0:T(8,128)S(1)}, u32[]{:S(2)}, u32[]{:S(2)}) collective-permute-start(f32[512,256]{1,0:T(8,128)S(1)} %slice.11), channel_id=1, source_target_pairs={{0,1},{1,0},{2,3},{3,2},{4,5},{5,4},{6,7},{7,6},{8,9},{9,8},{10,11... | collective-permute-start | bytes 1572872 | tf_op jit(solution)/shard_map/ppermute | solution.py:248
  51.4 2.7 %collective-permute-start.10 = (f32[128,128]{1,0:T(8,128)S(1)}, f32[128,128]{1,0:T(8,128)S(1)}, u32[]{:S(2)}, u32[]{:S(2)}) collective-permute-start(f32[128,128]{1,0:T(8,128)S(1)} %get-tuple-element.62), channel_id=1, source_target_pairs={{0,8},{8,0},{16,24},{24,16},{1,9},{9,1},{17,25},{25,17},{2,10},{10... | collective-permute-start | bytes 196616 | tf_op jit(solution)/shard_map/ppermute | solution.py:257
  54.1 1.5 %collective-permute-start.11 = (f32[128,128]{1,0:T(8,128)S(1)}, f32[128,128]{1,0:T(8,128)S(1)}, u32[]{:S(2)}, u32[]{:S(2)}) collective-permute-start(f32[128,128]{1,0:T(8,128)S(1)} %get-tuple-element.63), channel_id=1, source_target_pairs={{0,16},{8,24},{16,0},{24,8},{1,17},{9,25},{17,1},{25,9},{2,18},{10... | collective-permute-start | bytes 196616 | tf_op jit(solution)/shard_map/ppermute | solution.py:257
  55.6 0.0 collective-permute-start.12
  55.6 0.8 %collective-permute-done.10.refs_1_ = f32[128,128]{1,0:T(8,128)S(1)} collective-permute-done((f32[128,128]{1,0:T(8,128)S(1)}, f32[128,128]{1,0:T(8,128)S(1)}, u32[]{:S(2)}, u32[]{:S(2)}) %collective-permute-start.10) | collective-permute-done | bytes 65568 | tf_op jit(solution)/shard_map/ppermute | solution.py:257
  56.5 1.9 %collective-permute-done.11.refs_2_ = f32[128,128]{1,0:T(8,128)S(1)} collective-permute-done((f32[128,128]{1,0:T(8,128)S(1)}, f32[128,128]{1,0:T(8,128)S(1)}, u32[]{:S(2)}, u32[]{:S(2)}) %collective-permute-start.11) | collective-permute-done | bytes 65568 | tf_op jit(solution)/shard_map/ppermute | solution.py:257
  58.4 2.4 %collective-permute-done.12.refs_3_ = f32[128,128]{1,0:T(8,128)S(1)} collective-permute-done((f32[128,128]{1,0:T(8,128)S(1)}, f32[128,128]{1,0:T(8,128)S(1)}, u32[]{:S(2)}, u32[]{:S(2)}) %collective-permute-start.12) | collective-permute-done | bytes 65568 | tf_op jit(solution)/shard_map/ppermute | solution.py:257
  60.8 0.0 collective-permute-done.13.refs_4_
  60.8 1.0 %finish.1 = (f32[512,256]{1,0:T(8,128)}, f32[128,256]{1,0:T(8,128)}, f32[128,256]{1,0:T(8,128)}) custom-call(s32[1]{0:T(128)} %bitcast.place.refs_0_, f32[1024,256]{1,0:T(8,128)S(1)} %get-tuple-element.60.dq, f32[128,128]{1,0:T(8,128)S(1)} %get-tuple-element.61.refs_0_, f32[128,128]{1,0:T(8,128)S(1)} %collective-permute-done.10.refs_1_, ...), custom_call_target="tpu_custom_call" | custom-call | tf_op jit(solution)/shard_map/finish/pallas_call | solution.py:336
  (8 shorter events, 0.1 us)
Async XLA Ops:
  3.0 3.6 %copy-start.5 = (s32[4096]{0:T(1024)S(1)}, s32[4096]{0:T(1024)}, u32[]{:S(2)}) copy-start(s32[4096]{0:T(1024)} %param.13) | copy-start | bytes 49156
  3.0 4.0 %collective-permute-start = (bf16[512,640]{1,0:T(8,128)(2,1)}, bf16[512,640]{1,0:T(8,128)(2,1)S(1)}, u32[]{:S(2)}, u32[]{:S(2)}) collective-permute-start(bf16[512,640]{1,0:T(8,128)(2,1)} %get-tuple-element.34.refs_0_), channel_id=1, source_target_pairs={{0,1},{1,0},{2,3},{3,2},{4,5},{5,4},{6,7},{7,6},{8,9},{9,8},{10,11... | collective-permute-start | bytes 1966088 | tf_op jit(solution)/shard_map/ppermute | solution.py:248
  3.0 7.2 %collective-permute-start.1 = (bf16[128,128]{1,0:T(8,128)(2,1)}, bf16[128,128]{1,0:T(8,128)(2,1)S(1)}, u32[]{:S(2)}, u32[]{:S(2)}) collective-permute-start(bf16[128,128]{1,0:T(8,128)(2,1)} %get-tuple-element.40), channel_id=1, source_target_pairs={{0,8},{8,0},{16,24},{24,16},{1,9},{9,1},{17,25},{25,17},{2,10},{10... | collective-permute-start | bytes 98312 | tf_op jit(solution)/shard_map/ppermute | solution.py:257
  4.6 5.7 %collective-permute-start.2 = (bf16[128,128]{1,0:T(8,128)(2,1)}, bf16[128,128]{1,0:T(8,128)(2,1)S(1)}, u32[]{:S(2)}, u32[]{:S(2)}) collective-permute-start(bf16[128,128]{1,0:T(8,128)(2,1)} %get-tuple-element.41), channel_id=1, source_target_pairs={{0,16},{8,24},{16,0},{24,8},{1,17},{9,25},{17,1},{25,9},{2,18},{10... | collective-permute-start | bytes 98312 | tf_op jit(solution)/shard_map/ppermute | solution.py:257
  6.1 5.0 %collective-permute-start.3 = (bf16[128,128]{1,0:T(8,128)(2,1)}, bf16[128,128]{1,0:T(8,128)(2,1)S(1)}, u32[]{:S(2)}, u32[]{:S(2)}) collective-permute-start(bf16[128,128]{1,0:T(8,128)(2,1)} %get-tuple-element.42), channel_id=1, source_target_pairs={{0,24},{8,16},{16,8},{24,0},{1,25},{9,17},{17,9},{25,1},{2,26},{10... | collective-permute-start | bytes 98312 | tf_op jit(solution)/shard_map/ppermute | solution.py:257
  7.0 1.1 %copy-start = (bf16[512,640]{1,0:T(8,128)(2,1)S(1)}, bf16[512,640]{1,0:T(8,128)(2,1)}, u32[]{:S(2)}) copy-start(bf16[512,640]{1,0:T(8,128)(2,1)} %get-tuple-element.34.refs_0_) | copy-start | bytes 1966084
  8.1 3.1 %copy-start.4 = (bf16[128,128]{1,0:T(8,128)(2,1)S(1)}, bf16[128,128]{1,0:T(8,128)(2,1)}, u32[]{:S(2)}) copy-start(bf16[128,128]{1,0:T(8,128)(2,1)} %get-tuple-element.45.refs_0_) | copy-start | bytes 98308
  9.5 0.8 %copy-start.1 = (bf16[256,1024]{1,0:T(8,128)(2,1)}, bf16[256,1024]{1,0:T(8,128)(2,1)S(1)}, u32[]{:S(2)}) copy-start(bf16[256,1024]{1,0:T(8,128)(2,1)S(1)} %get-tuple-element.38.refs_8_) | copy-start | bytes 1572868
  11.2 10.7 %collective-permute-start.6 = (bf16[512,128]{1,0:T(8,128)(2,1)S(1)}, bf16[512,128]{1,0:T(8,128)(2,1)S(1)}, u32[]{:S(2)}, u32[]{:S(2)}) collective-permute-start(bf16[512,128]{1,0:T(8,128)(2,1)S(1)} %join.1.refs_10_), channel_id=1, source_target_pairs={{0,4},{1,5},{2,6},{3,7},{8,12},{9,13},{10,14},{11,15},{16,20},{17,... | collective-permute-start | bytes 393224 | tf_op jit(solution)/shard_map/ppermute | solution.py:251
  12.5 10.1 %collective-permute-start.5 = (bf16[512,128]{1,0:T(8,128)(2,1)S(1)}, bf16[512,128]{1,0:T(8,128)(2,1)S(1)}, u32[]{:S(2)}, u32[]{:S(2)}) collective-permute-start(bf16[512,128]{1,0:T(8,128)(2,1)S(1)} %join.1.refs_10_), channel_id=1, source_target_pairs={{0,6},{1,7},{8,14},{9,15},{16,22},{17,23},{24,30},{25,31}} | collective-permute-start | bytes 393224 | tf_op jit(solution)/shard_map/ppermute | solution.py:251
  13.1 14.8 %collective-permute-start.4 = (bf16[512,128]{1,0:T(8,128)(2,1)S(1)}, bf16[512,128]{1,0:T(8,128)(2,1)S(1)}, u32[]{:S(2)}, u32[]{:S(2)}) collective-permute-start(bf16[512,128]{1,0:T(8,128)(2,1)S(1)} %join.1.refs_10_), channel_id=1, source_target_pairs={{0,2},{1,3},{2,4},{3,5},{4,6},{5,7},{8,10},{9,11},{10,12},{11,13},... | collective-permute-start | bytes 393224 | tf_op jit(solution)/shard_map/ppermute | solution.py:251
  17.2 1.0 %copy-start.2 = (bf16[256,1024]{1,0:T(8,128)(2,1)S(1)}, bf16[256,1024]{1,0:T(8,128)(2,1)}, u32[]{:S(2)}) copy-start(bf16[256,1024]{1,0:T(8,128)(2,1)} %copy-done.1) | copy-start | bytes 1572868
  23.1 13.0 %collective-permute-start.8 = (bf16[128,512]{1,0:T(8,128)(2,1)S(1)}, bf16[128,512]{1,0:T(8,128)(2,1)S(1)}, u32[]{:S(2)}, u32[]{:S(2)}) collective-permute-start(bf16[128,512]{1,0:T(8,128)(2,1)S(1)} %get-tuple-element.54), channel_id=1, source_target_pairs={{6,0},{7,1},{14,8},{15,9},{22,16},{23,17},{30,24},{31,25}} | collective-permute-start | bytes 393224 | tf_op jit(solution)/shard_map/ppermute | solution.py:254
  23.8 12.4 %collective-permute-start.7 = (bf16[128,512]{1,0:T(8,128)(2,1)S(1)}, bf16[128,512]{1,0:T(8,128)(2,1)S(1)}, u32[]{:S(2)}, u32[]{:S(2)}) collective-permute-start(bf16[128,512]{1,0:T(8,128)(2,1)S(1)} %get-tuple-element.53), channel_id=1, source_target_pairs={{4,0},{5,1},{6,2},{7,3},{12,8},{13,9},{14,10},{15,11},{20,16},{21,... | collective-permute-start | bytes 393224 | tf_op jit(solution)/shard_map/ppermute | solution.py:254
  27.9 18.3 %copy-start.3 = (bf16[256,1024]{1,0:T(8,128)(2,1)S(1)}, bf16[256,1024]{1,0:T(8,128)(2,1)}, u32[]{:S(2)}) copy-start(bf16[256,1024]{1,0:T(8,128)(2,1)} %copy-done.1) | copy-start | bytes 1572868
  34.2 12.0 %collective-permute-start.9 = (bf16[128,512]{1,0:T(8,128)(2,1)S(1)}, bf16[128,512]{1,0:T(8,128)(2,1)S(1)}, u32[]{:S(2)}, u32[]{:S(2)}) collective-permute-start(bf16[128,512]{1,0:T(8,128)(2,1)S(1)} %get-tuple-element.59), channel_id=1, source_target_pairs={{2,0},{3,1},{4,2},{5,3},{6,4},{7,5},{10,8},{11,9},{12,10},{13,11},... | collective-permute-start | bytes 393224 | tf_op jit(solution)/shard_map/ppermute | solution.py:254
  49.5 11.4 %collective-permute-start.13 = (f32[512,256]{1,0:T(8,128)S(1)}, f32[512,256]{1,0:T(8,128)S(1)}, u32[]{:S(2)}, u32[]{:S(2)}) collective-permute-start(f32[512,256]{1,0:T(8,128)S(1)} %slice.11), channel_id=1, source_target_pairs={{0,1},{1,0},{2,3},{3,2},{4,5},{5,4},{6,7},{7,6},{8,9},{9,8},{10,11... | collective-permute-start | bytes 1572872 | tf_op jit(solution)/shard_map/ppermute | solution.py:248
  51.4 5.1 %collective-permute-start.10 = (f32[128,128]{1,0:T(8,128)S(1)}, f32[128,128]{1,0:T(8,128)S(1)}, u32[]{:S(2)}, u32[]{:S(2)}) collective-permute-start(f32[128,128]{1,0:T(8,128)S(1)} %get-tuple-element.62), channel_id=1, source_target_pairs={{0,8},{8,0},{16,24},{24,16},{1,9},{9,1},{17,25},{25,17},{2,10},{10... | collective-permute-start | bytes 196616 | tf_op jit(solution)/shard_map/ppermute | solution.py:257
  54.1 4.3 %collective-permute-start.11 = (f32[128,128]{1,0:T(8,128)S(1)}, f32[128,128]{1,0:T(8,128)S(1)}, u32[]{:S(2)}, u32[]{:S(2)}) collective-permute-start(f32[128,128]{1,0:T(8,128)S(1)} %get-tuple-element.63), channel_id=1, source_target_pairs={{0,16},{8,24},{16,0},{24,8},{1,17},{9,25},{17,1},{25,9},{2,18},{10... | collective-permute-start | bytes 196616 | tf_op jit(solution)/shard_map/ppermute | solution.py:257
  55.6 5.2 %collective-permute-start.12 = (f32[128,128]{1,0:T(8,128)S(1)}, f32[128,128]{1,0:T(8,128)S(1)}, u32[]{:S(2)}, u32[]{:S(2)}) collective-permute-start(f32[128,128]{1,0:T(8,128)S(1)} %get-tuple-element.64), channel_id=1, source_target_pairs={{0,24},{8,16},{16,8},{24,0},{1,25},{9,17},{17,9},{25,1},{2,26},{10... | collective-permute-start | bytes 196616 | tf_op jit(solution)/shard_map/ppermute | solution.py:257

commit v6 on v5

--- a/solution.py
+++ b/solution.py
@@ -86,8 +86,7 @@
 
 def expand_kernel(sides, panel, first, last, *refs):
     packs, docs = refs[:sides], refs[sides]
-    q_ext, g_ext, q_t, g_t, docs_out = refs[sides + 1 :]
-    docs_out[...] = docs[...]
+    q_ext, g_ext, q_t, g_t = refs[sides + 1 :]
     feats = q_t.shape[0]
     heads = feats // HEAD_DIM
     rows = docs.shape[1]
@@ -119,11 +118,11 @@
             g_ext[2 * p + 1, dst, :] = jnp.where(low_half, g_more, g_pair).astype(bf16)
 
 
-def band_kernel(causal, q_tile, chained, returns, q_base, *refs):
-    place, q_panel, k_panel, first, last, q_ext, g_ext, q_t, g_t, docs, pair = refs[:11]
-    refs = refs[11 + (1 if chained else 0) :]
-    parts, refs = refs[:returns], refs[returns:]
-    dq, *outs, acc, k_ext, v_ext, k_lone = refs
+def band_kernel(shift, q_tile, chained, *refs):
+    causal = shift == 0
+    q_panel, first, last, q_ext, g_ext, q_t, g_t, docs, pair = refs[:9]
+    refs = refs[9 + (1 if chained else 0) :]
+    dq, out, acc, k_ext, v_ext, k_lone = refs
     heads, q_rows, _ = q_ext.shape
     rows = pair.shape[0]
     subs = rows // SUB
@@ -132,16 +131,10 @@
     q_tiles = q_panel.shape[0] * per_panel
     if not chained:
         dq[...] = jnp.zeros_like(dq)
-    if returns:
-        total = parts[0][...].astype(f32)
-        for part in parts[1:]:
-            total = total + part[...].astype(f32)
-        acc[...] = total
-    else:
-        acc[...] = jnp.zeros_like(acc)
+    acc[...] = jnp.zeros_like(acc)
 
     def one(qt, kt, masked):
-        at_q = pl.ds(pl.multiple_of(q_base * rows + qt * q_tile, q_tile), q_tile)
+        at_q = pl.ds(pl.multiple_of(qt * q_tile, q_tile), q_tile)
         at_k = pl.ds(pl.multiple_of(kt * SUB, SUB), SUB)
         weights, score_grads = [], []
         if masked:
@@ -167,7 +160,7 @@
         acc[:HEAD_DIM, at_k] += key_sum
         acc[HEAD_DIM:, at_k] += value_sum
 
-    key_side = k_panel[0]
+    key_side = q_panel[0] - shift
     some = first[q_panel[0] * subs] <= last[jnp.maximum(key_side, 0) * subs + subs - 1]
     for j in range(1, q_panel.shape[0]):
         some = some | (first[q_panel[j] * subs] <= last[jnp.maximum(key_side, 0) * subs + subs - 1])
@@ -211,12 +204,18 @@
 
         lax.fori_loop(0, q_tiles * subs, step, 0)
 
-    if len(outs) > 1:
-        chunk = outs[0].shape[1]
-        for j, out in enumerate(outs):
-            out[...] = acc[:, pl.ds(pl.multiple_of((place[0] ^ j) * chunk, chunk), chunk)]
-    else:
-        outs[0][...] = acc[...].astype(outs[0].dtype)
+    out[...] = acc[...].astype(out.dtype)
+
+
+def collect_kernel(ways, place, *refs):
+    parts, outs = refs[:-ways], refs[-ways:]
+    chunk = outs[0].shape[1]
+    for j, out in enumerate(outs):
+        at = pl.ds(pl.multiple_of((place[0] ^ j) * chunk, chunk), chunk)
+        total = parts[0][:, at]
+        for part in parts[1:]:
+            total = total + part[:, at].astype(f32)
+        out[...] = total
 
 
 def finish_kernel(ways, count, place, dq, *refs):
@@ -274,17 +273,15 @@
     first, last = docs[:, ::SUB].reshape(-1), docs[:, SUB - 1 :: SUB].reshape(-1)
     mine = jnp.stack([col, col ^ 1]).astype(jnp.int32)
 
-    q_ext, g_ext, q_t, g_t, docs = pl.pallas_call(
+    q_ext, g_ext, q_t, g_t = pl.pallas_call(
         functools.partial(expand_kernel, 2),
         in_specs=[SMEM_SPEC] * 3 + [VMEM_SPEC] * 3,
-        out_specs=[VMEM_SPEC] * 5,
+        out_specs=[VMEM_SPEC] * 4,
         out_shape=[jax.ShapeDtypeStruct((heads, 2 * rows, 128), bf16)] * 2
-        + [jax.ShapeDtypeStruct((feats, 2 * rows), bf16)] * 2
-        + [jax.ShapeDtypeStruct(docs.shape, jnp.int32)],
+        + [jax.ShapeDtypeStruct((feats, 2 * rows), bf16)] * 2,
         compiler_params=small(16),
         name="expand",
     )(mine, first, last, packed, packed_other, docs)
-    *pieces, docs = lax.optimization_barrier((*pieces, docs))
     pair = pl.pallas_call(
         join_kernel,
         in_specs=[SMEM_SPEC] + [VMEM_SPEC] * row_count,
@@ -294,16 +291,19 @@
         name="join",
     )(place, *pieces)
 
-    def band(name, q_panel, k_panel, block, dq, parts, q_tile, causal, q_base, outs):
+    def band(name, shift, block, dq, q_tile, out_type):
         chained = dq is not None
         extra = [dq] if chained else []
         return pl.pallas_call(
-            functools.partial(band_kernel, causal, q_tile, chained, len(parts), q_base),
-            in_specs=[SMEM_SPEC] * 5 + [VMEM_SPEC] * (6 + len(extra) + len(parts)),
-            out_specs=[VMEM_SPEC] * (1 + len(outs)),
-            out_shape=[jax.ShapeDtypeStruct((2 * rows, feats), f32), *outs],
+            functools.partial(band_kernel, shift, q_tile, chained),
+            in_specs=[SMEM_SPEC] * 3 + [VMEM_SPEC] * (6 + len(extra)),
+            out_specs=[VMEM_SPEC] * 2,
+            out_shape=[
+                jax.ShapeDtypeStruct((2 * rows, feats), f32),
+                jax.ShapeDtypeStruct((pair_feats, rows), out_type),
+            ],
             scratch_shapes=[pltpu.VMEM((pair_feats, rows), f32)] + [pltpu.VMEM((2, rows, 128), bf16)] * 3,
-            input_output_aliases={11: 0} if chained else {},
+            input_output_aliases={9: 0} if chained else {},
             compiler_params=small(24),
             cost_estimate=pl.CostEstimate(
                 flops=20 * rows * rows * feats,
@@ -311,26 +311,29 @@
                 transcendentals=2 * rows * rows * heads,
             ),
             name=name,
-        )(place, q_panel, k_panel, first, last, q_ext, g_ext, q_t, g_t, docs, block, *extra, *parts)
+        )(mine, first, last, q_ext, g_ext, q_t, g_t, docs, block, *extra)
 
     reach = min(chips - 1, chips // 2 + 1)
     order = [*range(2, reach + 1), 1]
-    blocks = {d: up(pair, d) for d in order}
-    wire = jax.ShapeDtypeStruct((pair_feats, rows), bf16)
-    whole = jax.ShapeDtypeStruct((pair_feats, rows), f32)
-    here = mine[:1]
-    dq, own = band("own1", mine[1:], here, pair, None, [], 2 * SUB, True, 1, [whole])
+    blocks = {d: up(pair, d) for d in order[:-1]}
+    dq, own = band("own", 0, pair, None, SUB, f32)
+    late, own = lax.optimization_barrier((pair, own))
+    blocks[1] = up(late, 1)
     back = []
     for d in order:
-        panel = (col - 2 * d).astype(jnp.int32)[None]
         q_tile = 2 * SUB if d < reach else SUB
-        dq, grads = band(f"band{d}", mine, panel, blocks[d], dq, [], q_tile, False, 0, [wire])
+        dq, grads = band(f"band{d}", 2 * d, blocks[d], dq, q_tile, bf16)
         back.append(down(grads, d))
-        if d == order[-1]:
-            dq, *early = lax.optimization_barrier((dq, *back[:-1]))
+    dq, *back = lax.optimization_barrier((dq, *back))
     chunk = jax.ShapeDtypeStruct((pair_feats, key_rows), f32)
-    parts = [own, *early, back[-1]]
-    dq, *chunks = band("own0", here, here, pair, dq, parts, SUB, True, 0, [chunk] * row_count)
+    chunks = pl.pallas_call(
+        functools.partial(collect_kernel, row_count),
+        in_specs=[SMEM_SPEC] + [VMEM_SPEC] * (1 + len(back)),
+        out_specs=[VMEM_SPEC] * row_count,
+        out_shape=[chunk] * row_count,
+        compiler_params=small(8),
+        name="collect",
+    )(place, own, *back)
     chunks = [across(x, j) for j, x in enumerate(chunks)]
     other = swap(dq[rows:])
     return pl.pallas_call(

time: 62.2 us -> 57.1 us (0.918)
  waiting for transfers between devices: 16.1 us -> 13.5 us
  starting transfers between devices: 22.5 us -> 21.4 us
  local copies, waits for them, and re-layouts: 3.27 us -> 2.19 us
    ppermute x3, waiting for transfers between devices: 10 us -> 6.19 us  [down(): lax.ppermute(x, 'kcol', [(i + 2 * d, i) for i in range(col_count - 2 * d)])]
    ppermute x2, starting transfers between devices: 1.94 us -> 0.18 us  [swap(): return lax.ppermute(x, 'kcol', [(i, i ^ 1) for i in range(col_count)])]
    ppermute x3, starting transfers between devices: 6.69 us -> 8.05 us  [down(): lax.ppermute(x, 'kcol', [(i + 2 * d, i) for i in range(col_count - 2 * d)])]
    ppermute x6, waiting for transfers between devices: 6.03 us -> 7.27 us  [across(): lax.ppermute(x, 'qrow', [(i, i ^ j) for i in range(row_count)])]
    unnamed x12 -> x6, local copies, waits for them, and re-layouts: 2.92 us -> 1.84 us
    ppermute x6, starting transfers between devices: 7.8 us -> 7.07 us  [across(): lax.ppermute(x, 'qrow', [(i, i ^ j) for i in range(row_count)])]
  transfers between devices with their start and end apart: 14 -> 14, of which waited for: 5 -> 8; matrix products, arithmetic and copies ran while one was open for 1% -> 1% of each run, Pallas kernels for 20% -> 27%
where the time goes in v6:
time: 57.1 us; the launch traced here: 56.7 us
  starting transfers between devices  21.4 us (37%)
  Pallas kernels  18.8 us (33%)
  waiting for transfers between devices  13.5 us (24%)
  local copies, waits for them, and re-layouts  2.19 us (4%)
  between operations  0.8 us (1%)
    pallas_call x4, Pallas kernels, band(): pl.pallas_call(functools.partial(band_kernel, shift, q_tile, chained), in...  13.9 us
    ppermute x3, starting transfers between devices, down(): lax.ppermute(x, 'kcol', [(i + 2 * d, i) for i in range(col_count - 2 * d)])  8.05 us
    ppermute x6, waiting for transfers between devices, across(): lax.ppermute(x, 'qrow', [(i, i ^ j) for i in range(row_count)])  7.27 us
    ppermute x6, starting transfers between devices, across(): lax.ppermute(x, 'qrow', [(i, i ^ j) for i in range(row_count)])  7.07 us
    ppermute x3, waiting for transfers between devices, down(): lax.ppermute(x, 'kcol', [(i + 2 * d, i) for i in range(col_count - 2 * d)])  6.19 us
    ppermute x3, starting transfers between devices, up(): lax.ppermute(x, 'kcol', [(i, i + 2 * d) for i in range(col_count - 2 * d)])  6.07 us
    pallas_call x1, Pallas kernels, per_device(): pl.pallas_call(prep_kernel, in_specs=[SMEM_SPEC] + [VMEM_SPEC] * 6, out_s...  2.4 us
    unnamed x6, local copies, waits for them, and re-layouts  1.84 us
  transfers between devices with their start and end apart: 14, of which 8 were waited for; matrix products, arithmetic and copies ran while one was open for 1% of the time, Pallas kernels for 27%

profile of v6, /device:TPU:16, one launch (start us, length us, event | category | flops | bytes accessed | tf_op | source)
XLA Modules:
  0.0 56.7 jit_solution(15511061500915026826)
XLA Ops:
  0.6 2.4 %prep.1 = (bf16[128,128]{1,0:T(8,128)(2,1)}, bf16[128,128]{1,0:T(8,128)(2,1)}, bf16[128,128]{1,0:T(8,128)(2,1)}, bf16[128,128]{1,0:T(8,128)(2,1)}, bf16[512,640]{1,0:T(8,128)(2,1)}) custom-call(s32[1]{0:T(128)} %bitcast.place, bf16[128,256]{1,0:T(8,128)(2,1)} %key.1, bf16[128,256]{1,0:T(8,128)(2,1)} %value.1, bf16[512,256]{1,0:T(8,128)(2,1)} %query.1, ...), custom_call_target="tpu_custom_call" | custom-call | tf_op jit(solution)/shard_map/prep/pallas_call | solution.py:259
  3.0 0.0 collective-permute-start
  3.0 1.5 %collective-permute-start.1 = (bf16[128,128]{1,0:T(8,128)(2,1)}, bf16[128,128]{1,0:T(8,128)(2,1)S(1)}, u32[]{:S(2)}, u32[]{:S(2)}) collective-permute-start(bf16[128,128]{1,0:T(8,128)(2,1)} %get-tuple-element.36), channel_id=1, source_target_pairs={{0,8},{8,0},{16,24},{24,16},{1,9},{9,1},{17,25},{25,17},{2,10},{10... | collective-permute-start | bytes 98312 | tf_op jit(solution)/shard_map/ppermute | solution.py:256
  4.5 1.5 %collective-permute-start.2 = (bf16[128,128]{1,0:T(8,128)(2,1)}, bf16[128,128]{1,0:T(8,128)(2,1)S(1)}, u32[]{:S(2)}, u32[]{:S(2)}) collective-permute-start(bf16[128,128]{1,0:T(8,128)(2,1)} %get-tuple-element.37), channel_id=1, source_target_pairs={{0,16},{8,24},{16,0},{24,8},{1,17},{9,25},{17,1},{25,9},{2,18},{10... | collective-permute-start | bytes 98312 | tf_op jit(solution)/shard_map/ppermute | solution.py:256
  6.1 0.5 collective-permute-start.3
  6.5 0.6 %collective-permute-done.1.refs_1_ = bf16[128,128]{1,0:T(8,128)(2,1)S(1)} collective-permute-done((bf16[128,128]{1,0:T(8,128)(2,1)}, bf16[128,128]{1,0:T(8,128)(2,1)S(1)}, u32[]{:S(2)}, u32[]{:S(2)}) %collective-permute-start.1) | collective-permute-done | bytes 32800 | tf_op jit(solution)/shard_map/ppermute | solution.py:256
  7.2 1.5 %collective-permute-done.2.refs_2_ = bf16[128,128]{1,0:T(8,128)(2,1)S(1)} collective-permute-done((bf16[128,128]{1,0:T(8,128)(2,1)}, bf16[128,128]{1,0:T(8,128)(2,1)S(1)}, u32[]{:S(2)}, u32[]{:S(2)}) %collective-permute-start.2) | collective-permute-done | bytes 32800 | tf_op jit(solution)/shard_map/ppermute | solution.py:256
  8.7 2.4 %collective-permute-done.3.refs_3_ = bf16[128,128]{1,0:T(8,128)(2,1)S(1)} collective-permute-done((bf16[128,128]{1,0:T(8,128)(2,1)}, bf16[128,128]{1,0:T(8,128)(2,1)S(1)}, u32[]{:S(2)}, u32[]{:S(2)}) %collective-permute-start.3) | collective-permute-done | bytes 32800 | tf_op jit(solution)/shard_map/ppermute | solution.py:256
  11.1 0.0 copy-start.1
  11.1 0.8 %copy-done.1 = bf16[128,128]{1,0:T(8,128)(2,1)S(1)} copy-done((bf16[128,128]{1,0:T(8,128)(2,1)S(1)}, bf16[128,128]{1,0:T(8,128)(2,1)}, u32[]{:S(2)}) %copy-start.1) | copy-done | bytes 32792
  11.8 0.0 copy-start.2
  11.9 1.3 %collective-permute-start.6 = (bf16[512,128]{1,0:T(8,128)(2,1)S(1)}, bf16[512,128]{1,0:T(8,128)(2,1)S(1)}, u32[]{:S(2)}, u32[]{:S(2)}) collective-permute-start(bf16[512,128]{1,0:T(8,128)(2,1)S(1)} %join.1.refs_8_), channel_id=1, source_target_pairs={{0,4},{1,5},{2,6},{3,7},{8,12},{9,13},{10,14},{11,15},{16,20},{17,... | collective-permute-start | bytes 393224 | tf_op jit(solution)/shard_map/ppermute | solution.py:250
  13.2 0.1 pad_add_fusion.panel.refs_0_
  13.2 0.0 copy-done.2
  13.2 0.1 slice.10
  13.3 0.1 slice.9
  13.4 0.1 reshape.17.last.refs_2_
  13.5 0.1 reshape.16.first.refs_1_
  13.6 0.7 %collective-permute-start.5 = (bf16[512,128]{1,0:T(8,128)(2,1)S(1)}, bf16[512,128]{1,0:T(8,128)(2,1)S(1)}, u32[]{:S(2)}, u32[]{:S(2)}) collective-permute-start(bf16[512,128]{1,0:T(8,128)(2,1)S(1)} %join.1.refs_8_), channel_id=1, source_target_pairs={{0,6},{1,7},{8,14},{9,15},{16,22},{17,23},{24,30},{25,31}} | collective-permute-start | bytes 393224 | tf_op jit(solution)/shard_map/ppermute | solution.py:250
  14.2 0.0 collective-permute-done.refs_1_
  14.2 0.0 copy-start
  14.2 1.1 %copy-done = bf16[512,640]{1,0:T(8,128)(2,1)S(1)} copy-done((bf16[512,640]{1,0:T(8,128)(2,1)S(1)}, bf16[512,640]{1,0:T(8,128)(2,1)}, u32[]{:S(2)}) %copy-start) | copy-done | bytes 655384
  15.3 1.4 %expand.1 = (bf16[4,1024,128]{2,1,0:T(8,128)(2,1)S(1)}, bf16[4,1024,128]{2,1,0:T(8,128)(2,1)S(1)}, bf16[256,1024]{1,0:T(8,128)(2,1)S(1)}, bf16[256,1024]{1,0:T(8,128)(2,1)S(1)}) custom-call(s32[2]{0:T(128)S(1)} %pad_add_fusion.panel.refs_0_, s32[16]{0:T(128)S(1)} %reshape.16.first.refs_1_, s32[16]{0:T(128)S(1)} %reshape.17.last.refs_2_, ...), custom_call_target="tpu_custom_call" | custom-call | tf_op jit(solution)/shard_map/expand/pallas_call | solution.py:276
  16.7 6.4 %own.1 = (f32[1024,256]{1,0:T(8,128)S(1)}, f32[128,512]{1,0:T(8,128)S(1)}) custom-call(s32[2]{0:T(128)S(1)} %pad_add_fusion.panel.refs_0_, s32[16]{0:T(128)S(1)} %reshape.16.first.refs_1_, s32[16]{0:T(128)S(1)} %reshape.17.last.refs_2_, bf16[4,1024,128]{2,1,0:T(8,128)(2,1)S(1)} %get-tuple-element.31.refs_3_, ...), custom_call_target="tpu_custom_call" | custom-call | flops 1342177280 | bytes 6291456 | tf_op jit(solution)/shard_map/own/pallas_call | solution.py:297
  23.1 4.1 %collective-permute-start.4 = (bf16[512,128]{1,0:T(8,128)(2,1)S(1)}, bf16[512,128]{1,0:T(8,128)(2,1)S(1)}, u32[]{:S(2)}, u32[]{:S(2)}) collective-permute-start(bf16[512,128]{1,0:T(8,128)(2,1)S(1)} %join.1.refs_8_), channel_id=1, source_target_pairs={{0,2},{1,3},{2,4},{3,5},{4,6},{5,7},{8,10},{9,11},{10,12},{11,13},... | collective-permute-start | bytes 393224 | tf_op jit(solution)/shard_map/ppermute | solution.py:250
  27.3 0.0 collective-permute-done.6.refs_8_
  27.3 0.6 %band2.1 = (f32[1024,256]{1,0:T(8,128)S(1)}, bf16[128,512]{1,0:T(8,128)(2,1)S(1)}) custom-call(s32[2]{0:T(128)S(1)} %pad_add_fusion.panel.refs_0_, s32[16]{0:T(128)S(1)} %reshape.16.first.refs_1_, s32[16]{0:T(128)S(1)} %reshape.17.last.refs_2_, bf16[4,1024,128]{2,1,0:T(8,128)(2,1)S(1)} %get-tuple-element.31.refs_3_, ...), custom_call_target="tpu_custom_call", output_to_operand_aliasing={{0}: (9, {})} | custom-call | flops 1342177280 | bytes 6291456 | tf_op jit(solution)/shard_map/band2/pallas_call | solution.py:297
  27.9 0.0 collective-permute-done.5.refs_8_
  27.9 0.6 %band3.1 = (f32[1024,256]{1,0:T(8,128)S(1)}, bf16[128,512]{1,0:T(8,128)(2,1)S(1)}) custom-call(s32[2]{0:T(128)S(1)} %pad_add_fusion.panel.refs_0_, s32[16]{0:T(128)S(1)} %reshape.16.first.refs_1_, s32[16]{0:T(128)S(1)} %reshape.17.last.refs_2_, bf16[4,1024,128]{2,1,0:T(8,128)(2,1)S(1)} %get-tuple-element.31.refs_3_, ...), custom_call_target="tpu_custom_call", output_to_operand_aliasing={{0}: (9, {})} | custom-call | flops 1342177280 | bytes 6291456 | tf_op jit(solution)/shard_map/band3/pallas_call | solution.py:297
  28.5 0.7 %collective-permute-start.8 = (bf16[128,512]{1,0:T(8,128)(2,1)S(1)}, bf16[128,512]{1,0:T(8,128)(2,1)S(1)}, u32[]{:S(2)}, u32[]{:S(2)}) collective-permute-start(bf16[128,512]{1,0:T(8,128)(2,1)S(1)} %get-tuple-element.46), channel_id=1, source_target_pairs={{6,0},{7,1},{14,8},{15,9},{22,16},{23,17},{30,24},{31,25}} | collective-permute-start | bytes 393224 | tf_op jit(solution)/shard_map/ppermute | solution.py:253
  29.1 5.5 %collective-permute-start.7 = (bf16[128,512]{1,0:T(8,128)(2,1)S(1)}, bf16[128,512]{1,0:T(8,128)(2,1)S(1)}, u32[]{:S(2)}, u32[]{:S(2)}) collective-permute-start(bf16[128,512]{1,0:T(8,128)(2,1)S(1)} %get-tuple-element.45), channel_id=1, source_target_pairs={{4,0},{5,1},{6,2},{7,3},{12,8},{13,9},{14,10},{15,11},{20,16},{21,... | collective-permute-start | bytes 393224 | tf_op jit(solution)/shard_map/ppermute | solution.py:253
  34.6 0.0 collective-permute-done.4.refs_8_
  34.6 6.3 %band1.1 = (f32[1024,256]{1,0:T(8,128)S(1)}, bf16[128,512]{1,0:T(8,128)(2,1)S(1)}) custom-call(s32[2]{0:T(128)S(1)} %pad_add_fusion.panel.refs_0_, s32[16]{0:T(128)S(1)} %reshape.16.first.refs_1_, s32[16]{0:T(128)S(1)} %reshape.17.last.refs_2_, bf16[4,1024,128]{2,1,0:T(8,128)(2,1)S(1)} %get-tuple-element.31.refs_3_, ...), custom_call_target="tpu_custom_call", output_to_operand_aliasing={{0}: (9, {})} | custom-call | flops 1342177280 | bytes 6291456 | tf_op jit(solution)/shard_map/band1/pallas_call | solution.py:297
  40.9 1.9 %collective-permute-start.9 = (bf16[128,512]{1,0:T(8,128)(2,1)S(1)}, bf16[128,512]{1,0:T(8,128)(2,1)S(1)}, u32[]{:S(2)}, u32[]{:S(2)}) collective-permute-start(bf16[128,512]{1,0:T(8,128)(2,1)S(1)} %get-tuple-element.47), channel_id=1, source_target_pairs={{2,0},{3,1},{4,2},{5,3},{6,4},{7,5},{10,8},{11,9},{12,10},{13,11},... | collective-permute-start | bytes 393224 | tf_op jit(solution)/shard_map/ppermute | solution.py:253
  42.9 0.0 collective-permute-done.8.refs_2_
  42.9 0.8 %collective-permute-done.7.refs_1_ = bf16[128,512]{1,0:T(8,128)(2,1)S(1)} collective-permute-done((bf16[128,512]{1,0:T(8,128)(2,1)S(1)}, bf16[128,512]{1,0:T(8,128)(2,1)S(1)}, u32[]{:S(2)}, u32[]{:S(2)}) %collective-permute-start.7) | collective-permute-done | bytes 131104 | tf_op jit(solution)/shard_map/ppermute | solution.py:253
  43.7 5.4 %collective-permute-done.9.refs_3_ = bf16[128,512]{1,0:T(8,128)(2,1)S(1)} collective-permute-done((bf16[128,512]{1,0:T(8,128)(2,1)S(1)}, bf16[128,512]{1,0:T(8,128)(2,1)S(1)}, u32[]{:S(2)}, u32[]{:S(2)}) %collective-permute-start.9) | collective-permute-done | bytes 131104 | tf_op jit(solution)/shard_map/ppermute | solution.py:253
  49.1 0.2 collective-permute-start.13
  49.3 0.1 collect.1
  49.4 0.6 %collective-permute-start.10 = (f32[128,128]{1,0:T(8,128)S(1)}, f32[128,128]{1,0:T(8,128)S(1)}, u32[]{:S(2)}, u32[]{:S(2)}) collective-permute-start(f32[128,128]{1,0:T(8,128)S(1)} %get-tuple-element.54), channel_id=1, source_target_pairs={{0,8},{8,0},{16,24},{24,16},{1,9},{9,1},{17,25},{25,17},{2,10},{10... | collective-permute-start | bytes 196616 | tf_op jit(solution)/shard_map/ppermute | solution.py:256
  50.0 0.5 collective-permute-start.11
  50.5 2.4 %collective-permute-start.12 = (f32[128,128]{1,0:T(8,128)S(1)}, f32[128,128]{1,0:T(8,128)S(1)}, u32[]{:S(2)}, u32[]{:S(2)}) collective-permute-start(f32[128,128]{1,0:T(8,128)S(1)} %get-tuple-element.56), channel_id=1, source_target_pairs={{0,24},{8,16},{16,8},{24,0},{1,25},{9,17},{17,9},{25,1},{2,26},{10... | collective-permute-start | bytes 196616 | tf_op jit(solution)/shard_map/ppermute | solution.py:256
  53.0 0.9 %collective-permute-done.10.refs_1_ = f32[128,128]{1,0:T(8,128)S(1)} collective-permute-done((f32[128,128]{1,0:T(8,128)S(1)}, f32[128,128]{1,0:T(8,128)S(1)}, u32[]{:S(2)}, u32[]{:S(2)}) %collective-permute-start.10) | collective-permute-done | bytes 65568 | tf_op jit(solution)/shard_map/ppermute | solution.py:256
  53.8 1.1 %collective-permute-done.11.refs_2_ = f32[128,128]{1,0:T(8,128)S(1)} collective-permute-done((f32[128,128]{1,0:T(8,128)S(1)}, f32[128,128]{1,0:T(8,128)S(1)}, u32[]{:S(2)}, u32[]{:S(2)}) %collective-permute-start.11) | collective-permute-done | bytes 65568 | tf_op jit(solution)/shard_map/ppermute | solution.py:256
  55.0 0.7 %collective-permute-done.12.refs_3_ = f32[128,128]{1,0:T(8,128)S(1)} collective-permute-done((f32[128,128]{1,0:T(8,128)S(1)}, f32[128,128]{1,0:T(8,128)S(1)}, u32[]{:S(2)}, u32[]{:S(2)}) %collective-permute-start.12) | collective-permute-done | bytes 65568 | tf_op jit(solution)/shard_map/ppermute | solution.py:256
  55.7 0.0 collective-permute-done.13.refs_4_
  55.7 1.0 %finish.1 = (f32[512,256]{1,0:T(8,128)}, f32[128,256]{1,0:T(8,128)}, f32[128,256]{1,0:T(8,128)}) custom-call(s32[1]{0:T(128)} %bitcast.place, f32[1024,256]{1,0:T(8,128)S(1)} %get-tuple-element.48.dq, f32[128,128]{1,0:T(8,128)S(1)} %get-tuple-element.53.refs_0_, f32[128,128]{1,0:T(8,128)S(1)} %collective-permute-done.10.refs_1_, ...), custom_call_target="tpu_custom_call" | custom-call | tf_op jit(solution)/shard_map/finish/pallas_call | solution.py:339
  (3 shorter events, 0.0 us)
Async XLA Ops:
  3.0 11.2 %collective-permute-start = (bf16[512,640]{1,0:T(8,128)(2,1)}, bf16[512,640]{1,0:T(8,128)(2,1)S(1)}, u32[]{:S(2)}, u32[]{:S(2)}) collective-permute-start(bf16[512,640]{1,0:T(8,128)(2,1)} %get-tuple-element.30.refs_0_), channel_id=1, source_target_pairs={{0,1},{1,0},{2,3},{3,2},{4,5},{5,4},{6,7},{7,6},{8,9},{9,8},{10,11... | collective-permute-start | bytes 1966088 | tf_op jit(solution)/shard_map/ppermute | solution.py:247
  3.0 4.1 %collective-permute-start.1 = (bf16[128,128]{1,0:T(8,128)(2,1)}, bf16[128,128]{1,0:T(8,128)(2,1)S(1)}, u32[]{:S(2)}, u32[]{:S(2)}) collective-permute-start(bf16[128,128]{1,0:T(8,128)(2,1)} %get-tuple-element.36), channel_id=1, source_target_pairs={{0,8},{8,0},{16,24},{24,16},{1,9},{9,1},{17,25},{25,17},{2,10},{10... | collective-permute-start | bytes 98312 | tf_op jit(solution)/shard_map/ppermute | solution.py:256
  4.5 4.1 %collective-permute-start.2 = (bf16[128,128]{1,0:T(8,128)(2,1)}, bf16[128,128]{1,0:T(8,128)(2,1)S(1)}, u32[]{:S(2)}, u32[]{:S(2)}) collective-permute-start(bf16[128,128]{1,0:T(8,128)(2,1)} %get-tuple-element.37), channel_id=1, source_target_pairs={{0,16},{8,24},{16,0},{24,8},{1,17},{9,25},{17,1},{25,9},{2,18},{10... | collective-permute-start | bytes 98312 | tf_op jit(solution)/shard_map/ppermute | solution.py:256
  6.1 5.0 %collective-permute-start.3 = (bf16[128,128]{1,0:T(8,128)(2,1)}, bf16[128,128]{1,0:T(8,128)(2,1)S(1)}, u32[]{:S(2)}, u32[]{:S(2)}) collective-permute-start(bf16[128,128]{1,0:T(8,128)(2,1)} %get-tuple-element.38), channel_id=1, source_target_pairs={{0,24},{8,16},{16,8},{24,0},{1,25},{9,17},{17,9},{25,1},{2,26},{10... | collective-permute-start | bytes 98312 | tf_op jit(solution)/shard_map/ppermute | solution.py:256
  11.1 0.8 %copy-start.1 = (bf16[128,128]{1,0:T(8,128)(2,1)S(1)}, bf16[128,128]{1,0:T(8,128)(2,1)}, u32[]{:S(2)}) copy-start(bf16[128,128]{1,0:T(8,128)(2,1)} %get-tuple-element.35.refs_0_) | copy-start | bytes 98308
  11.8 1.4 %copy-start.2 = (s32[4096]{0:T(1024)S(1)}, s32[4096]{0:T(1024)}, u32[]{:S(2)}) copy-start(s32[4096]{0:T(1024)} %param.13) | copy-start | bytes 49156
  11.9 15.4 %collective-permute-start.6 = (bf16[512,128]{1,0:T(8,128)(2,1)S(1)}, bf16[512,128]{1,0:T(8,128)(2,1)S(1)}, u32[]{:S(2)}, u32[]{:S(2)}) collective-permute-start(bf16[512,128]{1,0:T(8,128)(2,1)S(1)} %join.1.refs_8_), channel_id=1, source_target_pairs={{0,4},{1,5},{2,6},{3,7},{8,12},{9,13},{10,14},{11,15},{16,20},{17,... | collective-permute-start | bytes 393224 | tf_op jit(solution)/shard_map/ppermute | solution.py:250
  13.6 14.3 %collective-permute-start.5 = (bf16[512,128]{1,0:T(8,128)(2,1)S(1)}, bf16[512,128]{1,0:T(8,128)(2,1)S(1)}, u32[]{:S(2)}, u32[]{:S(2)}) collective-permute-start(bf16[512,128]{1,0:T(8,128)(2,1)S(1)} %join.1.refs_8_), channel_id=1, source_target_pairs={{0,6},{1,7},{8,14},{9,15},{16,22},{17,23},{24,30},{25,31}} | collective-permute-start | bytes 393224 | tf_op jit(solution)/shard_map/ppermute | solution.py:250
  14.2 1.1 %copy-start = (bf16[512,640]{1,0:T(8,128)(2,1)S(1)}, bf16[512,640]{1,0:T(8,128)(2,1)}, u32[]{:S(2)}) copy-start(bf16[512,640]{1,0:T(8,128)(2,1)} %get-tuple-element.30.refs_0_) | copy-start | bytes 1966084
  23.1 11.5 %collective-permute-start.4 = (bf16[512,128]{1,0:T(8,128)(2,1)S(1)}, bf16[512,128]{1,0:T(8,128)(2,1)S(1)}, u32[]{:S(2)}, u32[]{:S(2)}) collective-permute-start(bf16[512,128]{1,0:T(8,128)(2,1)S(1)} %join.1.refs_8_), channel_id=1, source_target_pairs={{0,2},{1,3},{2,4},{3,5},{4,6},{5,7},{8,10},{9,11},{10,12},{11,13},... | collective-permute-start | bytes 393224 | tf_op jit(solution)/shard_map/ppermute | solution.py:250
  28.5 14.4 %collective-permute-start.8 = (bf16[128,512]{1,0:T(8,128)(2,1)S(1)}, bf16[128,512]{1,0:T(8,128)(2,1)S(1)}, u32[]{:S(2)}, u32[]{:S(2)}) collective-permute-start(bf16[128,512]{1,0:T(8,128)(2,1)S(1)} %get-tuple-element.46), channel_id=1, source_target_pairs={{6,0},{7,1},{14,8},{15,9},{22,16},{23,17},{30,24},{31,25}} | collective-permute-start | bytes 393224 | tf_op jit(solution)/shard_map/ppermute | solution.py:253
  29.1 14.6 %collective-permute-start.7 = (bf16[128,512]{1,0:T(8,128)(2,1)S(1)}, bf16[128,512]{1,0:T(8,128)(2,1)S(1)}, u32[]{:S(2)}, u32[]{:S(2)}) collective-permute-start(bf16[128,512]{1,0:T(8,128)(2,1)S(1)} %get-tuple-element.45), channel_id=1, source_target_pairs={{4,0},{5,1},{6,2},{7,3},{12,8},{13,9},{14,10},{15,11},{20,16},{21,... | collective-permute-start | bytes 393224 | tf_op jit(solution)/shard_map/ppermute | solution.py:253
  40.9 8.1 %collective-permute-start.9 = (bf16[128,512]{1,0:T(8,128)(2,1)S(1)}, bf16[128,512]{1,0:T(8,128)(2,1)S(1)}, u32[]{:S(2)}, u32[]{:S(2)}) collective-permute-start(bf16[128,512]{1,0:T(8,128)(2,1)S(1)} %get-tuple-element.47), channel_id=1, source_target_pairs={{2,0},{3,1},{4,2},{5,3},{6,4},{7,5},{10,8},{11,9},{12,10},{13,11},... | collective-permute-start | bytes 393224 | tf_op jit(solution)/shard_map/ppermute | solution.py:253
  49.1 6.6 %collective-permute-start.13 = (f32[512,256]{1,0:T(8,128)S(1)}, f32[512,256]{1,0:T(8,128)S(1)}, u32[]{:S(2)}, u32[]{:S(2)}) collective-permute-start(f32[512,256]{1,0:T(8,128)S(1)} %slice.11), channel_id=1, source_target_pairs={{0,1},{1,0},{2,3},{3,2},{4,5},{5,4},{6,7},{7,6},{8,9},{9,8},{10,11... | collective-permute-start | bytes 1572872 | tf_op jit(solution)/shard_map/ppermute | solution.py:247
  49.4 4.5 %collective-permute-start.10 = (f32[128,128]{1,0:T(8,128)S(1)}, f32[128,128]{1,0:T(8,128)S(1)}, u32[]{:S(2)}, u32[]{:S(2)}) collective-permute-start(f32[128,128]{1,0:T(8,128)S(1)} %get-tuple-element.54), channel_id=1, source_target_pairs={{0,8},{8,0},{16,24},{24,16},{1,9},{9,1},{17,25},{25,17},{2,10},{10... | collective-permute-start | bytes 196616 | tf_op jit(solution)/shard_map/ppermute | solution.py:256
  50.0 5.0 %collective-permute-start.11 = (f32[128,128]{1,0:T(8,128)S(1)}, f32[128,128]{1,0:T(8,128)S(1)}, u32[]{:S(2)}, u32[]{:S(2)}) collective-permute-start(f32[128,128]{1,0:T(8,128)S(1)} %get-tuple-element.55), channel_id=1, source_target_pairs={{0,16},{8,24},{16,0},{24,8},{1,17},{9,25},{17,1},{25,9},{2,18},{10... | collective-permute-start | bytes 196616 | tf_op jit(solution)/shard_map/ppermute | solution.py:256
  50.5 5.2 %collective-permute-start.12 = (f32[128,128]{1,0:T(8,128)S(1)}, f32[128,128]{1,0:T(8,128)S(1)}, u32[]{:S(2)}, u32[]{:S(2)}) collective-permute-start(f32[128,128]{1,0:T(8,128)S(1)} %get-tuple-element.56), channel_id=1, source_target_pairs={{0,24},{8,16},{16,8},{24,0},{1,25},{9,17},{17,9},{25,1},{2,26},{10... | collective-permute-start | bytes 196616 | tf_op jit(solution)/shard_map/ppermute | solution.py:256

commit v7 on v6

--- a/solution.py
+++ b/solution.py
@@ -86,7 +86,8 @@
 
 def expand_kernel(sides, panel, first, last, *refs):
     packs, docs = refs[:sides], refs[sides]
-    q_ext, g_ext, q_t, g_t = refs[sides + 1 :]
+    q_ext, g_ext, q_t, g_t, docs_out = refs[sides + 1 :]
+    docs_out[...] = docs[...]
     feats = q_t.shape[0]
     heads = feats // HEAD_DIM
     rows = docs.shape[1]
@@ -266,19 +267,21 @@
         compiler_params=small(56),
         name="prep",
     )(place, key, value, query, grad_out, output, lse)
-    packed_other = swap(packed)
     pieces = [across(x, j) for j, x in enumerate(pieces)]
+    source, *pieces = lax.optimization_barrier((packed, *pieces))
+    packed_other = swap(source)
 
     docs = doc_ids.reshape(col_count, rows)
     first, last = docs[:, ::SUB].reshape(-1), docs[:, SUB - 1 :: SUB].reshape(-1)
     mine = jnp.stack([col, col ^ 1]).astype(jnp.int32)
 
-    q_ext, g_ext, q_t, g_t = pl.pallas_call(
+    q_ext, g_ext, q_t, g_t, docs = pl.pallas_call(
         functools.partial(expand_kernel, 2),
         in_specs=[SMEM_SPEC] * 3 + [VMEM_SPEC] * 3,
-        out_specs=[VMEM_SPEC] * 4,
+        out_specs=[VMEM_SPEC] * 5,
         out_shape=[jax.ShapeDtypeStruct((heads, 2 * rows, 128), bf16)] * 2
-        + [jax.ShapeDtypeStruct((feats, 2 * rows), bf16)] * 2,
+        + [jax.ShapeDtypeStruct((feats, 2 * rows), bf16)] * 2
+        + [jax.ShapeDtypeStruct(docs.shape, jnp.int32)],
         compiler_params=small(16),
         name="expand",
     )(mine, first, last, packed, packed_other, docs)
@@ -314,16 +317,19 @@
         )(mine, first, last, q_ext, g_ext, q_t, g_t, docs, block, *extra)
 
     reach = min(chips - 1, chips // 2 + 1)
-    order = [*range(2, reach + 1), 1]
-    blocks = {d: up(pair, d) for d in order[:-1]}
-    dq, own = band("own", 0, pair, None, SUB, f32)
-    late, own = lax.optimization_barrier((pair, own))
-    blocks[1] = up(late, 1)
+    blocks = {1: up(pair, 1)}
+    late, docs = lax.optimization_barrier((pair, docs))
+    for d in range(2, reach + 1):
+        blocks[d] = up(late, d)
+    dq = None
     back = []
-    for d in order:
+    for d in range(1, reach + 1):
         q_tile = 2 * SUB if d < reach else SUB
         dq, grads = band(f"band{d}", 2 * d, blocks[d], dq, q_tile, bf16)
         back.append(down(grads, d))
+        if d == 2:
+            dq, back[0] = lax.optimization_barrier((dq, back[0]))
+    dq, own = band("own", 0, pair, dq, SUB, f32)
     dq, *back = lax.optimization_barrier((dq, *back))
     chunk = jax.ShapeDtypeStruct((pair_feats, key_rows), f32)
     chunks = pl.pallas_call(

time: 57.1 us -> 57.9 us (1.014)
  the two profiles are of different devices: /device:TPU:16 before, /device:TPU:0 now
where the time goes in v7:
time: 57.9 us
  starting transfers between devices  29.2 us (50%)
  waiting for transfers between devices  14 us (24%)
  Pallas kernels  11.6 us (20%)
  local copies, waits for them, and re-layouts  2.21 us (4%)
  between operations  0.8 us (1%)
    ppermute x3, starting transfers between devices, up(): lax.ppermute(x, 'kcol', [(i, i + 2 * d) for i in range(col_count - 2 * d)])  17.2 us
    ppermute x6, starting transfers between devices, across(): lax.ppermute(x, 'qrow', [(i, i ^ j) for i in range(row_count)])  8.01 us
    ppermute x6, waiting for transfers between devices, across(): lax.ppermute(x, 'qrow', [(i, i ^ j) for i in range(row_count)])  7.75 us
    pallas_call x4, Pallas kernels, band(): pl.pallas_call(functools.partial(band_kernel, shift, q_tile, chained), in...  6.7 us
    ppermute x3, waiting for transfers between devices, down(): lax.ppermute(x, 'kcol', [(i + 2 * d, i) for i in range(col_count - 2 * d)])  5.46 us
    ppermute x3, starting transfers between devices, down(): lax.ppermute(x, 'kcol', [(i + 2 * d, i) for i in range(col_count - 2 * d)])  3.88 us
    pallas_call x1, Pallas kernels, per_device(): pl.pallas_call(prep_kernel, in_specs=[SMEM_SPEC] + [VMEM_SPEC] * 6, out_s...  2.4 us
    unnamed x6, local copies, waits for them, and re-layouts  1.86 us
  transfers between devices with their start and end apart: 14, of which 9 were waited for; matrix products, arithmetic and copies ran while one was open for 1% of the time, Pallas kernels for 14%

profile of v7, /device:TPU:0, one launch (start us, length us, event | category | flops | bytes accessed | tf_op | source)
XLA Modules:
  0.0 57.9 jit_solution(1870755227610214203)
XLA Ops:
  0.6 2.4 %prep.1 = (bf16[128,128]{1,0:T(8,128)(2,1)}, bf16[128,128]{1,0:T(8,128)(2,1)}, bf16[128,128]{1,0:T(8,128)(2,1)}, bf16[128,128]{1,0:T(8,128)(2,1)}, bf16[512,640]{1,0:T(8,128)(2,1)}) custom-call(s32[1]{0:T(128)} %bitcast.place, bf16[128,256]{1,0:T(8,128)(2,1)} %key.1, bf16[128,256]{1,0:T(8,128)(2,1)} %value.1, bf16[512,256]{1,0:T(8,128)(2,1)} %query.1, ...), custom_call_target="tpu_custom_call" | custom-call | tf_op jit(solution)/shard_map/prep/pallas_call | solution.py:260
  3.0 2.9 %collective-permute-start = (bf16[128,128]{1,0:T(8,128)(2,1)}, bf16[128,128]{1,0:T(8,128)(2,1)S(1)}, u32[]{:S(2)}, u32[]{:S(2)}) collective-permute-start(bf16[128,128]{1,0:T(8,128)(2,1)} %get-tuple-element.40), channel_id=1, source_target_pairs={{0,8},{8,0},{16,24},{24,16},{1,9},{9,1},{17,25},{25,17},{2,10},{10... | collective-permute-start | bytes 98312 | tf_op jit(solution)/shard_map/ppermute | solution.py:257
  6.0 1.5 %collective-permute-start.1 = (bf16[128,128]{1,0:T(8,128)(2,1)}, bf16[128,128]{1,0:T(8,128)(2,1)S(1)}, u32[]{:S(2)}, u32[]{:S(2)}) collective-permute-start(bf16[128,128]{1,0:T(8,128)(2,1)} %get-tuple-element.41), channel_id=1, source_target_pairs={{0,16},{8,24},{16,0},{24,8},{1,17},{9,25},{17,1},{25,9},{2,18},{10... | collective-permute-start | bytes 98312 | tf_op jit(solution)/shard_map/ppermute | solution.py:257
  7.5 0.0 collective-permute-start.2
  7.5 0.6 collective-permute-done.refs_1_
  8.1 2.0 %collective-permute-done.1.refs_2_ = bf16[128,128]{1,0:T(8,128)(2,1)S(1)} collective-permute-done((bf16[128,128]{1,0:T(8,128)(2,1)}, bf16[128,128]{1,0:T(8,128)(2,1)S(1)}, u32[]{:S(2)}, u32[]{:S(2)}) %collective-permute-start.1) | collective-permute-done | bytes 32800 | tf_op jit(solution)/shard_map/ppermute | solution.py:257
  10.1 2.4 %collective-permute-done.2.refs_3_ = bf16[128,128]{1,0:T(8,128)(2,1)S(1)} collective-permute-done((bf16[128,128]{1,0:T(8,128)(2,1)}, bf16[128,128]{1,0:T(8,128)(2,1)S(1)}, u32[]{:S(2)}, u32[]{:S(2)}) %collective-permute-start.2) | collective-permute-done | bytes 32800 | tf_op jit(solution)/shard_map/ppermute | solution.py:257
  12.5 0.0 collective-permute-start.3
  12.5 0.0 copy-start.1
  12.5 0.8 %copy-done.1 = bf16[128,128]{1,0:T(8,128)(2,1)S(1)} copy-done((bf16[128,128]{1,0:T(8,128)(2,1)S(1)}, bf16[128,128]{1,0:T(8,128)(2,1)}, u32[]{:S(2)}) %copy-start.1) | copy-done | bytes 32792
  13.3 0.0 copy-start.2
  13.3 3.5 %collective-permute-start.6 = (bf16[512,128]{1,0:T(8,128)(2,1)S(1)}, bf16[512,128]{1,0:T(8,128)(2,1)S(1)}, u32[]{:S(2)}, u32[]{:S(2)}) collective-permute-start(bf16[512,128]{1,0:T(8,128)(2,1)S(1)} %join.1.refs_8_), channel_id=1, source_target_pairs={{0,2},{1,3},{2,4},{3,5},{4,6},{5,7},{8,10},{9,11},{10,12},{11,13},... | collective-permute-start | bytes 393224 | tf_op jit(solution)/shard_map/ppermute | solution.py:251
  16.8 0.0 copy-done.2
  16.8 0.1 slice.10
  16.9 0.1 slice.9
  17.0 0.1 reshape.17.last.refs_2_
  17.1 0.1 reshape.16.first.refs_1_
  17.1 0.1 pad_add_fusion.panel.refs_0_
  17.2 0.0 collective-permute-done.3.refs_1_
  17.2 0.0 copy-start
  17.2 1.1 %copy-done = bf16[512,640]{1,0:T(8,128)(2,1)S(1)} copy-done((bf16[512,640]{1,0:T(8,128)(2,1)S(1)}, bf16[512,640]{1,0:T(8,128)(2,1)}, u32[]{:S(2)}) %copy-start) | copy-done | bytes 655384
  18.3 1.4 %expand.1 = (bf16[4,1024,128]{2,1,0:T(8,128)(2,1)S(1)}, bf16[4,1024,128]{2,1,0:T(8,128)(2,1)S(1)}, bf16[256,1024]{1,0:T(8,128)(2,1)S(1)}, bf16[256,1024]{1,0:T(8,128)(2,1)S(1)}, s32[8,512]{1,0:T(8,128)S(1)}) custom-call(s32[2]{0:T(128)S(1)} %pad_add_fusion.panel.refs_0_, s32[16]{0:T(128)S(1)} %reshape.16.first.refs_1_, s32[16]{0:T(128)S(1)} %reshape.17.last.refs_2_, ...), custom_call_target="tpu_custom_call" | custom-call | tf_op jit(solution)/shard_map/expand/pallas_call | solution.py:278
  19.7 4.5 %collective-permute-start.5 = (bf16[512,128]{1,0:T(8,128)(2,1)S(1)}, bf16[512,128]{1,0:T(8,128)(2,1)S(1)}, u32[]{:S(2)}, u32[]{:S(2)}) collective-permute-start(bf16[512,128]{1,0:T(8,128)(2,1)S(1)} %join.1.refs_8_), channel_id=1, source_target_pairs={{0,4},{1,5},{2,6},{3,7},{8,12},{9,13},{10,14},{11,15},{16,20},{17,... | collective-permute-start | bytes 393224 | tf_op jit(solution)/shard_map/ppermute | solution.py:251
  24.2 0.0 collective-permute-done.6.refs_8_
  24.2 0.7 %band1.1 = (f32[1024,256]{1,0:T(8,128)S(1)}, bf16[128,512]{1,0:T(8,128)(2,1)S(1)}) custom-call(s32[2]{0:T(128)S(1)} %pad_add_fusion.panel.refs_0_, s32[16]{0:T(128)S(1)} %reshape.16.first.refs_1_, s32[16]{0:T(128)S(1)} %reshape.17.last.refs_2_, bf16[4,1024,128]{2,1,0:T(8,128)(2,1)S(1)} %get-tuple-element.44.refs_3_, ...), custom_call_target="tpu_custom_call" | custom-call | flops 1342177280 | bytes 6291456 | tf_op jit(solution)/shard_map/band1/pallas_call | solution.py:300
  24.9 1.3 %collective-permute-start.7 = (bf16[128,512]{1,0:T(8,128)(2,1)S(1)}, bf16[128,512]{1,0:T(8,128)(2,1)S(1)}, u32[]{:S(2)}, u32[]{:S(2)}) collective-permute-start(bf16[128,512]{1,0:T(8,128)(2,1)S(1)} %get-tuple-element.57), channel_id=1, source_target_pairs={{2,0},{3,1},{4,2},{5,3},{6,4},{7,5},{10,8},{11,9},{12,10},{13,11},... | collective-permute-start | bytes 393224 | tf_op jit(solution)/shard_map/ppermute | solution.py:254
  26.2 9.2 %collective-permute-start.4 = (bf16[512,128]{1,0:T(8,128)(2,1)S(1)}, bf16[512,128]{1,0:T(8,128)(2,1)S(1)}, u32[]{:S(2)}, u32[]{:S(2)}) collective-permute-start(bf16[512,128]{1,0:T(8,128)(2,1)S(1)} %join.1.refs_8_), channel_id=1, source_target_pairs={{0,6},{1,7},{8,14},{9,15},{16,22},{17,23},{24,30},{25,31}} | collective-permute-start | bytes 393224 | tf_op jit(solution)/shard_map/ppermute | solution.py:251
  35.4 0.0 collective-permute-done.5.refs_8_
  35.4 0.6 %band2.1 = (f32[1024,256]{1,0:T(8,128)S(1)}, bf16[128,512]{1,0:T(8,128)(2,1)S(1)}) custom-call(s32[2]{0:T(128)S(1)} %pad_add_fusion.panel.refs_0_, s32[16]{0:T(128)S(1)} %reshape.16.first.refs_1_, s32[16]{0:T(128)S(1)} %reshape.17.last.refs_2_, bf16[4,1024,128]{2,1,0:T(8,128)(2,1)S(1)} %get-tuple-element.44.refs_3_, ...), custom_call_target="tpu_custom_call", output_to_operand_aliasing={{0}: (9, {})} | custom-call | flops 1342177280 | bytes 6291456 | tf_op jit(solution)/shard_map/band2/pallas_call | solution.py:300
  36.0 1.3 %collective-permute-start.8 = (bf16[128,512]{1,0:T(8,128)(2,1)S(1)}, bf16[128,512]{1,0:T(8,128)(2,1)S(1)}, u32[]{:S(2)}, u32[]{:S(2)}) collective-permute-start(bf16[128,512]{1,0:T(8,128)(2,1)S(1)} %get-tuple-element.62), channel_id=1, source_target_pairs={{4,0},{5,1},{6,2},{7,3},{12,8},{13,9},{14,10},{15,11},{20,16},{21,... | collective-permute-start | bytes 393224 | tf_op jit(solution)/shard_map/ppermute | solution.py:254
  37.3 0.0 collective-permute-done.7.refs_1_
  37.3 0.8 %collective-permute-done.4.refs_8_ = bf16[512,128]{1,0:T(8,128)(2,1)S(1)} collective-permute-done((bf16[512,128]{1,0:T(8,128)(2,1)S(1)}, bf16[512,128]{1,0:T(8,128)(2,1)S(1)}, u32[]{:S(2)}, u32[]{:S(2)}) %collective-permute-start.4) | collective-permute-done | bytes 131104 | tf_op jit(solution)/shard_map/ppermute | solution.py:251
  38.1 0.6 %band3.1 = (f32[1024,256]{1,0:T(8,128)S(1)}, bf16[128,512]{1,0:T(8,128)(2,1)S(1)}) custom-call(s32[2]{0:T(128)S(1)} %pad_add_fusion.panel.refs_0_, s32[16]{0:T(128)S(1)} %reshape.16.first.refs_1_, s32[16]{0:T(128)S(1)} %reshape.17.last.refs_2_, bf16[4,1024,128]{2,1,0:T(8,128)(2,1)S(1)} %get-tuple-element.44.refs_3_, ...), custom_call_target="tpu_custom_call", output_to_operand_aliasing={{0}: (9, {})} | custom-call | flops 1342177280 | bytes 6291456 | tf_op jit(solution)/shard_map/band3/pallas_call | solution.py:300
  38.7 1.3 %collective-permute-start.9 = (bf16[128,512]{1,0:T(8,128)(2,1)S(1)}, bf16[128,512]{1,0:T(8,128)(2,1)S(1)}, u32[]{:S(2)}, u32[]{:S(2)}) collective-permute-start(bf16[128,512]{1,0:T(8,128)(2,1)S(1)} %get-tuple-element.63), channel_id=1, source_target_pairs={{6,0},{7,1},{14,8},{15,9},{22,16},{23,17},{30,24},{31,25}} | collective-permute-start | bytes 393224 | tf_op jit(solution)/shard_map/ppermute | solution.py:254
  40.0 4.9 %own.1 = (f32[1024,256]{1,0:T(8,128)S(1)}, f32[128,512]{1,0:T(8,128)S(1)}) custom-call(s32[2]{0:T(128)S(1)} %pad_add_fusion.panel.refs_0_, s32[16]{0:T(128)S(1)} %reshape.16.first.refs_1_, s32[16]{0:T(128)S(1)} %reshape.17.last.refs_2_, bf16[4,1024,128]{2,1,0:T(8,128)(2,1)S(1)} %get-tuple-element.44.refs_3_, ...), custom_call_target="tpu_custom_call", output_to_operand_aliasing={{0}: (9, {})} | custom-call | flops 1342177280 | bytes 6291456 | tf_op jit(solution)/shard_map/own/pallas_call | solution.py:300
  44.9 1.1 %collective-permute-done.8.refs_2_ = bf16[128,512]{1,0:T(8,128)(2,1)S(1)} collective-permute-done((bf16[128,512]{1,0:T(8,128)(2,1)S(1)}, bf16[128,512]{1,0:T(8,128)(2,1)S(1)}, u32[]{:S(2)}, u32[]{:S(2)}) %collective-permute-start.8) | collective-permute-done | bytes 131104 | tf_op jit(solution)/shard_map/ppermute | solution.py:254
  45.9 4.4 %collective-permute-done.9.refs_3_ = bf16[128,512]{1,0:T(8,128)(2,1)S(1)} collective-permute-done((bf16[128,512]{1,0:T(8,128)(2,1)S(1)}, bf16[128,512]{1,0:T(8,128)(2,1)S(1)}, u32[]{:S(2)}, u32[]{:S(2)}) %collective-permute-start.9) | collective-permute-done | bytes 131104 | tf_op jit(solution)/shard_map/ppermute | solution.py:254
  50.4 0.1 collective-permute-start.13
  50.5 0.1 collect.1
  50.6 0.6 %collective-permute-start.10 = (f32[128,128]{1,0:T(8,128)S(1)}, f32[128,128]{1,0:T(8,128)S(1)}, u32[]{:S(2)}, u32[]{:S(2)}) collective-permute-start(f32[128,128]{1,0:T(8,128)S(1)} %get-tuple-element.70), channel_id=1, source_target_pairs={{0,8},{8,0},{16,24},{24,16},{1,9},{9,1},{17,25},{25,17},{2,10},{10... | collective-permute-start | bytes 196616 | tf_op jit(solution)/shard_map/ppermute | solution.py:257
  51.2 0.5 collective-permute-start.11
  51.7 2.4 %collective-permute-start.12 = (f32[128,128]{1,0:T(8,128)S(1)}, f32[128,128]{1,0:T(8,128)S(1)}, u32[]{:S(2)}, u32[]{:S(2)}) collective-permute-start(f32[128,128]{1,0:T(8,128)S(1)} %get-tuple-element.72), channel_id=1, source_target_pairs={{0,24},{8,16},{16,8},{24,0},{1,25},{9,17},{17,9},{25,1},{2,26},{10... | collective-permute-start | bytes 196616 | tf_op jit(solution)/shard_map/ppermute | solution.py:257
  54.1 1.0 %collective-permute-done.10.refs_1_ = f32[128,128]{1,0:T(8,128)S(1)} collective-permute-done((f32[128,128]{1,0:T(8,128)S(1)}, f32[128,128]{1,0:T(8,128)S(1)}, u32[]{:S(2)}, u32[]{:S(2)}) %collective-permute-start.10) | collective-permute-done | bytes 65568 | tf_op jit(solution)/shard_map/ppermute | solution.py:257
  55.1 1.0 %collective-permute-done.11.refs_2_ = f32[128,128]{1,0:T(8,128)S(1)} collective-permute-done((f32[128,128]{1,0:T(8,128)S(1)}, f32[128,128]{1,0:T(8,128)S(1)}, u32[]{:S(2)}, u32[]{:S(2)}) %collective-permute-start.11) | collective-permute-done | bytes 65568 | tf_op jit(solution)/shard_map/ppermute | solution.py:257
  56.1 0.7 %collective-permute-done.12.refs_3_ = f32[128,128]{1,0:T(8,128)S(1)} collective-permute-done((f32[128,128]{1,0:T(8,128)S(1)}, f32[128,128]{1,0:T(8,128)S(1)}, u32[]{:S(2)}, u32[]{:S(2)}) %collective-permute-start.12) | collective-permute-done | bytes 65568 | tf_op jit(solution)/shard_map/ppermute | solution.py:257
  56.9 0.0 collective-permute-done.13.refs_4_
  56.9 1.0 %finish.1 = (f32[512,256]{1,0:T(8,128)}, f32[128,256]{1,0:T(8,128)}, f32[128,256]{1,0:T(8,128)}) custom-call(s32[1]{0:T(128)} %bitcast.place, f32[1024,256]{1,0:T(8,128)S(1)} %get-tuple-element.64.dq, f32[128,128]{1,0:T(8,128)S(1)} %get-tuple-element.69.refs_0_, f32[128,128]{1,0:T(8,128)S(1)} %collective-permute-done.10.refs_1_, ...), custom_call_target="tpu_custom_call" | custom-call | tf_op jit(solution)/shard_map/finish/pallas_call | solution.py:345
  (3 shorter events, 0.1 us)
Async XLA Ops:
  3.0 5.0 %collective-permute-start = (bf16[128,128]{1,0:T(8,128)(2,1)}, bf16[128,128]{1,0:T(8,128)(2,1)S(1)}, u32[]{:S(2)}, u32[]{:S(2)}) collective-permute-start(bf16[128,128]{1,0:T(8,128)(2,1)} %get-tuple-element.40), channel_id=1, source_target_pairs={{0,8},{8,0},{16,24},{24,16},{1,9},{9,1},{17,25},{25,17},{2,10},{10... | collective-permute-start | bytes 98312 | tf_op jit(solution)/shard_map/ppermute | solution.py:257
  6.0 4.1 %collective-permute-start.1 = (bf16[128,128]{1,0:T(8,128)(2,1)}, bf16[128,128]{1,0:T(8,128)(2,1)S(1)}, u32[]{:S(2)}, u32[]{:S(2)}) collective-permute-start(bf16[128,128]{1,0:T(8,128)(2,1)} %get-tuple-element.41), channel_id=1, source_target_pairs={{0,16},{8,24},{16,0},{24,8},{1,17},{9,25},{17,1},{25,9},{2,18},{10... | collective-permute-start | bytes 98312 | tf_op jit(solution)/shard_map/ppermute | solution.py:257
  7.5 5.0 %collective-permute-start.2 = (bf16[128,128]{1,0:T(8,128)(2,1)}, bf16[128,128]{1,0:T(8,128)(2,1)S(1)}, u32[]{:S(2)}, u32[]{:S(2)}) collective-permute-start(bf16[128,128]{1,0:T(8,128)(2,1)} %get-tuple-element.42), channel_id=1, source_target_pairs={{0,24},{8,16},{16,8},{24,0},{1,25},{9,17},{17,9},{25,1},{2,26},{10... | collective-permute-start | bytes 98312 | tf_op jit(solution)/shard_map/ppermute | solution.py:257
  12.5 4.7 %collective-permute-start.3 = (bf16[512,640]{1,0:T(8,128)(2,1)}, bf16[512,640]{1,0:T(8,128)(2,1)S(1)}, u32[]{:S(2)}, u32[]{:S(2)}) collective-permute-start(bf16[512,640]{1,0:T(8,128)(2,1)} %get-tuple-element.43.refs_0_), channel_id=1, source_target_pairs={{0,1},{1,0},{2,3},{3,2},{4,5},{5,4},{6,7},{7,6},{8,9},{9,8},{10,11... | collective-permute-start | bytes 1966088 | tf_op jit(solution)/shard_map/ppermute | solution.py:248
  12.5 0.8 %copy-start.1 = (bf16[128,128]{1,0:T(8,128)(2,1)S(1)}, bf16[128,128]{1,0:T(8,128)(2,1)}, u32[]{:S(2)}) copy-start(bf16[128,128]{1,0:T(8,128)(2,1)} %get-tuple-element.48.refs_0_) | copy-start | bytes 98308
  13.3 3.5 %copy-start.2 = (s32[4096]{0:T(1024)S(1)}, s32[4096]{0:T(1024)}, u32[]{:S(2)}) copy-start(s32[4096]{0:T(1024)} %param.13) | copy-start | bytes 49156
  13.3 10.9 %collective-permute-start.6 = (bf16[512,128]{1,0:T(8,128)(2,1)S(1)}, bf16[512,128]{1,0:T(8,128)(2,1)S(1)}, u32[]{:S(2)}, u32[]{:S(2)}) collective-permute-start(bf16[512,128]{1,0:T(8,128)(2,1)S(1)} %join.1.refs_8_), channel_id=1, source_target_pairs={{0,2},{1,3},{2,4},{3,5},{4,6},{5,7},{8,10},{9,11},{10,12},{11,13},... | collective-permute-start | bytes 393224 | tf_op jit(solution)/shard_map/ppermute | solution.py:251
  17.2 1.1 %copy-start = (bf16[512,640]{1,0:T(8,128)(2,1)S(1)}, bf16[512,640]{1,0:T(8,128)(2,1)}, u32[]{:S(2)}) copy-start(bf16[512,640]{1,0:T(8,128)(2,1)} %get-tuple-element.43.refs_0_) | copy-start | bytes 1966084
  19.7 15.7 %collective-permute-start.5 = (bf16[512,128]{1,0:T(8,128)(2,1)S(1)}, bf16[512,128]{1,0:T(8,128)(2,1)S(1)}, u32[]{:S(2)}, u32[]{:S(2)}) collective-permute-start(bf16[512,128]{1,0:T(8,128)(2,1)S(1)} %join.1.refs_8_), channel_id=1, source_target_pairs={{0,4},{1,5},{2,6},{3,7},{8,12},{9,13},{10,14},{11,15},{16,20},{17,... | collective-permute-start | bytes 393224 | tf_op jit(solution)/shard_map/ppermute | solution.py:251
  24.9 12.4 %collective-permute-start.7 = (bf16[128,512]{1,0:T(8,128)(2,1)S(1)}, bf16[128,512]{1,0:T(8,128)(2,1)S(1)}, u32[]{:S(2)}, u32[]{:S(2)}) collective-permute-start(bf16[128,512]{1,0:T(8,128)(2,1)S(1)} %get-tuple-element.57), channel_id=1, source_target_pairs={{2,0},{3,1},{4,2},{5,3},{6,4},{7,5},{10,8},{11,9},{12,10},{13,11},... | collective-permute-start | bytes 393224 | tf_op jit(solution)/shard_map/ppermute | solution.py:254
  26.2 12.0 %collective-permute-start.4 = (bf16[512,128]{1,0:T(8,128)(2,1)S(1)}, bf16[512,128]{1,0:T(8,128)(2,1)S(1)}, u32[]{:S(2)}, u32[]{:S(2)}) collective-permute-start(bf16[512,128]{1,0:T(8,128)(2,1)S(1)} %join.1.refs_8_), channel_id=1, source_target_pairs={{0,6},{1,7},{8,14},{9,15},{16,22},{17,23},{24,30},{25,31}} | collective-permute-start | bytes 393224 | tf_op jit(solution)/shard_map/ppermute | solution.py:251
  36.0 10.0 %collective-permute-start.8 = (bf16[128,512]{1,0:T(8,128)(2,1)S(1)}, bf16[128,512]{1,0:T(8,128)(2,1)S(1)}, u32[]{:S(2)}, u32[]{:S(2)}) collective-permute-start(bf16[128,512]{1,0:T(8,128)(2,1)S(1)} %get-tuple-element.62), channel_id=1, source_target_pairs={{4,0},{5,1},{6,2},{7,3},{12,8},{13,9},{14,10},{15,11},{20,16},{21,... | collective-permute-start | bytes 393224 | tf_op jit(solution)/shard_map/ppermute | solution.py:254
  38.7 11.6 %collective-permute-start.9 = (bf16[128,512]{1,0:T(8,128)(2,1)S(1)}, bf16[128,512]{1,0:T(8,128)(2,1)S(1)}, u32[]{:S(2)}, u32[]{:S(2)}) collective-permute-start(bf16[128,512]{1,0:T(8,128)(2,1)S(1)} %get-tuple-element.63), channel_id=1, source_target_pairs={{6,0},{7,1},{14,8},{15,9},{22,16},{23,17},{30,24},{31,25}} | collective-permute-start | bytes 393224 | tf_op jit(solution)/shard_map/ppermute | solution.py:254
  50.4 6.5 %collective-permute-start.13 = (f32[512,256]{1,0:T(8,128)S(1)}, f32[512,256]{1,0:T(8,128)S(1)}, u32[]{:S(2)}, u32[]{:S(2)}) collective-permute-start(f32[512,256]{1,0:T(8,128)S(1)} %slice.11), channel_id=1, source_target_pairs={{0,1},{1,0},{2,3},{3,2},{4,5},{5,4},{6,7},{7,6},{8,9},{9,8},{10,11... | collective-permute-start | bytes 1572872 | tf_op jit(solution)/shard_map/ppermute | solution.py:248
  50.6 4.5 %collective-permute-start.10 = (f32[128,128]{1,0:T(8,128)S(1)}, f32[128,128]{1,0:T(8,128)S(1)}, u32[]{:S(2)}, u32[]{:S(2)}) collective-permute-start(f32[128,128]{1,0:T(8,128)S(1)} %get-tuple-element.70), channel_id=1, source_target_pairs={{0,8},{8,0},{16,24},{24,16},{1,9},{9,1},{17,25},{25,17},{2,10},{10... | collective-permute-start | bytes 196616 | tf_op jit(solution)/shard_map/ppermute | solution.py:257
  51.2 5.0 %collective-permute-start.11 = (f32[128,128]{1,0:T(8,128)S(1)}, f32[128,128]{1,0:T(8,128)S(1)}, u32[]{:S(2)}, u32[]{:S(2)}) collective-permute-start(f32[128,128]{1,0:T(8,128)S(1)} %get-tuple-element.71), channel_id=1, source_target_pairs={{0,16},{8,24},{16,0},{24,8},{1,17},{9,25},{17,1},{25,9},{2,18},{10... | collective-permute-start | bytes 196616 | tf_op jit(solution)/shard_map/ppermute | solution.py:257
  51.7 5.2 %collective-permute-start.12 = (f32[128,128]{1,0:T(8,128)S(1)}, f32[128,128]{1,0:T(8,128)S(1)}, u32[]{:S(2)}, u32[]{:S(2)}) collective-permute-start(f32[128,128]{1,0:T(8,128)S(1)} %get-tuple-element.72), channel_id=1, source_target_pairs={{0,24},{8,16},{16,8},{24,0},{1,25},{9,17},{17,9},{25,1},{2,26},{10... | collective-permute-start | bytes 196616 | tf_op jit(solution)/shard_map/ppermute | solution.py:257
